TPU v7x, 32 devices: a whole 2x2x4 slice. The times are simulated.
32 devices in a mesh: dp: 2 (over core), ctx: 4 (over y, x), tp: 4 (over z).
Axes of the slice: x: 2, y: 2, z: 4, core: 2. Of those that a mesh axis runs over, the one named last changes fastest.
Arguments:
- layer_input: bfloat16 [6, 1024, 2048], P('dp', 'ctx'), may hold values from -6 to 6
- segments: int32 [6, 1024], P('dp', 'ctx'), may hold values from 0 to 3, never falling along the last dimension, each value on 1 to 384 neighbouring positions
- cotangent: bfloat16 [6, 1024, 2048], P('dp', 'ctx'), may hold values from -6 to 6
- norm1_gain: float32 [2048], replicated, may hold values from 0.5 to 1.5
- norm2_gain: float32 [2048], replicated, may hold values from 0.5 to 1.5
- head_gain: float32 [512], replicated, may hold values from 0.5 to 1.5
- decay_bias: float32 [256], replicated, may hold values from 0 to 10
- w_query: bfloat16 [2048, 2048], P(('dp', 'ctx'), 'tp'), may hold values from -0.375 to 0.375
- w_key: bfloat16 [2048, 2048], P(('dp', 'ctx'), 'tp'), may hold values from -0.375 to 0.375
- w_value: bfloat16 [2048, 2048], P(('dp', 'ctx'), 'tp'), may hold values from -0.125 to 0.125
- w_decay: bfloat16 [2048, 256], P(('dp', 'ctx'), 'tp'), may hold values from -0.125 to 0.125
- w_out: bfloat16 [2048, 2048], P('tp', ('dp', 'ctx')), may hold values from -0.125 to 0.125
- w_gate: bfloat16 [2048, 5632], P(('dp', 'ctx'), 'tp'), may hold values from -0.125 to 0.125
- w_up: bfloat16 [2048, 5632], P(('dp', 'ctx'), 'tp'), may hold values from -0.125 to 0.125
- w_down: bfloat16 [5632, 2048], P('tp', ('dp', 'ctx')), may hold values from -0.078125 to 0.078125
Outputs:
- output: bfloat16 [6, 1024, 2048], P('dp', 'ctx')
- input_grad: float32 [6, 1024, 2048], P('dp', 'ctx')
- norm1_gain_grad: float32 [2048], replicated
- norm2_gain_grad: float32 [2048], replicated
- head_gain_grad: float32 [512], replicated
- decay_bias_grad: float32 [256], replicated
- w_query_grad: float32 [2048, 2048], P(('dp', 'ctx'), 'tp')
- w_key_grad: float32 [2048, 2048], P(('dp', 'ctx'), 'tp')
- w_value_grad: float32 [2048, 2048], P(('dp', 'ctx'), 'tp')
- w_decay_grad: float32 [2048, 256], P(('dp', 'ctx'), 'tp')
- w_out_grad: float32 [2048, 2048], P('tp', ('dp', 'ctx'))
- w_gate_grad: float32 [2048, 5632], P(('dp', 'ctx'), 'tp')
- w_up_grad: float32 [2048, 5632], P(('dp', 'ctx'), 'tp')
- w_down_grad: float32 [5632, 2048], P('tp', ('dp', 'ctx'))
Inputs may be any that keep to these rules, and one draw needn't show every extreme that they name: `segments`: within each sequence the numbers never fall, start at 0 and take every value up to 3; a document holds 1 to 384 tokens, and some document holds exactly 384.
All inputs are finite; a program needn't handle non-finite values.
Results may differ from a plain program's by a relative error of at most 0.012.
The roundings to bfloat16 on the way count: a program that leaves them out, or rounds other values in their place, can miss the bound.
Values may be sent and summed in bfloat16 or wider, within the bound.
No kernel may reach another device: no remote copies, remote signals or barrier semaphores. Data moves between devices by JAX's collectives and lax.ppermute only.
A program may use at most 256 MiB of HBM per device.

v0:
```python
import jax
import jax.numpy as jnp
from jax import lax
from jax.sharding import PartitionSpec as P

HEADS = 4
HEAD_DIM = 512
SLOTS = 64


epsilon = 1e-05
gate_norm = 8.0
highest = lax.Precision.HIGHEST


def carried_in(x, axis, combine, identity, reverse):
    devices, index = (lax.axis_size(axis), lax.axis_index(axis))
    everything = jax.tree.map(lambda part: lax.all_gather(part, axis), x)
    start = jax.tree.map(
        lambda part, zero: jnp.broadcast_to(jnp.asarray(zero, part.dtype), part.shape), x, identity
    )

    def hop(k, before):
        at = devices - 1 - k if reverse else k
        reached = at > index if reverse else at < index
        new = combine(before, jax.tree.map(lambda part: part[at], everything))
        return jax.tree.map(lambda a, b: jnp.where(reached, a, b), new, before)

    return lax.fori_loop(0, devices, hop, start)


def matmul(left, right):
    return jnp.dot(left, right, precision=highest, preferred_element_type=jnp.float32)


def decay_terms(log_decay, seg_ids):
    count = log_decay.shape[0]
    levels = jnp.cumsum(log_decay, axis=0)
    position = jnp.arange(count)
    same_doc = (seg_ids[:, None] == seg_ids[None, :]) & (position[:, None] >= position[None, :])
    spread = jnp.where(same_doc[:, :, None], levels[:, None, :] - levels[None, :, :], -jnp.inf)
    weights = jnp.exp(spread) * (-jnp.expm1(log_decay))[None, :, :]
    carried = jnp.exp(levels) * (seg_ids == seg_ids[0]).astype(jnp.float32)[:, None]
    return (weights, carried)


def slot_full(queries, key_rows, values_all, log_decay, seg_ids, key_in, value_in):
    weights, carried = decay_terms(log_decay, seg_ids)
    qk_dots = matmul(queries, key_rows.T)
    scores = jnp.einsum("tsm,ts->tm", weights, qk_dots, precision=highest) + carried * matmul(
        queries, key_in.T
    )
    slot_probs = jax.nn.softmax(scores * HEAD_DIM ** (-0.5), axis=-1)
    mixing = jnp.einsum("tsm,tm->ts", weights, slot_probs, precision=highest)
    return matmul(mixing, values_all) + matmul(slot_probs * carried, value_in)


def slot_final(key_rows, values_all, log_decay, seg_ids, key_in, value_in):
    levels = jnp.cumsum(log_decay, axis=0)
    tail_weights = (
        jnp.exp(levels[-1][None, :] - levels)
        * -jnp.expm1(log_decay)
        * (seg_ids == seg_ids[-1]).astype(jnp.float32)[:, None]
    )
    decay_end = jnp.exp(levels[-1]) * (seg_ids[-1] == seg_ids[0]).astype(jnp.float32)
    return (
        decay_end[:, None] * key_in + matmul(tail_weights.T, key_rows),
        decay_end[:, None] * value_in + matmul(tail_weights.T, values_all),
    )


def slot_local(queries, key_rows, values_all, log_decay, seg_ids):
    weights, carried = decay_terms(log_decay, seg_ids)
    local_scores = jnp.einsum("tsm,ts->tm", weights, matmul(queries, key_rows.T), precision=highest)
    tail_weights = weights[-1]
    return (
        weights,
        carried,
        local_scores,
        carried[-1],
        matmul(tail_weights.T, key_rows),
        matmul(tail_weights.T, values_all),
    )


def slot_finish(queries, values_all, weights, carried, local_scores, key_in, value_in):
    scores = local_scores + carried * matmul(queries, key_in.T)
    slot_probs = jax.nn.softmax(scores * HEAD_DIM ** (-0.5), axis=-1)
    mixing = jnp.einsum("tsm,tm->ts", weights, slot_probs, precision=highest)
    return matmul(mixing, values_all) + matmul(slot_probs * carried, value_in)


def join_states(earlier, later):
    first_a, last_a, decay_a, key_a, value_a = earlier
    first_b, last_b, decay_b, key_b, value_b = later
    linked = ((last_a == first_b) | (last_a < -0.5) | (first_b < -0.5)).astype(jnp.float32)
    factor = linked * decay_b
    return (
        jnp.where(first_a < -0.5, first_b, first_a),
        jnp.where(last_b < -0.5, last_a, last_b),
        decay_a * factor,
        factor[..., None] * key_a + key_b,
        factor[..., None] * value_a + value_b,
    )


def join_grads(earlier, later):
    decay_a, key_a, value_a = earlier
    decay_b, key_b, value_b = later
    return (
        decay_b * decay_a,
        key_b + decay_b[..., None] * key_a,
        value_b + decay_b[..., None] * value_a,
    )


def rms_parts(array, gain_vec):
    factor = lax.rsqrt(jnp.mean(array * array, axis=-1, keepdims=True) + epsilon)
    unit_val = array * factor
    return (unit_val, factor, unit_val * gain_vec)


def norm_back(unit_val, factor, grad_unit):
    return factor * (grad_unit - unit_val * jnp.mean(grad_unit * unit_val, axis=-1, keepdims=True))


def per_device(
    layer_input,
    segments,
    cotangent,
    norm1_gain,
    norm2_gain,
    head_gain,
    decay_bias,
    w_query,
    w_key,
    w_value,
    w_decay,
    w_out,
    w_gate,
    w_up,
    w_down,
):
    micro_count, tok_rows, model_width = layer_input.shape
    heads_here = w_query.shape[1] // HEAD_DIM
    tp_place = lax.axis_index("tp")
    quarter = tok_rows // lax.axis_size("tp")
    bias_here = lax.dynamic_slice_in_dim(
        decay_bias, tp_place * (heads_here * SLOTS), heads_here * SLOTS
    )

    def fetch_weights():
        inner = (
            lax.all_gather(w_query, ("dp", "ctx"), axis=0, tiled=True),
            lax.all_gather(w_key, ("dp", "ctx"), axis=0, tiled=True),
            lax.all_gather(w_value, ("dp", "ctx"), axis=0, tiled=True),
            lax.all_gather(w_decay, ("dp", "ctx"), axis=0, tiled=True),
            lax.all_gather(w_gate, ("dp", "ctx"), axis=0, tiled=True),
            lax.all_gather(w_up, ("dp", "ctx"), axis=0, tiled=True),
        )
        outer = (
            lax.all_gather(w_out, ("dp", "ctx"), axis=1, tiled=True),
            lax.all_gather(w_down, ("dp", "ctx"), axis=1, tiled=True),
        )
        return tuple(inner) + tuple(outer)

    def split_heads(array):
        return array.reshape(tok_rows, heads_here, array.shape[-1] // heads_here).transpose(1, 0, 2)

    def merge_heads(array):
        return array.transpose(1, 0, 2).reshape(tok_rows, -1)

    def project(normed, gathered):
        queries = jnp.dot(normed, gathered[0], preferred_element_type=jnp.float32).astype(
            jnp.bfloat16
        )
        key_rows = jnp.dot(normed, gathered[1], preferred_element_type=jnp.float32).astype(
            jnp.bfloat16
        )
        values_all = jnp.dot(normed, gathered[2], preferred_element_type=jnp.float32).astype(
            jnp.bfloat16
        )
        logits = jnp.dot(normed, gathered[3], preferred_element_type=jnp.float32) + bias_here
        log_decay = split_heads(jax.nn.log_sigmoid(logits) / gate_norm)
        return (
            split_heads(queries).astype(jnp.float32),
            split_heads(key_rows).astype(jnp.float32),
            split_heads(values_all).astype(jnp.float32),
            logits,
            log_decay,
        )

    def quarter_sum(array):
        return jnp.sum(lax.dynamic_slice_in_dim(array, tp_place * quarter, quarter, 0), axis=0)

    kept_acts = []
    outputs = []
    for micro_index in range(micro_count):
        gathered = fetch_weights()
        seg_ids = segments[micro_index]
        inputs = layer_input[micro_index].astype(jnp.float32)
        unit_one, factor_one, scaled_one = rms_parts(inputs, norm1_gain)
        normed1 = scaled_one.astype(jnp.bfloat16)
        queries, key_rows, values_all, logits, log_decay = project(normed1, gathered)
        weights, carried, local_scores, decay_end, key_local, value_local = jax.vmap(
            slot_local, in_axes=(0, 0, 0, 0, None)
        )(queries, key_rows, values_all, log_decay, seg_ids)
        first_doc = seg_ids[0].astype(jnp.float32)
        last_doc = seg_ids[-1].astype(jnp.float32)
        identity = (
            jnp.float32(-1.0),
            jnp.float32(-1.0),
            jnp.ones_like(decay_end),
            jnp.zeros_like(key_local),
            jnp.zeros_like(value_local),
        )
        incoming = carried_in(
            (first_doc, last_doc, decay_end, key_local, value_local),
            "ctx",
            join_states,
            identity,
            False,
        )
        linked = (incoming[1] == first_doc).astype(jnp.float32)
        key_in = linked * incoming[3]
        value_in = linked * incoming[4]
        mixed_out = jax.vmap(slot_finish)(
            queries, values_all, weights, carried, local_scores, key_in, value_in
        )
        head_unit, head_factor, head_scaled = rms_parts(mixed_out, head_gain)
        normed_o = merge_heads(head_scaled).astype(jnp.bfloat16)
        attention = lax.psum(
            jnp.dot(normed_o, gathered[6], preferred_element_type=jnp.float32), "tp"
        )
        hidden = inputs + attention
        unit_two, factor_two, scaled_two = rms_parts(hidden, norm2_gain)
        normed2 = scaled_two.astype(jnp.bfloat16)
        gate_pre = jnp.dot(normed2, gathered[4], preferred_element_type=jnp.float32)
        up_pre = jnp.dot(normed2, gathered[5], preferred_element_type=jnp.float32)
        hidden_act = (jax.nn.silu(gate_pre) * up_pre).astype(jnp.bfloat16)
        feed_out = lax.psum(
            jnp.dot(hidden_act, gathered[7], preferred_element_type=jnp.float32).astype(
                jnp.bfloat16
            ),
            "tp",
        ).astype(jnp.float32)
        outputs.append((hidden + feed_out).astype(jnp.bfloat16))
        kept_acts.append((normed1, unit_one, factor_one, hidden, key_in, value_in, linked))
    totals = None
    small_totals = None
    input_grads = []
    for micro_index in range(micro_count):
        gathered = fetch_weights()
        normed1, unit_one, factor_one, hidden, key_in, value_in, linked = kept_acts[micro_index]
        seg_ids = segments[micro_index]
        grad_out = cotangent[micro_index].astype(jnp.float32)
        grad_feed = cotangent[micro_index]
        unit_two, factor_two, scaled_two = rms_parts(hidden, norm2_gain)
        normed2 = scaled_two.astype(jnp.bfloat16)
        gate_pre = jnp.dot(normed2, gathered[4], preferred_element_type=jnp.float32)
        up_pre = jnp.dot(normed2, gathered[5], preferred_element_type=jnp.float32)
        gate_sig = jax.nn.sigmoid(gate_pre)
        gate_silu = gate_pre * gate_sig
        hidden_act = (gate_silu * up_pre).astype(jnp.bfloat16)
        grad_wd = jnp.einsum("tf,td->fd", hidden_act, grad_feed, preferred_element_type=jnp.float32)
        grad_act = jnp.einsum(
            "td,fd->tf", grad_feed, gathered[7], preferred_element_type=jnp.float32
        )
        grad_gate = (grad_act * up_pre * gate_sig * (1.0 + gate_pre * (1.0 - gate_sig))).astype(
            jnp.bfloat16
        )
        grad_up = (grad_act * gate_silu).astype(jnp.bfloat16)
        grad_wg = jnp.einsum("td,tf->df", normed2, grad_gate, preferred_element_type=jnp.float32)
        grad_wu = jnp.einsum("td,tf->df", normed2, grad_up, preferred_element_type=jnp.float32)
        grad_part_two = jnp.einsum(
            "tf,df->td", grad_gate, gathered[4], preferred_element_type=jnp.float32
        ) + jnp.einsum("tf,df->td", grad_up, gathered[5], preferred_element_type=jnp.float32)
        grad_n2 = lax.psum(grad_part_two, "tp")
        gain_two_grad = quarter_sum(grad_n2 * unit_two)
        grad_hidden = grad_out + norm_back(unit_two, factor_two, grad_n2 * norm2_gain)
        grad_attn = grad_hidden.astype(jnp.bfloat16)
        queries, key_rows, values_all, logits, log_decay = project(normed1, gathered)

        def one_head(query_h, key_h, value_h, decay_h, key_state, value_state):
            return slot_full(query_h, key_h, value_h, decay_h, seg_ids, key_state, value_state)

        mixed_out, pull_out = jax.vjp(
            jax.vmap(one_head), queries, key_rows, values_all, log_decay, key_in, value_in
        )
        head_unit, head_factor, head_scaled = rms_parts(mixed_out, head_gain)
        normed_o = merge_heads(head_scaled).astype(jnp.bfloat16)
        grad_wo = jnp.einsum("th,td->hd", normed_o, grad_attn, preferred_element_type=jnp.float32)
        grad_normed_o = split_heads(
            jnp.einsum("td,hd->th", grad_attn, gathered[6], preferred_element_type=jnp.float32)
        )
        head_gain_part = jnp.sum(grad_normed_o * head_unit, axis=(0, 1))
        grad_mixed = norm_back(head_unit, head_factor, grad_normed_o * head_gain)
        grad_qh, grad_kh, grad_vh, grad_lh, grad_key_in, grad_value_in = pull_out(grad_mixed)
        decay_end = jnp.exp(jnp.cumsum(log_decay, axis=1)[:, -1]) * (
            seg_ids[-1] == seg_ids[0]
        ).astype(jnp.float32)
        back_identity = (
            jnp.ones_like(decay_end),
            jnp.zeros_like(grad_key_in),
            jnp.zeros_like(grad_value_in),
        )
        later = carried_in(
            (linked * decay_end, linked * grad_key_in, linked * grad_value_in),
            "ctx",
            join_grads,
            back_identity,
            True,
        )

        def one_state(key_h, value_h, decay_h, key_state, value_state):
            return slot_final(key_h, value_h, decay_h, seg_ids, key_state, value_state)

        def state_of(key_all, value_all, decay_all):
            return jax.vmap(one_state)(key_all, value_all, decay_all, key_in, value_in)

        _, pull_state = jax.vjp(state_of, key_rows, values_all, log_decay)
        state_k, state_v, state_l = pull_state((later[1], later[2]))
        grad_q = merge_heads(grad_qh).astype(jnp.bfloat16)
        grad_k = merge_heads(grad_kh + state_k).astype(jnp.bfloat16)
        grad_v = merge_heads(grad_vh + state_v).astype(jnp.bfloat16)
        grad_logits = (merge_heads(grad_lh + state_l) * jax.nn.sigmoid(-logits) / gate_norm).astype(
            jnp.bfloat16
        )
        grad_wq = jnp.einsum("td,th->dh", normed1, grad_q, preferred_element_type=jnp.float32)
        grad_wk = jnp.einsum("td,th->dh", normed1, grad_k, preferred_element_type=jnp.float32)
        grad_wv = jnp.einsum("td,th->dh", normed1, grad_v, preferred_element_type=jnp.float32)
        grad_wf = jnp.einsum("td,th->dh", normed1, grad_logits, preferred_element_type=jnp.float32)
        bias_part = lax.dynamic_update_slice_in_dim(
            jnp.zeros((HEADS * SLOTS,), jnp.float32),
            jnp.sum(grad_logits.astype(jnp.float32), axis=0),
            tp_place * (heads_here * SLOTS),
            0,
        )
        grad_part_one = (
            jnp.einsum("th,dh->td", grad_q, gathered[0], preferred_element_type=jnp.float32)
            + jnp.einsum("th,dh->td", grad_k, gathered[1], preferred_element_type=jnp.float32)
            + jnp.einsum("th,dh->td", grad_v, gathered[2], preferred_element_type=jnp.float32)
            + jnp.einsum("th,dh->td", grad_logits, gathered[3], preferred_element_type=jnp.float32)
        )
        grad_n1 = lax.psum(grad_part_one, "tp")
        gain_one_grad = quarter_sum(grad_n1 * unit_one)
        input_grads.append(grad_hidden + norm_back(unit_one, factor_one, grad_n1 * norm1_gain))
        grads_now = (grad_wq, grad_wk, grad_wv, grad_wf, grad_wg, grad_wu, grad_wo, grad_wd)
        small_now = (gain_one_grad, gain_two_grad, head_gain_part, bias_part)
        totals = grads_now if totals is None else jax.tree.map(jnp.add, totals, grads_now)
        small_totals = (
            small_now if small_totals is None else jax.tree.map(jnp.add, small_totals, small_now)
        )
    small_sums = lax.psum(
        (small_totals[0], small_totals[1], small_totals[2], small_totals[3]), ("dp", "ctx", "tp")
    )
    rows_sum = (
        lax.psum_scatter(totals[0], ("dp", "ctx"), scatter_dimension=0, tiled=True),
        lax.psum_scatter(totals[1], ("dp", "ctx"), scatter_dimension=0, tiled=True),
        lax.psum_scatter(totals[2], ("dp", "ctx"), scatter_dimension=0, tiled=True),
        lax.psum_scatter(totals[3], ("dp", "ctx"), scatter_dimension=0, tiled=True),
        lax.psum_scatter(totals[4], ("dp", "ctx"), scatter_dimension=0, tiled=True),
        lax.psum_scatter(totals[5], ("dp", "ctx"), scatter_dimension=0, tiled=True),
    )
    cols_sum = (
        lax.psum_scatter(totals[6], ("dp", "ctx"), scatter_dimension=1, tiled=True),
        lax.psum_scatter(totals[7], ("dp", "ctx"), scatter_dimension=1, tiled=True),
    )
    return (
        jnp.stack(outputs),
        jnp.stack(input_grads),
        small_sums[0],
        small_sums[1],
        small_sums[2],
        small_sums[3],
        rows_sum[0],
        rows_sum[1],
        rows_sum[2],
        rows_sum[3],
        cols_sum[0],
        rows_sum[4],
        rows_sum[5],
        cols_sum[1],
    )


def solution(mesh):
    return jax.shard_map(
        per_device,
        mesh=mesh,
        in_specs=(
            P("dp", "ctx", None),
            P("dp", "ctx"),
            P("dp", "ctx", None),
            P(),
            P(),
            P(),
            P(),
            P(("dp", "ctx"), "tp"),
            P(("dp", "ctx"), "tp"),
            P(("dp", "ctx"), "tp"),
            P(("dp", "ctx"), "tp"),
            P("tp", ("dp", "ctx")),
            P(("dp", "ctx"), "tp"),
            P(("dp", "ctx"), "tp"),
            P("tp", ("dp", "ctx")),
        ),
        out_specs=(
            P("dp", "ctx", None),
            P("dp", "ctx", None),
            P(),
            P(),
            P(),
            P(),
            P(("dp", "ctx"), "tp"),
            P(("dp", "ctx"), "tp"),
            P(("dp", "ctx"), "tp"),
            P(("dp", "ctx"), "tp"),
            P("tp", ("dp", "ctx")),
            P(("dp", "ctx"), "tp"),
            P(("dp", "ctx"), "tp"),
            P("tp", ("dp", "ctx")),
        ),
        check_vma=False,
    )
```

profile of v0, /device:TPU:0, one launch (start us, length us, event | category | flops | bytes accessed | tf_op | source)
XLA Modules:
  0.0 2172.7 jit_solution(5432649835595384970)
XLA Ops:
  27.1 26.2 %all_gather.193 = bf16[2048,64]{0,1:T(8,128)(2,1)S(1)} all-gather(bf16[256,64]{0,1:T(8,128)(2,1)S(1)} %copy-done.283), channel_id=1, replica_groups=mesh['dp'=2,'ctx'=4,'tp'=4] {'dp','ctx'}, dimensions={0}, use_global_device_ids=true | all-gather | bytes 294912 | tf_op jit(solution)/shard_map/all_gather | solution.py:157
  147.3 10.1 all-reduce.16
  163.2 30.6 %fusion.32 = f32[256,1,64]{2,1,0:T(1,128)} fusion(f32[256,64]{0,1:T(8,128)S(1)} %copy-done.203, f32[256,64]{0,1:T(8,128)S(1)} %copy-done.226, f32[256,64]{1,0:T(8,128)S(1)} %bitcast.1220, pred[256,256]{1,0:T(8,128)(4,1)S(1)} %copy-done.238, f32[256,256,1]{1,0,2:T(8,128)S(1)} %bitcast.1267), kind=kOutput, calls=%fused_computation.65 | convolution fusion | flops 62914560 | bytes 589824 | tf_op jit(solution)/shard_map/vmap(tsm,ts->tm)/dot_general | solution.py:74
  199.8 10.6 all-gather
  220.4 30.4 %while.108 = (s32[]{:T(128)}, f32[]{:T(128)}, f32[1,64,512]{2,1,0:T(8,128)}, f32[1,64,512]{2,1,0:T(8,128)}, s32[]{:T(128)}, /*index=5*/f32[4]{0:T(128)}, f32[4]{...) while((s32[]{:T(128)}, f32[]{:T(128)}, ...), condition=%wide.region_4.5_spmd.clone, body=%wide.region_3.4_spmd.clone.sunk | while | flops 262221 | bytes 787470 | solution.py:29
  254.0 13.3 fusion.31
  272.0 17.8 fusion.28
  293.5 10.3 all-gather.2
  303.9 10.3 all-gather.3
  314.1 28.2 %while.109 = (s32[]{:T(128)}, f32[]{:T(128)}, f32[1,64,512]{2,1,0:T(8,128)}, f32[1,64,512]{2,1,0:T(8,128)}, s32[]{:T(128)}, /*index=5*/f32[4]{0:T(128)S(1)}, f32...) while((s32[]{:T(128)}, f32[]{:T(128)}, ...), condition=%wide.region_15.16_spmd.clone, body=%wide.region_14.15_spmd.clone.sunk | while | flops 262221 | bytes 787470 | solution.py:29
  346.0 17.8 fusion.24
  367.5 10.1 all-gather.4
  377.6 10.3 all-gather.5
  387.9 27.8 %while.110 = (s32[]{:T(128)}, f32[]{:T(128)}, f32[1,64,512]{2,1,0:T(8,128)}, f32[1,64,512]{2,1,0:T(8,128)}, s32[]{:T(128)}, /*index=5*/f32[4]{0:T(128)S(1)}, f32...) while((s32[]{:T(128)}, f32[]{:T(128)}, ...), condition=%wide.region_26.27_spmd.clone, body=%wide.region_25.26_spmd.clone.sunk | while | flops 262221 | bytes 787470 | solution.py:29
  422.2 12.3 fusion.27
  436.6 12.1 fusion.23
  460.9 221.6 %all-reduce.27.cloned.1.call-done = (f32[256,2048]{1,0:T(8,128)}, f32[256,2048]{1,0:T(8,128)}, f32[256,2048]{1,0:T(8,128)}) async-done(((f32[256,2048]{1,0:T(8,128)}, f32[256,2048]{1,0:T(8,128)}, f32[256,2048]{1,0:T(8,128)}), (f32[256,2048]{1,0:T(8,128)}, f32[256,2048]{1,0:T(8,128)}, f32[256,2048]{1,0:T(8,128)})) %all-reduce.27.cloned.1.call-update) | async-done | bytes 6291472 | tf_op jit(solution)/shard_map/psum | solution.py:232
  692.2 34.4 %all-gather.30.cloned.1.call-done = bf16[2048,1408]{1,0:T(8,128)(2,1)} async-done(((bf16[256,1408]{1,0:T(8,128)(2,1)}), bf16[2048,1408]{1,0:T(8,128)(2,1)}) %all-gather.30.cloned.1.call-update) | async-done | bytes 5767184 | tf_op jit(solution)/shard_map/all_gather | solution.py:159
  732.5 39.3 %all-gather.28.cloned.1.call-done = bf16[2048,1408]{1,0:T(8,128)(2,1)} async-done(((bf16[256,1408]{1,0:T(8,128)(2,1)}), bf16[2048,1408]{1,0:T(8,128)(2,1)}) %all-gather.28.cloned.1.call-update) | async-done | bytes 5767184 | tf_op jit(solution)/shard_map/all_gather | solution.py:158
  789.2 28.8 %all-gather.32.cloned.1.call-done = bf16[1408,2048]{1,0:T(8,128)(2,1)} async-done(((bf16[1408,256]{1,0:T(8,128)(2,1)}), bf16[1408,2048]{1,0:T(8,128)(2,1)}) %all-gather.32.cloned.1.call-update) | async-done | bytes 5767184 | tf_op jit(solution)/shard_map/all_gather | solution.py:163
  901.3 174.6 %all-reduce.25.cloned.1.call-done = (f32[256,2048]{1,0:T(8,128)}, f32[256,2048]{1,0:T(8,128)}, f32[256,2048]{1,0:T(8,128)}) async-done(((f32[256,2048]{1,0:T(8,128)}, f32[256,2048]{1,0:T(8,128)}, f32[256,2048]{1,0:T(8,128)}), (f32[256,2048]{1,0:T(8,128)}, f32[256,2048]{1,0:T(8,128)}, f32[256,2048]{1,0:T(8,128)})) %all-reduce.25.cloned.1.call-update) | async-done | bytes 6291472 | tf_op jit(solution)/shard_map/psum | solution.py:278
  1105.9 15.8 fusion.26
  1122.8 11.1 fusion.25
  1136.5 16.2 fusion.30
  1154.1 11.3 fusion.29
  1167.8 10.4 all-gather.8
  1178.2 11.0 all-gather.9
  1197.8 16.9 fusion.22
  1215.5 10.5 all-gather.10
  1226.0 10.4 all-gather.11
  1245.0 10.9 all-gather.6
  1255.9 10.6 all-gather.7
  1274.9 13.3 fusion.34
  1288.9 11.6 fusion.21
  1300.6 12.6 fusion.38
  1314.0 13.4 fusion.36
  1455.6 10.9 add_add_fusion.1
  1476.2 11.0 add_add_fusion.2
  1496.6 10.9 add_add_fusion
  1512.6 121.7 %all-reduce.23.cloned.1.call-done = (f32[256,2048]{1,0:T(8,128)}, f32[256,2048]{1,0:T(8,128)}, f32[256,2048]{1,0:T(8,128)}) async-done(((f32[256,2048]{1,0:T(8,128)}, f32[256,2048]{1,0:T(8,128)}, f32[256,2048]{1,0:T(8,128)}), (f32[256,2048]{1,0:T(8,128)}, f32[256,2048]{1,0:T(8,128)}, f32[256,2048]{1,0:T(8,128)})) %all-reduce.23.cloned.1.call-update) | async-done | bytes 6291472 | tf_op jit(solution)/shard_map/psum | solution.py:345
  1648.6 39.6 %all-reduce.12 = (f32[2048]{0:T(1024)}, f32[2048]{0:T(1024)}, f32[512]{0:T(512)}, f32[256]{0:T(256)}) all-reduce(f32[2048]{0:T(1024)S(1)} %add_add_fusion.8, f32[2048]{0:T(1024)S(1)} %add_add_fusion.7, f32[512]{0:T(512)S(1)} %add_add_fusion.9, ...), channel_id=1, replica_groups=mesh['dp'=2,'ctx'=4,'tp'=4] {'dp','ctx','tp'}, use_global_device_ids=true, to_apply=%region_90.91 | all-reduce | flops 4864 | bytes 38912 | tf_op jit(solution)/shard_map/psum | solution.py:354
  1695.5 31.3 %reduce-scatter.17.cloned.1.call-done = f32[512,256]{1,0:T(8,128)} async-done(((f32[512,2048]{1,0:T(8,128)}), f32[512,256]{1,0:T(8,128)}) %reduce-scatter.17.cloned.1.call-update) | async-done | bytes 524304 | tf_op jit(solution)/shard_map/reduce_scatter | solution.py:366
  1726.7 55.1 %reduce-scatter.13.cloned.1.call-done = f32[256,512]{1,0:T(8,128)} async-done(((f32[2048,512]{1,0:T(8,128)}), f32[256,512]{1,0:T(8,128)}) %reduce-scatter.13.cloned.1.call-update) | async-done | bytes 524304 | tf_op jit(solution)/shard_map/reduce_scatter | solution.py:360
  1781.8 55.5 %reduce-scatter.11.cloned.1.call-done = f32[256,512]{1,0:T(8,128)} async-done(((f32[2048,512]{1,0:T(8,128)}), f32[256,512]{1,0:T(8,128)}) %reduce-scatter.11.cloned.1.call-update) | async-done | bytes 524304 | tf_op jit(solution)/shard_map/reduce_scatter | solution.py:359
  1837.3 55.1 %reduce-scatter.9.cloned.1.call-done = f32[256,512]{1,0:T(8,128)} async-done(((f32[2048,512]{1,0:T(8,128)}), f32[256,512]{1,0:T(8,128)}) %reduce-scatter.9.cloned.1.call-update) | async-done | bytes 524304 | tf_op jit(solution)/shard_map/reduce_scatter | solution.py:358
  1892.5 91.1 %reduce-scatter.21.cloned.1.call-done = f32[256,1408]{1,0:T(8,128)} async-done(((f32[2048,1408]{1,0:T(8,128)}), f32[256,1408]{1,0:T(8,128)}) %reduce-scatter.21.cloned.1.call-update) | async-done | bytes 1441808 | tf_op jit(solution)/shard_map/reduce_scatter | solution.py:363
  1983.6 91.1 %reduce-scatter.19.cloned.1.call-done = f32[256,1408]{1,0:T(8,128)} async-done(((f32[2048,1408]{1,0:T(8,128)}), f32[256,1408]{1,0:T(8,128)}) %reduce-scatter.19.cloned.1.call-update) | async-done | bytes 1441808 | tf_op jit(solution)/shard_map/reduce_scatter | solution.py:362
  2074.7 91.3 %reduce-scatter.23.cloned.1.call-done = f32[1408,256]{1,0:T(8,128)} async-done(((f32[1408,2048]{1,0:T(8,128)}), f32[1408,256]{1,0:T(8,128)}) %reduce-scatter.23.cloned.1.call-update) | async-done | bytes 1441808 | tf_op jit(solution)/shard_map/reduce_scatter | solution.py:367
  (1112 shorter events, 593.9 us)
Async XLA Ops:
  7.2 150.2 %all-gather.22.cloned.1.call-start = ((), (), s32[]{:S(2)}) async-start(), calls=%async_computation.9 | async-start | bytes 2359296 | tf_op jit(solution)/shard_map/all_gather | solution.py:155
  7.9 152.5 %all-gather.20.cloned.1.call-start = ((), (), s32[]{:S(2)}) async-start(), calls=%async_computation.8 | async-start | bytes 2359296 | tf_op jit(solution)/shard_map/all_gather | solution.py:154
  8.7 44.6 %copy-start.319 = (f32[256]{0:T(256)S(1)}, f32[256]{0:T(256)}, u32[]{:S(2)}) copy-start(f32[256]{0:T(256)} %param.33) | copy-start | bytes 3076
  8.7 44.7 %copy-start = (bf16[3,256,2048]{2,1,0:T(8,128)(2,1)S(1)}, bf16[3,256,2048]{2,1,0:T(8,128)(2,1)}, u32[]{:S(2)}) copy-start(bf16[3,256,2048]{2,1,0:T(8,128)(2,1)} %param.27) | copy-start | bytes 9437188
  8.7 44.7 %copy-start.86 = (f32[2048]{0:T(1024)S(1)}, f32[2048]{0:T(1024)}, u32[]{:S(2)}) copy-start(f32[2048]{0:T(1024)} %param.30) | copy-start | bytes 24580
  8.7 186.8 %all-gather.24.cloned.1.call-start = ((), (), s32[]{:S(2)}) async-start(), calls=%async_computation.10 | async-start | bytes 2359296 | tf_op jit(solution)/shard_map/all_gather | solution.py:156
  9.4 441.1 %all-gather.26.cloned.1.call-start = ((), (), s32[]{:S(2)}) async-start(), calls=%async_computation.11 | async-start | bytes 2359296 | tf_op jit(solution)/shard_map/all_gather | solution.py:162
  10.0 672.5 %all-reduce.27.cloned.1.call-start = ((), (), s32[]{:S(2)}) async-start(), calls=%async_computation.25 | async-start | bytes 12582912 | tf_op jit(solution)/shard_map/psum | solution.py:232
  58.5 137.0 %copy-start.259 = (f32[256]{0:T(256)}, f32[256]{0:T(256)S(1)}, u32[]{:S(2)}) copy-start(f32[256]{0:T(256)S(1)} %get-tuple-element.1767) | copy-start | bytes 3076
  58.5 232.4 %copy-start.257 = (f32[256]{0:T(256)}, f32[256]{0:T(256)S(1)}, u32[]{:S(2)}) copy-start(f32[256]{0:T(256)S(1)} %get-tuple-element.1766) | copy-start | bytes 3076
  162.9 30.9 %copy-start.101 = (bf16[256,512]{1,0:T(8,128)(2,1)}, bf16[256,512]{1,0:T(8,128)(2,1)S(1)}, u32[]{:S(2)}) copy-start(bf16[256,512]{1,0:T(8,128)(2,1)S(1)} %convolution_convert_fusion.11) | copy-start | bytes 786436
  163.2 30.6 %copy-start.246 = (f32[256,256]{1,0:T(8,128)}, f32[256,256]{1,0:T(8,128)S(1)}, u32[]{:S(2)}) copy-start(f32[256,256]{1,0:T(8,128)S(1)} %fusion.430) | copy-start | bytes 786436
  421.9 28.7 %copy-start.267 = (f32[256]{0:T(256)}, f32[256]{0:T(256)S(1)}, u32[]{:S(2)}) copy-start(f32[256]{0:T(256)S(1)} %add_rsqrt_fusion.7) | copy-start | bytes 3076
  450.5 641.8 %copy-start.262 = (f32[256]{0:T(256)}, f32[256]{0:T(256)S(1)}, u32[]{:S(2)}) copy-start(f32[256]{0:T(256)S(1)} %add_rsqrt_fusion.1) | copy-start | bytes 3076
  458.8 267.8 %all-gather.30.cloned.1.call-start = ((), (), s32[]{:S(2)}) async-start(), calls=%async_computation.13 | async-start | bytes 6488064 | tf_op jit(solution)/shard_map/all_gather | solution.py:159
  459.4 312.4 %all-gather.28.cloned.1.call-start = ((), (), s32[]{:S(2)}) async-start(), calls=%async_computation.12 | async-start | bytes 6488064 | tf_op jit(solution)/shard_map/all_gather | solution.py:158
  460.1 358.0 %all-gather.32.cloned.1.call-start = ((), (), s32[]{:S(2)}) async-start(), calls=%async_computation.14 | async-start | bytes 6488064 | tf_op jit(solution)/shard_map/all_gather | solution.py:163
  460.9 615.1 %all-reduce.25.cloned.1.call-start = ((), (), s32[]{:S(2)}) async-start(), calls=%async_computation.24 | async-start | bytes 12582912 | tf_op jit(solution)/shard_map/psum | solution.py:278
  726.6 45.2 %copy-start.36 = (bf16[256,2048]{1,0:T(8,128)(2,1)S(1)}, bf16[256,2048]{1,0:T(8,128)(2,1)}, u32[]{:S(2)}) copy-start(bf16[256,2048]{1,0:T(8,128)(2,1)} %get-tuple-element.1662) | copy-start | bytes 3145732
  732.5 45.0 %copy-start.39 = (bf16[256,2048]{1,0:T(8,128)(2,1)S(1)}, bf16[256,2048]{1,0:T(8,128)(2,1)}, u32[]{:S(2)}) copy-start(bf16[256,2048]{1,0:T(8,128)(2,1)} %get-tuple-element.1698) | copy-start | bytes 3145732
  786.3 31.7 %copy-start.33 = (bf16[3,256,2048]{2,1,0:T(8,128)(2,1)S(1)}, bf16[3,256,2048]{2,1,0:T(8,128)(2,1)}, u32[]{:S(2)}) copy-start(bf16[3,256,2048]{2,1,0:T(8,128)(2,1)} %param.29) | copy-start | bytes 9437188
  852.2 30.8 %copy-start.285 = (f32[256]{0:T(256)S(1)}, f32[256]{0:T(256)}, u32[]{:S(2)}) copy-start(f32[256]{0:T(256)} %copy-done.284) | copy-start | bytes 3076
  852.2 31.4 %copy-start.291 = (f32[256]{0:T(256)S(1)}, f32[256]{0:T(256)}, u32[]{:S(2)}) copy-start(f32[256]{0:T(256)} %copy-done.290) | copy-start | bytes 3076
  852.2 31.9 %copy-start.288 = (f32[256]{0:T(256)S(1)}, f32[256]{0:T(256)}, u32[]{:S(2)}) copy-start(f32[256]{0:T(256)} %copy-done.287) | copy-start | bytes 3076
  852.2 32.5 %copy-start.78 = (f32[1,256,64]{2,1,0:T(8,128)S(1)}, f32[1,256,64]{2,1,0:T(8,128)}, u32[]{:S(2)}) copy-start(f32[1,256,64]{2,1,0:T(8,128)} %copy-done.77) | copy-start | bytes 196612
  852.2 32.5 %copy-start.271 = (f32[256]{0:T(256)S(1)}, f32[256]{0:T(256)}, u32[]{:S(2)}) copy-start(f32[256]{0:T(256)} %copy-done.270) | copy-start | bytes 3076
  852.2 33.3 %copy-start.84 = (f32[1,256,64]{2,1,0:T(8,128)S(1)}, f32[1,256,64]{2,1,0:T(8,128)}, u32[]{:S(2)}) copy-start(f32[1,256,64]{2,1,0:T(8,128)} %copy-done.83) | copy-start | bytes 196612
  852.2 33.3 %copy-start.277 = (f32[256]{0:T(256)S(1)}, f32[256]{0:T(256)}, u32[]{:S(2)}) copy-start(f32[256]{0:T(256)} %copy-done.276) | copy-start | bytes 3076
  852.2 34.1 %copy-start.81 = (f32[1,256,64]{2,1,0:T(8,128)S(1)}, f32[1,256,64]{2,1,0:T(8,128)}, u32[]{:S(2)}) copy-start(f32[1,256,64]{2,1,0:T(8,128)} %copy-done.80) | copy-start | bytes 196612
  852.2 34.1 %copy-start.274 = (f32[256]{0:T(256)S(1)}, f32[256]{0:T(256)}, u32[]{:S(2)}) copy-start(f32[256]{0:T(256)} %copy-done.273) | copy-start | bytes 3076
  852.2 34.9 %copy-start.176 = (bf16[256,1408]{1,0:T(8,128)(2,1)S(1)}, bf16[256,1408]{1,0:T(8,128)(2,1)}, u32[]{:S(2)}) copy-start(bf16[256,1408]{1,0:T(8,128)(2,1)} %get-tuple-element.1713) | copy-start | bytes 2162692
  852.3 660.4 %all-reduce.29.cloned.1.call-start = ((), (), s32[]{:S(2)}) async-start(), calls=%async_computation.26 | async-start | bytes 6291456 | tf_op jit(solution)/shard_map/psum | solution.py:241
  901.3 174.7 %copy-start.11 = (f32[256,2048]{1,0:T(8,128)S(1)}, f32[256,2048]{1,0:T(8,128)}, u32[]{:S(2)}) copy-start(f32[256,2048]{1,0:T(8,128)} %get-tuple-element.1699) | copy-start | bytes 6291460
  901.3 733.1 %all-reduce.23.cloned.1.call-start = ((), (), s32[]{:S(2)}) async-start(), calls=%async_computation.23 | async-start | bytes 12582912 | tf_op jit(solution)/shard_map/psum | solution.py:345
  1093.8 59.2 %copy-start.158 = (f32[1,256,64]{2,1,0:T(8,128)}, f32[1,256,64]{2,1,0:T(8,128)S(1)}, u32[]{:S(2)}) copy-start(f32[1,256,64]{2,1,0:T(8,128)S(1)} %convolution_bitcast_fusion.8) | copy-start | bytes 196612
  1098.7 37.7 %copy-start.253 = (f32[256,256]{1,0:T(8,128)}, f32[256,256]{1,0:T(8,128)S(1)}, u32[]{:S(2)}) copy-start(f32[256,256]{1,0:T(8,128)S(1)} %fusion.440) | copy-start | bytes 786436
  1215.2 115.7 %copy-start.150 = (f32[1,256,64]{2,1,0:T(8,128)}, f32[1,256,64]{2,1,0:T(8,128)S(1)}, u32[]{:S(2)}) copy-start(f32[1,256,64]{2,1,0:T(8,128)S(1)} %multiply_multiply_fusion) | copy-start | bytes 196612
  1412.5 283.0 %reduce-scatter.15.cloned.1.call-start = ((), (), s32[]{:S(2)}) async-start(), calls=%async_computation.18 | async-start | bytes 589824 | tf_op jit(solution)/shard_map/reduce_scatter | solution.py:361
  1422.2 304.5 %reduce-scatter.17.cloned.1.call-start = ((), (), s32[]{:S(2)}) async-start(), calls=%async_computation.19 | async-start | bytes 4718592 | tf_op jit(solution)/shard_map/reduce_scatter | solution.py:366
  1428.9 352.9 %reduce-scatter.13.cloned.1.call-start = ((), (), s32[]{:S(2)}) async-start(), calls=%async_computation.17 | async-start | bytes 4718592 | tf_op jit(solution)/shard_map/reduce_scatter | solution.py:360
  1434.7 402.6 %reduce-scatter.11.cloned.1.call-start = ((), (), s32[]{:S(2)}) async-start(), calls=%async_computation.16 | async-start | bytes 4718592 | tf_op jit(solution)/shard_map/reduce_scatter | solution.py:359
  1439.7 452.8 %reduce-scatter.9.cloned.1.call-start = ((), (), s32[]{:S(2)}) async-start(), calls=%async_computation.15 | async-start | bytes 4718592 | tf_op jit(solution)/shard_map/reduce_scatter | solution.py:358
  1445.6 538.1 %reduce-scatter.21.cloned.1.call-start = ((), (), s32[]{:S(2)}) async-start(), calls=%async_computation.21 | async-start | bytes 12976128 | tf_op jit(solution)/shard_map/reduce_scatter | solution.py:363
  1466.5 608.2 %reduce-scatter.19.cloned.1.call-start = ((), (), s32[]{:S(2)}) async-start(), calls=%async_computation.20 | async-start | bytes 12976128 | tf_op jit(solution)/shard_map/reduce_scatter | solution.py:362
  1487.2 678.8 %reduce-scatter.23.cloned.1.call-start = ((), (), s32[]{:S(2)}) async-start(), calls=%async_computation.22 | async-start | bytes 12976128 | tf_op jit(solution)/shard_map/reduce_scatter | solution.py:367
  1648.4 39.9 %copy-start.105 = (bf16[1,256,2048]{2,1,0:T(8,128)(2,1)S(1)}, bf16[1,256,2048]{2,1,0:T(8,128)(2,1)}, u32[]{:S(2)}) copy-start(bf16[1,256,2048]{2,1,0:T(8,128)(2,1)} %get-tuple-element.1705) | copy-start | bytes 3145732
  1648.4 39.9 %copy-start.106 = (bf16[1,256,2048]{2,1,0:T(8,128)(2,1)S(1)}, bf16[1,256,2048]{2,1,0:T(8,128)(2,1)}, u32[]{:S(2)}) copy-start(bf16[1,256,2048]{2,1,0:T(8,128)(2,1)} %get-tuple-element.1706) | copy-start | bytes 3145732
  1648.4 39.9 %copy-start.107 = (bf16[1,256,2048]{2,1,0:T(8,128)(2,1)S(1)}, bf16[1,256,2048]{2,1,0:T(8,128)(2,1)}, u32[]{:S(2)}) copy-start(bf16[1,256,2048]{2,1,0:T(8,128)(2,1)} %get-tuple-element.1707) | copy-start | bytes 3145732
  (305 other events, 2227.9 us)
Sparse Core Ops, SparseCore 0:
  9.9 32.0 all-gather.21
  43.9 27.8 all-gather.19
  73.7 27.8 all-gather.23
  103.3 28.1 all-gather.25
  458.9 223.5 all-reduce.26
  684.3 42.2 all-gather.29
  728.5 43.3 all-gather.27
  773.7 44.3 all-gather.31
  852.4 223.5 all-reduce.24
  1078.4 120.7 all-reduce.28
  1412.6 221.7 all-reduce.22
  1637.9 33.1 reduce-scatter.14
  1675.4 51.3 reduce-scatter.16
  1730.5 51.2 reduce-scatter.12
  1786.0 51.3 reduce-scatter.10
  1841.1 51.2 reduce-scatter.8
  1896.8 86.7 reduce-scatter.20
  1987.9 86.7 reduce-scatter.18
  2079.2 86.7 reduce-scatter.22
where the time goes:
time: 2180 us; the launch traced here: 2170 us
  waiting for transfers between devices  1100 us (50%)
  matrix products  458 us (21%)
  blocking collectives  250 us (11%)
  other arithmetic  199 us (9%)
  local copies, waits for them, and re-layouts  111 us (5%)
  loops' own time  32.1 us (1%)
  between operations  25.7 us (1%)
    psum x1, waiting for transfers between devices, per_device(): lax.psum(jnp.dot(normed_o, gathered[6], preferred_element_type=jnp.float3...  222 us
    psum x1, waiting for transfers between devices, per_device(): grad_n2 = lax.psum(grad_part_two, 'tp')  175 us
    all_gather x18, blocking collectives, carried_in(): everything = jax.tree.map(lambda part: lax.all_gather(part, axis), x)  174 us
    psum x1, waiting for transfers between devices, per_device(): grad_n1 = lax.psum(grad_part_one, 'tp')  122 us
    reduce_scatter x1, waiting for transfers between devices, per_device(): lax.psum_scatter(totals[7], ('dp', 'ctx'), scatter_dimension=1, tiled=True)  91.3 us
    reduce_scatter x1, waiting for transfers between devices, per_device(): lax.psum_scatter(totals[5], ('dp', 'ctx'), scatter_dimension=0, tiled=True)  91.1 us
    reduce_scatter x1, waiting for transfers between devices, per_device(): lax.psum_scatter(totals[4], ('dp', 'ctx'), scatter_dimension=0, tiled=True)  91.1 us
    dot_general x3, matrix products, slot_local(): jnp.einsum('tsm,ts->tm', weights, matmul(queries, key_rows.T), precision=...  66.3 us
  transfers between devices with their start and end apart: 19, of which 13 were waited for; matrix products, arithmetic and copies ran while one was open for 32% of the time, Pallas kernels for 0%

commit v1 on v0

v1 whole, which is shorter than its diff:
```python
import jax
import jax.numpy as jnp
from jax import lax
from jax.experimental import pallas as pl
from jax.experimental.pallas import tpu as pltpu
from jax.sharding import PartitionSpec as P

HEAD_DIM = 512
SLOTS = 64
CHUNK = 32
epsilon = 1e-05
gate_norm = 8.0
f32 = jnp.float32
bf16 = jnp.bfloat16
NEG = -1e30
SCALE = HEAD_DIM**-0.5


def split2(x):
    high = x.astype(bf16)
    return high, (x - high.astype(f32)).astype(bf16)


def dg(a, b, ca, cb):
    return lax.dot_general(a, b, (((ca,), (cb,)), ((), ())), preferred_element_type=f32)


def dot2(a, b, ca, cb):
    high, low = a
    return dg(high, b, ca, cb) + dg(low, b, ca, cb)


def dot2r(a, b, ca, cb):
    high, low = b
    return dg(a, high, ca, cb) + dg(a, low, ca, cb)


def dot3(a, b, ca, cb):
    return dg(a[0], b[0], ca, cb) + (dg(a[0], b[1], ca, cb) + dg(a[1], b[0], ca, cb))


def group_lane(x, index):
    rows, lanes = x.shape
    lane = lax.broadcasted_iota(jnp.int32, (rows, 128), 1)
    at = (lane // CHUNK) * CHUNK + index
    parts = [
        jnp.take_along_axis(x[:, i : i + 128], at, axis=1, mode="promise_in_bounds")
        for i in range(0, lanes, 128)
    ]
    return jnp.concatenate(parts, axis=1)


def chunk_of(rows, lanes):
    return lax.broadcasted_iota(jnp.int32, (rows, lanes), 1) // CHUNK


def pick_rows(array, rows, chunks, first=0):
    lanes = array.shape[1]
    chunk = chunk_of(rows, lanes)
    total = jnp.zeros((rows, lanes), f32)
    for c in range(first, chunks):
        total = jnp.where(chunk == c, array[(c - first) * rows : (c - first + 1) * rows], total)
    return total


def level_refs(levels):
    slots, tokens = levels.shape
    chunk = chunk_of(slots, tokens)
    refs = jnp.zeros_like(levels)
    for c in range(1, tokens // CHUNK):
        refs = jnp.where(chunk == c, levels[:, c * CHUNK - 1 : c * CHUNK], refs)
    return refs


def stack_chunks(array, chunks):
    chunk = chunk_of(*array.shape)
    return jnp.concatenate([jnp.where(chunk == c, array, 0.0) for c in range(1, chunks)], axis=0)


def aux_rows(tokens):
    chunks = tokens // CHUNK
    base = 2 * CHUNK + chunks
    return base, base + 8


def make_aux(seg, prev_doc):
    count, tokens = seg.shape
    chunks = tokens // CHUNK
    place = jnp.arange(tokens)
    local = place % CHUNK
    grouped = seg.reshape(count, chunks, CHUNK)
    spread = jnp.repeat(grouped.transpose(0, 2, 1), CHUNK, axis=2)
    index = jnp.arange(CHUNK)[:, None]
    same = spread == seg[:, None, :]
    from_j = same & (local[None, :] >= index)[None]
    to_i = same & (local[None, :] <= index)[None]
    ends = jnp.concatenate([jnp.full((count, 1), -5, seg.dtype), grouped[:, :-1, -1]], axis=1)
    before = (ends[:, :, None] == seg[:, None, :]) & (
        place[None, :] < (jnp.arange(chunks) * CHUNK)[:, None]
    )[None]
    after = jnp.repeat(ends, CHUNK, axis=1) == seg
    first = seg == seg[:, :1]
    last = seg == seg[:, -1:]
    bias = jnp.concatenate(
        [from_j, to_i, before, after[:, None], first[:, None], last[:, None]], axis=1
    )
    bias = jnp.where(bias, 0.0, NEG).astype(f32)
    previous = jnp.concatenate([prev_doc[:, None], seg[:, :-1]], axis=1)
    keeps = (previous == seg).astype(f32)[:, None]
    pad = jnp.zeros((count, 4, tokens), f32)
    return jnp.concatenate([bias, keeps, pad], axis=1)


def state_kernel(k_ref, v_ref, ld_ref, one_ref, aux_ref, lev_ref, ks_ref, vs_ref):
    tokens = ld_ref.shape[1]
    base, _ = aux_rows(tokens)
    earlier = lax.broadcasted_iota(jnp.int32, (tokens, tokens), 0)
    later = lax.broadcasted_iota(jnp.int32, (tokens, tokens), 1)
    upper = jnp.where(earlier <= later, 1.0, 0.0).astype(bf16)
    ld = ld_ref[...]
    high, rest = ld.astype(bf16), None
    rest = ld - high.astype(f32)
    mid, low = split2(rest)
    levels = dg(high, upper, 1, 0) + (dg(mid, upper, 1, 0) + dg(low, upper, 1, 0))
    lev_ref[...] = levels
    tail = jnp.exp(levels[:, tokens - 1 : tokens] - levels + aux_ref[0, base + 2 : base + 3, :])
    tail = split2(tail * one_ref[...])
    ks_ref[0] = dot2(tail, k_ref[...], 1, 0)
    vs_ref[0] = dot2(tail, v_ref[...], 1, 0)


def forward_kernel(
    q_ref, k_ref, v_ref, lev_ref, one_ref, aux_ref, ki_ref, vi_ref, gain_ref,
    no_ref, mix_ref, p_ref, sc_ref, mt_ref, w_scr, d_scr, wh_scr, wl_scr,
):
    tokens = lev_ref.shape[1]
    chunks = tokens // CHUNK
    base, _ = aux_rows(tokens)
    levels, one = lev_ref[...], one_ref[...]
    q, k, v = q_ref[...], k_ref[...], v_ref[...]
    chunk = chunk_of(SLOTS, tokens)
    kq = dg(k, q, 1, 1)
    d_scr[...] = pick_rows(kq, CHUNK, chunks)

    def inside(j, scores):
        gap = levels - group_lane(levels, j) + aux_ref[0, pl.ds(j, 1), :]
        w = jnp.exp(gap) * group_lane(one, j)
        w_scr[j] = w
        return scores + w * d_scr[pl.ds(j, 1), :]

    scores = lax.fori_loop(0, CHUNK, inside, jnp.zeros_like(levels), unroll=2)
    decay = jnp.exp(levels - level_refs(levels) + aux_ref[0, base : base + 1, :])
    for c in range(1, chunks):
        w = levels[:, c * CHUNK - 1 : c * CHUNK] - levels + aux_ref[0, 2 * CHUNK + c : 2 * CHUNK + c + 1, :]
        wh, wl = split2(jnp.exp(w) * one)
        wh_scr[(c - 1) * SLOTS : c * SLOTS] = wh
        wl_scr[(c - 1) * SLOTS : c * SLOTS] = wl
    wst = (wh_scr[...], wl_scr[...])
    scores += decay * pick_rows(dot3(wst, split2(kq), 1, 0), SLOTS, chunks, 1)
    carried = jnp.exp(levels + aux_ref[0, base + 1 : base + 2, :])
    scores += carried * dot2(split2(ki_ref[0]), q, 1, 1)
    sc_ref[...] = scores
    z = scores * SCALE
    e = jnp.exp(z - jnp.max(z, axis=0, keepdims=True))
    probs = e / jnp.sum(e, axis=0, keepdims=True)
    p_ref[...] = probs

    def mixing(j, carry):
        d_scr[pl.ds(j, 1), :] = jnp.sum(w_scr[j] * probs, axis=0, keepdims=True)
        return carry

    lax.fori_loop(0, CHUNK, mixing, 0, unroll=2)
    row = lax.broadcasted_iota(jnp.int32, (tokens, tokens), 0) // CHUNK
    col = lax.broadcasted_iota(jnp.int32, (tokens, tokens), 1) // CHUNK
    mixed_t = jnp.where(row == col, jnp.concatenate([d_scr[...]] * chunks, axis=0), 0.0)
    mixed_t += dot3(wst, split2(stack_chunks(probs * decay, chunks)), 0, 0)
    mt_ref[0] = mixed_t
    out = dot2(split2(mixed_t), v, 0, 0) + dot3(split2(probs * carried), split2(vi_ref[0]), 0, 0)
    mix_ref[...] = out
    unit = out * lax.rsqrt(jnp.mean(out * out, axis=1, keepdims=True) + epsilon)
    no_ref[...] = (unit * gain_ref[...]).astype(bf16)


def backward_kernel(
    q_ref, k_ref, v_ref, lev_ref, one_ref, aux_ref, ki_ref, vi_ref, gain_ref, mix_ref, p_ref, sc_ref, mt_ref, go_ref,
    gq_ref, gk_ref, gv_ref, r_ref, a_ref, dk_ref, dv_ref, hg_ref, w_scr, d_scr, e_scr, x_scr, wh_scr, wl_scr,
):
    tokens = lev_ref.shape[1]
    chunks = tokens // CHUNK
    base, _ = aux_rows(tokens)
    levels, one, probs = lev_ref[...], one_ref[...], p_ref[...]
    q, k, v = q_ref[...], k_ref[...], v_ref[...]
    out, go = mix_ref[...], go_ref[...]
    factor = lax.rsqrt(jnp.mean(out * out, axis=1, keepdims=True) + epsilon)
    unit = out * factor
    hg_ref[0] = jnp.sum(go * unit, axis=0, keepdims=True)
    go = go * gain_ref[...]
    grad = factor * (go - unit * jnp.mean(go * unit, axis=1, keepdims=True))
    g = split2(grad)
    kin, vin = split2(ki_ref[0]), split2(vi_ref[0])
    gv = dot2r(v, g, 1, 1)
    d_scr[...] = pick_rows(gv, CHUNK, chunks)

    def inside(j, dp):
        gap = levels - group_lane(levels, j) + aux_ref[0, pl.ds(j, 1), :]
        w = jnp.exp(gap) * group_lane(one, j)
        w_scr[j] = w
        return dp + w * d_scr[pl.ds(j, 1), :]

    dp = lax.fori_loop(0, CHUNK, inside, jnp.zeros_like(levels), unroll=2)
    decay = jnp.exp(levels - level_refs(levels) + aux_ref[0, base : base + 1, :])
    for c in range(1, chunks):
        w = levels[:, c * CHUNK - 1 : c * CHUNK] - levels + aux_ref[0, 2 * CHUNK + c : 2 * CHUNK + c + 1, :]
        w = jnp.exp(w)
        x_scr[(c - 1) * SLOTS : c * SLOTS] = w
        wh, wl = split2(w * one)
        wh_scr[(c - 1) * SLOTS : c * SLOTS] = wh
        wl_scr[(c - 1) * SLOTS : c * SLOTS] = wl
    wst = (wh_scr[...], wl_scr[...])
    dp += decay * pick_rows(dot3(wst, split2(gv), 1, 0), SLOTS, chunks, 1)
    carried = jnp.exp(levels + aux_ref[0, base + 1 : base + 2, :])
    dp += carried * dot3(vin, g, 1, 1)
    dz = SCALE * probs * (dp - jnp.sum(probs * dp, axis=0, keepdims=True))
    a_ref[...] = dz * sc_ref[...] + probs * dp

    def mixing(j, carry):
        d_scr[pl.ds(j, 1), :] = jnp.sum(w_scr[j] * dz, axis=0, keepdims=True)
        return carry

    lax.fori_loop(0, CHUNK, mixing, 0, unroll=2)
    row = lax.broadcasted_iota(jnp.int32, (tokens, tokens), 0) // CHUNK
    col = lax.broadcasted_iota(jnp.int32, (tokens, tokens), 1) // CHUNK
    mz_t = jnp.where(row == col, jnp.concatenate([d_scr[...]] * chunks, axis=0), 0.0)
    zst = split2(stack_chunks(dz * decay, chunks))
    pst = split2(stack_chunks(probs * decay, chunks))
    mz_t += dot3(wst, zst, 0, 0)
    mz = split2(mz_t)
    zc, pc = split2(dz * carried), split2(probs * carried)
    gq_ref[...] = (dot2(mz, k, 0, 0) + dot3(zc, kin, 0, 0)).astype(bf16)
    gk_ref[...] = dot2(mz, q, 1, 0)
    gv_ref[...] = dot3(split2(mt_ref[0]), g, 1, 0)
    dk_ref[0] = dot2(zc, q, 1, 0)
    dv_ref[0] = dot3(pc, g, 1, 0)
    qk = dg(q, k, 1, 1)
    gv_n = dot2(g, v, 1, 1)
    d_scr[...] = pick_rows(qk, CHUNK, chunks)
    e_scr[...] = pick_rows(gv_n, CHUNK, chunks)

    def onward(i, total):
        gap = group_lane(levels, i) - levels + aux_ref[0, pl.ds(CHUNK + i, 1), :]
        term = group_lane(dz, i) * d_scr[pl.ds(i, 1), :] + group_lane(probs, i) * e_scr[pl.ds(i, 1), :]
        return total + jnp.exp(gap) * term

    total = lax.fori_loop(0, CHUNK, onward, jnp.zeros_like(levels), unroll=2)
    cross = dot3(zst, split2(qk), 1, 0) + dot3(pst, split2(gv_n), 1, 0)
    for c in range(1, chunks):
        total += x_scr[(c - 1) * SLOTS : c * SLOTS] * cross[(c - 1) * SLOTS : c * SLOTS]
    r_ref[...] = total


def finish_kernel(
    k_ref, v_ref, lev_ref, one_ref, sig_ref, aux_ref, sums_ref, ki_ref, vi_ref, ks_ref, vs_ref, gk_ref, gv_ref,
    r_ref, a_ref, dk_ref, dv_ref, gko_ref, gvo_ref, gl_ref,
):
    tokens = lev_ref.shape[1]
    base, _ = aux_rows(tokens)
    levels, one = lev_ref[...], one_ref[...]
    k, v = k_ref[...], v_ref[...]
    tail = jnp.exp(levels[:, tokens - 1 : tokens] - levels + aux_ref[0, base + 2 : base + 3, :])
    end = jnp.exp(levels[:, tokens - 1 : tokens] + aux_ref[0, base + 1 : base + 2, tokens - 1 : tokens])
    dk, dv = dk_ref[0], dv_ref[0]
    dks, dvs = split2(dk), split2(dv)
    weights = split2(tail * one)
    gko_ref[...] = (gk_ref[...] + dot3(weights, dks, 0, 0)).astype(bf16)
    gvo_ref[...] = (gv_ref[...] + dot3(weights, dvs, 0, 0)).astype(bf16)
    rows = r_ref[...] + tail * (dot2(dks, k, 1, 1) + dot2(dvs, v, 1, 1))
    final_k = end * ki_ref[0] + ks_ref[0]
    final_v = end * vi_ref[0] + vs_ref[0]
    at_end = jnp.sum(dk * final_k + dv * final_v, axis=1, keepdims=True)
    x = a_ref[...] - one * rows
    high = x.astype(bf16)
    mid, low = split2(x - high.astype(f32))
    sums = sums_ref[0]
    flow = dg(high, sums, 1, 0) + (dg(mid, sums, 1, 0) + dg(low, sums, 1, 0))
    flow += jnp.where(aux_ref[0, base + 2 : base + 3, :] == 0.0, at_end, 0.0)
    grad = flow * aux_ref[0, base + 3 : base + 4, :] - (1.0 - one) * rows
    gl_ref[...] = (grad * sig_ref[...]).astype(bf16)


def seq_specs(tokens):
    def tok(col, width=HEAD_DIM):
        return pl.BlockSpec((tokens, width), lambda i: (i, col))

    lane = pl.BlockSpec((SLOTS, tokens), lambda i: (0, i))
    _, rows = aux_rows(tokens)
    aux = pl.BlockSpec((1, rows, tokens), lambda i: (i, 0, 0))
    state = pl.BlockSpec((1, SLOTS, HEAD_DIM), lambda i: (i, 0, 0))
    gain = pl.BlockSpec((1, HEAD_DIM), lambda i: (0, 0))
    square = pl.BlockSpec((1, tokens, tokens), lambda i: (i, 0, 0))
    row = pl.BlockSpec((1, 1, HEAD_DIM), lambda i: (i, 0, 0))
    return tok, lane, aux, state, gain, square, row


def params(mib):
    return pltpu.CompilerParams(vmem_limit_bytes=mib << 20)


def cost(count, flops, size):
    return pl.CostEstimate(flops=count * flops, bytes_accessed=count * size, transcendentals=count * 1000000)


def shape(dims, dtype):
    return jax.ShapeDtypeStruct(dims, dtype)


def run_states(qkv, ld, one, aux):
    count, _, tokens = aux.shape
    tok, lane, auxs, state, _, _, _ = seq_specs(tokens)
    return pl.pallas_call(
        state_kernel,
        grid=(count,),
        in_specs=[tok(1), tok(2), lane, lane, auxs],
        out_specs=[lane, state, state],
        out_shape=[
            shape((SLOTS, count * tokens), f32),
            shape((count, SLOTS, HEAD_DIM), f32),
            shape((count, SLOTS, HEAD_DIM), f32),
        ],
        compiler_params=params(24),
        cost_estimate=cost(count, 100000000, 1500000),
    )(qkv, qkv, ld, one, aux)


def big_scratch(tokens):
    stack = (tokens // CHUNK - 1) * SLOTS
    return stack


def run_forward(qkv, levels, one, aux, key_in, value_in, gain):
    count, _, tokens = aux.shape
    tok, lane, auxs, state, gains, square, _ = seq_specs(tokens)
    stack = big_scratch(tokens)
    return pl.pallas_call(
        forward_kernel,
        grid=(count,),
        in_specs=[tok(0), tok(1), tok(2), lane, lane, auxs, state, state, gains],
        out_specs=[tok(0), tok(0), lane, lane, square],
        out_shape=[
            shape((count * tokens, HEAD_DIM), bf16),
            shape((count * tokens, HEAD_DIM), f32),
            shape((SLOTS, count * tokens), f32),
            shape((SLOTS, count * tokens), f32),
            shape((count, tokens, tokens), f32),
        ],
        scratch_shapes=[
            pltpu.VMEM((CHUNK, SLOTS, tokens), f32),
            pltpu.VMEM((CHUNK, tokens), f32),
            pltpu.VMEM((stack, tokens), bf16),
            pltpu.VMEM((stack, tokens), bf16),
        ],
        compiler_params=params(40),
        cost_estimate=cost(count, 1000000000, 3000000),
    )(qkv, qkv, qkv, levels, one, aux, key_in, value_in, gain)


def run_backward(qkv, levels, one, aux, key_in, value_in, gain, mixed, probs, scores, mixed_t, grad_o):
    count, _, tokens = aux.shape
    tok, lane, auxs, state, gains, square, row = seq_specs(tokens)
    stack = big_scratch(tokens)
    return pl.pallas_call(
        backward_kernel,
        grid=(count,),
        in_specs=[tok(0), tok(1), tok(2), lane, lane, auxs, state, state, gains, tok(0), lane, lane, square, tok(0)],
        out_specs=[tok(0), tok(0), tok(0), lane, lane, state, state, row],
        out_shape=[
            shape((count * tokens, HEAD_DIM), bf16),
            shape((count * tokens, HEAD_DIM), f32),
            shape((count * tokens, HEAD_DIM), f32),
            shape((SLOTS, count * tokens), f32),
            shape((SLOTS, count * tokens), f32),
            shape((count, SLOTS, HEAD_DIM), f32),
            shape((count, SLOTS, HEAD_DIM), f32),
            shape((count, 1, HEAD_DIM), f32),
        ],
        scratch_shapes=[
            pltpu.VMEM((CHUNK, SLOTS, tokens), f32),
            pltpu.VMEM((CHUNK, tokens), f32),
            pltpu.VMEM((CHUNK, tokens), f32),
            pltpu.VMEM((stack, tokens), f32),
            pltpu.VMEM((stack, tokens), bf16),
            pltpu.VMEM((stack, tokens), bf16),
        ],
        compiler_params=params(48),
        cost_estimate=cost(count, 3000000000, 5000000),
    )(qkv, qkv, qkv, levels, one, aux, key_in, value_in, gain, mixed, probs, scores, mixed_t, grad_o)


def run_finish(qkv, levels, one, sig, aux, sums, key_in, value_in, key_own, value_own, gk, gv, rows, acts, dk, dv):
    count, _, tokens = aux.shape
    tok, lane, auxs, state, _, square, _ = seq_specs(tokens)
    return pl.pallas_call(
        finish_kernel,
        grid=(count,),
        in_specs=[tok(1), tok(2), lane, lane, lane, auxs, square, state, state, state, state]
        + [tok(0), tok(0), lane, lane, state, state],
        out_specs=[tok(0), tok(0), lane],
        out_shape=[
            shape((count * tokens, HEAD_DIM), bf16),
            shape((count * tokens, HEAD_DIM), bf16),
            shape((SLOTS, count * tokens), bf16),
        ],
        compiler_params=params(40),
        cost_estimate=cost(count, 300000000, 4000000),
    )(qkv, qkv, levels, one, sig, aux, sums, key_in, value_in, key_own, value_own, gk, gv, rows, acts, dk, dv)


def matmul(a, b, ca=1, cb=0):
    return lax.dot_general(a, b, (((ca,), (cb,)), ((), ())), preferred_element_type=f32)


def rms_parts(array, gain_vec):
    factor = lax.rsqrt(jnp.mean(array * array, axis=-1, keepdims=True) + epsilon)
    unit_val = array * factor
    return unit_val, factor, unit_val * gain_vec


def norm_back(unit_val, factor, grad_unit):
    return factor * (grad_unit - unit_val * jnp.mean(grad_unit * unit_val, axis=-1, keepdims=True))


def per_device(
    layer_input, segments, cotangent, norm1_gain, norm2_gain, head_gain, decay_bias,
    w_query, w_key, w_value, w_decay, w_out, w_gate, w_up, w_down,
):
    count, tokens, width = layer_input.shape
    rows = count * tokens
    hidden_units = w_gate.shape[1]
    heads = w_query.shape[1]
    tp_place, here = lax.axis_index("tp"), lax.axis_index("ctx")
    places = lax.axis_size("ctx")
    shard = rows // lax.axis_size("tp")

    def mine(array):
        return lax.dynamic_slice_in_dim(array, tp_place * shard, shard, 0)

    def gather_rows(array):
        return lax.all_gather(array, ("dp", "ctx"), axis=0, tiled=True)

    def scatter_rows(array):
        return lax.psum_scatter(array, ("dp", "ctx"), scatter_dimension=0, tiled=True).astype(f32)

    def to_shards(array):
        return lax.psum_scatter(array.astype(bf16), "tp", scatter_dimension=0, tiled=True).astype(f32)

    def from_shards(array):
        return lax.all_gather(array.astype(bf16), "tp", axis=0, tiled=True)

    w_in = gather_rows(jnp.concatenate([w_query, w_key, w_value, w_decay], axis=1))
    w_rest = gather_rows(jnp.concatenate([w_out.T, w_gate, w_up, w_down.T], axis=1))
    w_qkv, w_dec = w_in[:, : 3 * heads], w_in[:, 3 * heads :]
    w_o = w_rest[:, :heads]
    w_gu = w_rest[:, heads : heads + 2 * hidden_units]
    w_d = w_rest[:, heads + 2 * hidden_units :]

    edges = lax.all_gather(jnp.stack([segments[:, 0], segments[:, -1]]), "ctx")
    prev_doc = jnp.where(here > 0, edges[jnp.maximum(here - 1, 0), 1], -1)
    aux = make_aux(segments, prev_doc)
    place = jnp.arange(tokens)
    sums = (
        (place[:, None] >= place[None, :])[None] & (segments[:, :, None] == segments[:, None, :])
    ).astype(bf16)
    index = jnp.arange(places)
    reach_in = (index[:, None] < here) & (edges[:, 1] == segments[:, 0])
    reach_out = (index[:, None] > here) & (edges[:, 0] == segments[:, -1])
    between = (index[None, :] > jnp.minimum(index[:, None], here)) & (
        index[None, :] < jnp.maximum(index[:, None], here)
    )

    def exchange(keys, values, coefs):
        every = lax.all_gather(jnp.concatenate([keys, values], axis=2), "ctx")
        total = jnp.sum(every * coefs[..., None], axis=0)
        return total[..., :HEAD_DIM], total[..., HEAD_DIM:]

    x = layer_input.reshape(rows, width)
    unit_one, factor_one, scaled_one = rms_parts(x.astype(f32), norm1_gain)
    normed1 = scaled_one.astype(bf16)
    qkv = matmul(normed1, w_qkv).astype(bf16)
    bias_here = lax.dynamic_slice_in_dim(decay_bias, tp_place * SLOTS, SLOTS)
    logits = matmul(w_dec, normed1, 0, 1) + bias_here[:, None]
    log_decay = jax.nn.log_sigmoid(logits) / gate_norm
    one = -jnp.expm1(log_decay)
    sig = jax.nn.sigmoid(-logits) / gate_norm
    levels, key_own, value_own = run_states(qkv, log_decay, one, aux)
    ends = lax.all_gather(levels[:, tokens - 1 :: tokens].T, "ctx")
    span = jnp.exp(jnp.sum(jnp.where(between[:, :, None, None], ends[None], 0.0), axis=1))
    coef_in = jnp.where(reach_in[..., None], span, 0.0)
    coef_out = jnp.where(reach_out[..., None], span, 0.0)
    key_in, value_in = exchange(key_own, value_own, coef_in)
    gain = head_gain[None, :]
    normed_o, mixed, probs, scores, mixed_t = run_forward(
        qkv, levels, one, aux, key_in, value_in, gain
    )
    hidden = mine(x).astype(f32) + to_shards(matmul(normed_o, w_o, 1, 1))
    unit_two, factor_two, scaled_two = rms_parts(hidden, norm2_gain)
    normed2 = from_shards(scaled_two)
    pre = matmul(normed2, w_gu)
    gate_pre, up_pre = pre[:, :hidden_units], pre[:, hidden_units:]
    gate_sig = jax.nn.sigmoid(gate_pre)
    gate_silu = gate_pre * gate_sig
    hidden_act = (gate_silu * up_pre).astype(bf16)
    feed = to_shards(matmul(hidden_act, w_d, 1, 1))
    output = from_shards(hidden + feed)

    grad_feed = cotangent.reshape(rows, width)
    grad_act = matmul(grad_feed, w_d)
    grad_gate = (grad_act * up_pre * gate_sig * (1.0 + gate_pre * (1.0 - gate_sig))).astype(bf16)
    grad_up = (grad_act * gate_silu).astype(bf16)
    grad_gu = jnp.concatenate([grad_gate, grad_up], axis=1)
    grad_n2 = to_shards(matmul(grad_gu, w_gu, 1, 1))
    grad_wgu = matmul(normed2, grad_gu, 0, 0).astype(bf16)
    grad_wd = matmul(grad_feed, hidden_act, 0, 0).astype(bf16)
    ffn_rows = scatter_rows(jnp.concatenate([grad_wgu, grad_wd], axis=1))
    gain_two_part = jnp.sum(grad_n2 * unit_two, axis=0)
    grad_hidden = mine(grad_feed).astype(f32) + norm_back(unit_two, factor_two, grad_n2 * norm2_gain)
    grad_attn = from_shards(grad_hidden)
    grad_o = matmul(grad_attn, w_o)
    grad_wo = matmul(grad_attn, normed_o, 0, 0).astype(bf16)
    grad_q, gk, gv, row_sums, acts, dk, dv, head_part = run_backward(
        qkv, levels, one, aux, key_in, value_in, gain, mixed, probs, scores, mixed_t, grad_o
    )
    dk_later, dv_later = exchange(dk, dv, coef_out)
    grad_k, grad_v, grad_logits = run_finish(
        qkv, levels, one, sig, aux, sums, key_in, value_in, key_own, value_own,
        gk, gv, row_sums, acts, dk_later, dv_later,
    )
    grad_all = jnp.concatenate([grad_q, grad_k, grad_v, grad_logits.T], axis=1)
    grad_n1 = to_shards(matmul(grad_all, w_in, 1, 1))
    grad_in = matmul(normed1, grad_all, 0, 0).astype(bf16)
    att_rows = scatter_rows(jnp.concatenate([grad_in, grad_wo], axis=1))
    unit_mine, factor_mine = mine(unit_one), mine(factor_one)
    gain_one_part = jnp.sum(grad_n1 * unit_mine, axis=0)
    input_grad = grad_hidden + norm_back(unit_mine, factor_mine, grad_n1 * norm1_gain)
    input_grad = from_shards(input_grad).astype(f32)
    bias_part = lax.dynamic_update_slice_in_dim(
        jnp.zeros_like(decay_bias),
        jnp.sum(grad_logits.astype(f32), axis=1),
        tp_place * SLOTS,
        0,
    )
    small = lax.psum(
        jnp.concatenate([gain_one_part, gain_two_part, jnp.sum(head_part, axis=(0, 1)), bias_part]),
        ("dp", "ctx", "tp"),
    )
    cut = 3 * heads
    return (
        output.reshape(count, tokens, width),
        input_grad.reshape(count, tokens, width),
        small[:width],
        small[width : 2 * width],
        small[2 * width : 2 * width + HEAD_DIM],
        small[2 * width + HEAD_DIM :],
        att_rows[:, :heads],
        att_rows[:, heads : 2 * heads],
        att_rows[:, 2 * heads : cut],
        att_rows[:, cut : cut + SLOTS],
        att_rows[:, cut + SLOTS :].T,
        ffn_rows[:, :hidden_units],
        ffn_rows[:, hidden_units : 2 * hidden_units],
        ffn_rows[:, 2 * hidden_units :].T,
    )


def solution(mesh):
    return jax.shard_map(
        per_device,
        mesh=mesh,
        in_specs=(
            P("dp", "ctx", None),
            P("dp", "ctx"),
            P("dp", "ctx", None),
            P(),
            P(),
            P(),
            P(),
            P(("dp", "ctx"), "tp"),
            P(("dp", "ctx"), "tp"),
            P(("dp", "ctx"), "tp"),
            P(("dp", "ctx"), "tp"),
            P("tp", ("dp", "ctx")),
            P(("dp", "ctx"), "tp"),
            P(("dp", "ctx"), "tp"),
            P("tp", ("dp", "ctx")),
        ),
        out_specs=(
            P("dp", "ctx", None),
            P("dp", "ctx", None),
            P(),
            P(),
            P(),
            P(),
            P(("dp", "ctx"), "tp"),
            P(("dp", "ctx"), "tp"),
            P(("dp", "ctx"), "tp"),
            P(("dp", "ctx"), "tp"),
            P("tp", ("dp", "ctx")),
            P(("dp", "ctx"), "tp"),
            P(("dp", "ctx"), "tp"),
            P("tp", ("dp", "ctx")),
        ),
        check_vma=False,
    )
```

time: 2180 us -> 1110 us (0.51)
  waiting for transfers between devices: 1100 us -> 752 us
  matrix products: 458 us -> 111 us
  blocking collectives: 250 us -> 58.3 us
  other arithmetic: 199 us -> 62.2 us
  local copies, waits for them, and re-layouts: 111 us -> 47.3 us
  Pallas kernels: 0 us -> 53.6 us
  loops' own time: 32.1 us -> 0 us
    psum x4 -> x0, waiting for transfers between devices: 518 us -> none  [the longest x1 222 us: per_device(): lax.psum(jnp.dot(normed_o, gathered[6], preferred_element_type=jnp.float3...]
    dot_general x138 -> x13, matrix products: 458 us -> 111 us  [matmul(): lax.dot_general(a, b, (((ca,), (cb,)), ((), ())), preferred_element_type=...]
    all_gather x7 -> x8, waiting for transfers between devices: 103 us -> 425 us  [the longest x4 248 us: from_shards(): return lax.all_gather(array.astype(bf16), 'tp', axis=0, tiled=True)]
    all_gather x19 -> x2, blocking collectives: 200 us -> 17.6 us  [the longest x1 9.52 us: per_device(): edges = lax.all_gather(jnp.stack([segments[:, 0], segments[:, -1]]), 'ctx')]
    reduce_scatter x8 -> x6, waiting for transfers between devices: 471 us -> 327 us  [the longest x4 198 us: to_shards(): lax.psum_scatter(array.astype(bf16), 'tp', scatter_dimension=0, tiled=True)]
    reduce_sum x26 -> x7, other arithmetic: 65.5 us -> 9.81 us  [the longest x2 4.66 us: exchange(): total = jnp.sum(every * coefs[..., None], axis=0)]
    pallas_call x0 -> x4, Pallas kernels: none -> 53.6 us  [the longest x1 31.6 us: run_backward(): pl.pallas_call(backward_kernel, grid=(count,), in_specs=[tok(0), tok(1),...]
    select_n x24 -> x4, other arithmetic: 35 us -> 0.71 us  [the longest x1 0.67 us: per_device(): coef_out = jnp.where(reach_out[..., None], span, 0.0)]
  transfers between devices with their start and end apart: 19 -> 14, of which waited for: 13 -> 14; matrix products, arithmetic and copies ran while one was open for 32% -> 9% of each run, Pallas kernels for 0% -> 1%
where the time goes in v1:
time: 1110 us; the launch traced here: 1100 us
  waiting for transfers between devices  752 us (68%)
  matrix products  111 us (10%)
  other arithmetic  62.2 us (6%)
  blocking collectives  58.3 us (5%)
  Pallas kernels  53.6 us (5%)
  local copies, waits for them, and re-layouts  47.3 us (4%)
  between operations  15.2 us (1%)
    all_gather x4, waiting for transfers between devices, from_shards(): return lax.all_gather(array.astype(bf16), 'tp', axis=0, tiled=True)  248 us
    reduce_scatter x4, waiting for transfers between devices, to_shards(): lax.psum_scatter(array.astype(bf16), 'tp', scatter_dimension=0, tiled=True)  198 us
    reduce_scatter x2, waiting for transfers between devices, scatter_rows(): lax.psum_scatter(array, ('dp', 'ctx'), scatter_dimension=0, tiled=True)  129 us
    dot_general x13, matrix products, matmul(): lax.dot_general(a, b, (((ca,), (cb,)), ((), ())), preferred_element_type=...  111 us
    all_gather x2, waiting for transfers between devices, gather_rows(): return lax.all_gather(array, ('dp', 'ctx'), axis=0, tiled=True)  108 us
    all_gather x2, waiting for transfers between devices, exchange(): every = lax.all_gather(jnp.concatenate([keys, values], axis=2), 'ctx')  68.8 us
    psum x1, blocking collectives, per_device(): lax.psum(jnp.concatenate([gain_one_part, gain_two_part, jnp.sum(head_part...  40.8 us
    unnamed x149, local copies, waits for them, and re-layouts  34.5 us
  transfers between devices with their start and end apart: 14, of which 14 were waited for; matrix products, arithmetic and copies ran while one was open for 9% of the time, Pallas kernels for 1%

profile of v1, /device:TPU:0, one launch (start us, length us, event | category | flops | bytes accessed | tf_op | source)
XLA Modules:
  0.0 1101.2 jit_solution(905223866463585380)
XLA Ops:
  11.2 9.5 all-gather.4
  21.6 2.8 multiply_reduce_fusion
  26.6 6.5 convert_multiply_fusion
  33.1 27.9 %all-gather.15.cloned.1.call-done = bf16[2048,1600]{1,0:T(8,128)(2,1)} async-done(((bf16[256,1600]{1,0:T(8,128)(2,1)}), bf16[2048,1600]{1,0:T(8,128)(2,1)}) %all-gather.15.cloned.1.call-update) | async-done | bytes 6553616 | tf_op jit(solution)/shard_map/all_gather | solution.py:447
  61.0 8.8 fusion.16.k_ref.v_ref.q_ref
  69.8 3.4 divide_multiply_fusion
  76.8 2.2 copy.86
  79.0 2.2 copy.87
  81.3 3.1 pad_maximum_fusion.6
  85.8 8.0 all-gather.5
  94.6 26.3 %all-gather.27.cloned.1.call-done = f32[12,64,1024]{2,1,0:T(8,128)} async-done(((f32[3,64,1024]{2,1,0:T(8,128)}), f32[12,64,1024]{2,1,0:T(8,128)}) %all-gather.27.cloned.1.call-update) | async-done | bytes 3145744 | tf_op jit(solution)/shard_map/all_gather | solution.py:480
  121.0 2.3 multiply_reduce_fusion.2
  126.3 16.0 %shard_map.255 = (bf16[768,512]{1,0:T(8,128)(2,1)S(1)}, f32[768,512]{1,0:T(8,128)S(1)}, f32[64,768]{1,0:T(8,128)S(1)}, f32[64,768]{1,0:T(8,128)S(1)}, f32[3,256,256]{2,1,0:T(8,128)S(1)}) custom-call(bf16[768,1536]{1,0:T(8,128)(2,1)S(1)} %fusion.16.k_ref.v_ref.q_ref, bf16[768,1536]{1,0:T(8,128)(2,1)S(1)} %fusion.16.k_ref.v_ref.q_ref, ...), custom_call_target="tpu_custom_call" | custom-call | flops 3000000000 | bytes 9000000 | tf_op jit(solution)/shard_map/pallas_call | solution.py:343
  147.3 80.3 %all-gather.17.cloned.1.call-done = bf16[2048,4736]{0,1:T(8,128)(2,1)} async-done(((bf16[256,4736]{0,1:T(8,128)(2,1)}), bf16[2048,4736]{0,1:T(8,128)(2,1)}) %all-gather.17.cloned.1.call-update) | async-done | bytes 19398672 | tf_op jit(solution)/shard_map/all_gather | solution.py:447
  227.6 5.4 convolution_convert_fusion.3
  233.1 60.4 %reduce-scatter.7.cloned.1.call-done = bf16[192,2048]{1,0:T(8,128)(2,1)} async-done(((bf16[768,2048]{1,0:T(8,128)(2,1)}), bf16[192,2048]{1,0:T(8,128)(2,1)}) %reduce-scatter.7.cloned.1.call-update) | async-done | bytes 786448 | tf_op jit(solution)/shard_map/reduce_scatter | solution.py:453
  295.2 2.6 multiply_convert_fusion.2
  298.3 63.2 %all-gather.19.cloned.1.call-done = bf16[768,2048]{1,0:T(8,128)(2,1)} async-done(((bf16[192,2048]{1,0:T(8,128)(2,1)}), bf16[768,2048]{1,0:T(8,128)(2,1)}) %all-gather.19.cloned.1.call-update) | async-done | bytes 3145744 | tf_op jit(solution)/shard_map/all_gather | solution.py:456
  361.4 13.9 %fusion.2 = f32[768,2816]{1,0:T(8,128)S(1)} fusion(bf16[768,2048]{1,0:T(8,128)(2,1)} %all-gather.19.cloned.1.call-done, bf16[2048,4736]{0,1:T(8,128)(2,1)} %all-gather.17.cloned.1.call-done), kind=kOutput, calls=%fused_computation.4 | convolution fusion | flops 8858370048 | bytes 23330816 | tf_op jit(solution)/shard_map/dot_general | solution.py:418
  375.3 10.6 fusion.13
  387.9 13.4 %fusion.22 = bf16[768,2048]{1,0:T(8,128)(2,1)} fusion(bf16[2048,4736]{0,1:T(8,128)(2,1)} %all-gather.17.cloned.1.call-done, bf16[768,1408]{1,0:T(8,128)(2,1)S(1)} %get-tuple-element.117, bf16[768,1408]{1,0:T(8,128)(2,1)S(1)} %get-tuple-element.116), kind=kOutput, calls=%fused_computation.33 | convolution fusion | flops 8868593664 | bytes 19005440 | tf_op jit(solution)/shard_map/dot_general | solution.py:418
  401.4 59.0 %reduce-scatter.11.cloned.1.call-done = bf16[192,2048]{1,0:T(8,128)(2,1)} async-done(((bf16[768,2048]{1,0:T(8,128)(2,1)}), bf16[192,2048]{1,0:T(8,128)(2,1)}) %reduce-scatter.11.cloned.1.call-update) | async-done | bytes 786448 | tf_op jit(solution)/shard_map/reduce_scatter | solution.py:453
  460.4 2.8 fusion.39
  463.2 3.2 fusion.53
  466.6 63.6 %all-gather.23.cloned.1.call-done = bf16[768,2048]{1,0:T(8,128)(2,1)} async-done(((bf16[192,2048]{1,0:T(8,128)(2,1)}), bf16[768,2048]{1,0:T(8,128)(2,1)}) %all-gather.23.cloned.1.call-update) | async-done | bytes 3145744 | tf_op jit(solution)/shard_map/all_gather | solution.py:456
  530.1 5.5 fusion.29.go_ref
  535.7 31.6 %shard_map.256 = (bf16[768,512]{1,0:T(8,128)(2,1)S(1)}, f32[768,512]{1,0:T(8,128)S(1)}, f32[768,512]{1,0:T(8,128)}, f32[64,768]{1,0:T(8,128)S(1)}, f32[64,768]{1...) custom-call(bf16[768,1536]{1,0:T(8,128)(2,1)} %copy-done, ...), custom_call_target="tpu_custom_call" | custom-call | flops 8999999488 | bytes 15000000 | tf_op jit(solution)/shard_map/pallas_call | solution.py:370
  571.9 42.5 %all-gather.29.cloned.1.call-done = f32[12,64,1024]{2,1,0:T(8,128)} async-done(((f32[3,64,1024]{2,1,0:T(8,128)}), f32[12,64,1024]{2,1,0:T(8,128)}) %all-gather.29.cloned.1.call-update) | async-done | bytes 3145744 | tf_op jit(solution)/shard_map/all_gather | solution.py:480
  614.5 2.4 multiply_reduce_fusion.1
  618.7 4.2 shard_map.257
  626.3 9.9 convolution_convert_fusion.4
  637.9 9.2 fusion.19
  647.1 9.0 fusion.4
  656.2 12.2 %convolution_convert_fusion = bf16[2048,2816]{1,0:T(8,128)(2,1)S(1)} fusion(bf16[768,2048]{1,0:T(8,128)(2,1)S(1)} %copy-done.64, bf16[768,1408]{1,0:T(8,128)(2,1)} %copy-done.68, bf16[768,1408]{1,0:T(8,128)(2,1)} %copy-done.67), kind=kOutput, calls=%fused_computation.1 | convolution fusion | flops 8872787968 | bytes 19005440 | tf_op jit(solution)/shard_map/dot_general | solution.py:418
  668.4 9.7 pad_maximum_fusion
  678.9 17.9 %reduce-scatter.13.cloned.1.call-done = bf16[192,2048]{1,0:T(8,128)(2,1)} async-done(((bf16[768,2048]{1,0:T(8,128)(2,1)}), bf16[192,2048]{1,0:T(8,128)(2,1)}) %reduce-scatter.13.cloned.1.call-update) | async-done | bytes 786448 | tf_op jit(solution)/shard_map/reduce_scatter | solution.py:453
  698.9 60.3 %reduce-scatter.9.cloned.1.call-done = bf16[192,2048]{1,0:T(8,128)(2,1)} async-done(((bf16[768,2048]{1,0:T(8,128)(2,1)}), bf16[192,2048]{1,0:T(8,128)(2,1)}) %reduce-scatter.9.cloned.1.call-update) | async-done | bytes 786448 | tf_op jit(solution)/shard_map/reduce_scatter | solution.py:453
  759.2 4.5 fusion.35
  764.5 3.9 convolution_convert_fusion.5
  768.4 5.6 convolution_convert_fusion.1
  774.1 4.7 pad_maximum_fusion.1
  780.1 40.8 %psum.7 = f32[4864]{0:T(1024)S(1)} all-reduce(f32[4864]{0:T(1024)S(1)} %pad_maximum_fusion.12), channel_id=1, replica_groups=mesh['dp'=2,'ctx'=4,'tp'=4] {'dp','ctx','tp'}, use_global_device_ids=true, to_apply=%region_15.16 | all-reduce | flops 4864 | bytes 38912 | tf_op jit(solution)/shard_map/psum | solution.py:550
  822.6 59.5 %reduce-scatter.17.cloned.1.call-done = bf16[256,4224]{1,0:T(8,128)(2,1)} async-done(((bf16[2048,4224]{1,0:T(8,128)(2,1)}), bf16[256,4224]{1,0:T(8,128)(2,1)}) %reduce-scatter.17.cloned.1.call-update) | async-done | bytes 2162704 | tf_op jit(solution)/shard_map/reduce_scatter | solution.py:450
  885.3 2.9 copy.94
  889.9 57.2 %all-gather.21.cloned.1.call-done = bf16[768,2048]{1,0:T(8,128)(2,1)} async-done(((bf16[192,2048]{1,0:T(8,128)(2,1)}), bf16[768,2048]{1,0:T(8,128)(2,1)}) %all-gather.21.cloned.1.call-update) | async-done | bytes 3145744 | tf_op jit(solution)/shard_map/all_gather | solution.py:456
  947.2 63.8 %all-gather.25.cloned.1.call-done = bf16[768,2048]{1,0:T(8,128)(2,1)} async-done(((bf16[192,2048]{1,0:T(8,128)(2,1)}), bf16[768,2048]{1,0:T(8,128)(2,1)}) %all-gather.25.cloned.1.call-update) | async-done | bytes 3145744 | tf_op jit(solution)/shard_map/all_gather | solution.py:456
  1011.0 5.4 convert.2
  1016.5 69.7 %reduce-scatter.15.cloned.1.call-done = bf16[256,2112]{0,1:T(8,128)(2,1)} async-done(((bf16[2048,2112]{0,1:T(8,128)(2,1)}), bf16[256,2112]{0,1:T(8,128)(2,1)}) %reduce-scatter.15.cloned.1.call-update) | async-done | bytes 1081360 | tf_op jit(solution)/shard_map/reduce_scatter | solution.py:450
  (246 shorter events, 56.2 us)
Async XLA Ops:
  7.2 18.2 %copy-start.54 = (s32[3,256]{1,0:T(4,128)S(1)}, s32[3,256]{1,0:T(4,128)}, u32[]{:S(2)}) copy-start(s32[3,256]{1,0:T(4,128)} %param.16) | copy-start | bytes 9220
  7.2 53.8 %all-gather.15.cloned.1.call-start = ((), (), s32[]{:S(2)}) async-start(), calls=%async_computation.6 | async-start | bytes 7667712 | tf_op jit(solution)/shard_map/all_gather | solution.py:447
  8.1 17.8 %copy-start.65 = (f32[256]{0:T(256)S(1)}, f32[256]{0:T(256)}, u32[]{:S(2)}) copy-start(f32[256]{0:T(256)} %param.21) | copy-start | bytes 3076
  10.2 16.4 %copy-start.58 = (f32[2048]{0:T(1024)S(1)}, f32[2048]{0:T(1024)}, u32[]{:S(2)}) copy-start(f32[2048]{0:T(1024)} %param.18) | copy-start | bytes 24580
  10.2 110.7 %all-gather.27.cloned.1.call-start = ((), (), s32[]{:S(2)}) async-start(), calls=%async_computation.18 | async-start | bytes 3932160 | tf_op jit(solution)/shard_map/all_gather | solution.py:480
  26.6 46.6 %copy-start.10 = (f32[3,80,256]{2,1,0:T(8,128)}, f32[3,80,256]{2,1,0:T(8,128)S(1)}, u32[]{:S(2)}) copy-start(f32[3,80,256]{2,1,0:T(8,128)S(1)} %maximum_maximum_fusion.aux_ref) | copy-start | bytes 737284
  61.0 8.8 copy-start.51
  69.8 53.5 %copy-start = (bf16[768,1536]{1,0:T(8,128)(2,1)}, bf16[768,1536]{1,0:T(8,128)(2,1)S(1)}, u32[]{:S(2)}) copy-start(bf16[768,1536]{1,0:T(8,128)(2,1)S(1)} %fusion.16.k_ref.v_ref.q_ref) | copy-start | bytes 7077892
  75.8 5.5 copy-start.55
  76.8 150.8 %all-gather.17.cloned.1.call-start = ((), (), s32[]{:S(2)}) async-start(), calls=%async_computation.7 | async-start | bytes 21823488 | tf_op jit(solution)/shard_map/all_gather | solution.py:447
  84.4 38.9 %copy-start.33 = (f32[512]{0:T(512)S(1)}, f32[512]{0:T(512)}, u32[]{:S(2)}) copy-start(f32[512]{0:T(512)} %param.20) | copy-start | bytes 6148
  84.5 209.0 %reduce-scatter.7.cloned.1.call-start = ((), (), s32[]{:S(2)}) async-start(), calls=%async_computation.8 | async-start | bytes 3932160 | tf_op jit(solution)/shard_map/reduce_scatter | solution.py:453
  123.3 412.3 %copy-start.2 = (f32[3,64,512]{2,1,0:T(8,128)}, f32[3,64,512]{2,1,0:T(8,128)S(1)}, u32[]{:S(2)}) copy-start(f32[3,64,512]{2,1,0:T(8,128)S(1)} %get-tuple-element.130.vi_ref) | copy-start | bytes 1179652
  233.0 62.2 %copy-start.56 = (f32[2048]{0:T(1024)S(1)}, f32[2048]{0:T(1024)}, u32[]{:S(2)}) copy-start(f32[2048]{0:T(1024)} %param.19) | copy-start | bytes 24580
  233.0 128.4 %all-gather.19.cloned.1.call-start = ((), (), s32[]{:S(2)}) async-start(), calls=%async_computation.9 | async-start | bytes 3932160 | tf_op jit(solution)/shard_map/all_gather | solution.py:456
  297.7 162.6 %reduce-scatter.11.cloned.1.call-start = ((), (), s32[]{:S(2)}) async-start(), calls=%async_computation.12 | async-start | bytes 3932160 | tf_op jit(solution)/shard_map/reduce_scatter | solution.py:453
  361.4 13.9 %copy-start.53 = (bf16[3,256,2048]{2,1,0:T(8,128)(2,1)S(1)}, bf16[3,256,2048]{2,1,0:T(8,128)(2,1)}, u32[]{:S(2)}) copy-start(bf16[3,256,2048]{2,1,0:T(8,128)(2,1)} %param.17) | copy-start | bytes 9437188
  401.3 59.1 %copy-start.45 = (bf16[192,2048]{1,0:T(8,128)(2,1)S(1)}, bf16[192,2048]{1,0:T(8,128)(2,1)}, u32[]{:S(2)}) copy-start(bf16[192,2048]{1,0:T(8,128)(2,1)} %reduce-scatter.7.cloned.1.call-done) | copy-start | bytes 2359300
  401.3 128.8 %all-gather.23.cloned.1.call-start = ((), (), s32[]{:S(2)}) async-start(), calls=%async_computation.13 | async-start | bytes 3932160 | tf_op jit(solution)/shard_map/all_gather | solution.py:456
  463.2 3.2 copy-start.62
  466.4 69.2 %copy-start.5 = (f32[3,64,512]{2,1,0:T(8,128)S(1)}, f32[3,64,512]{2,1,0:T(8,128)}, u32[]{:S(2)}) copy-start(f32[3,64,512]{2,1,0:T(8,128)} %copy-done.4) | copy-start | bytes 1179652
  466.5 69.2 %copy-start.12 = (f32[3,80,256]{2,1,0:T(8,128)S(1)}, f32[3,80,256]{2,1,0:T(8,128)}, u32[]{:S(2)}) copy-start(f32[3,80,256]{2,1,0:T(8,128)} %copy-done.10) | copy-start | bytes 737284
  466.5 69.2 %copy-start.18 = (f32[64,768]{1,0:T(8,128)S(1)}, f32[64,768]{1,0:T(8,128)}, u32[]{:S(2)}) copy-start(f32[64,768]{1,0:T(8,128)} %copy-done.16) | copy-start | bytes 589828
  466.5 69.2 %copy-start.23 = (f32[64,768]{1,0:T(8,128)S(1)}, f32[64,768]{1,0:T(8,128)}, u32[]{:S(2)}) copy-start(f32[64,768]{1,0:T(8,128)} %copy-done.21) | copy-start | bytes 589828
  466.5 69.2 %copy-start.38 = (f32[3,256,256]{2,1,0:T(8,128)S(1)}, f32[3,256,256]{2,1,0:T(8,128)}, u32[]{:S(2)}) copy-start(f32[3,256,256]{2,1,0:T(8,128)} %copy-done.37) | copy-start | bytes 2359300
  466.5 69.2 %copy-start.40 = (f32[64,768]{1,0:T(8,128)S(1)}, f32[64,768]{1,0:T(8,128)}, u32[]{:S(2)}) copy-start(f32[64,768]{1,0:T(8,128)} %copy-done.39) | copy-start | bytes 589828
  466.5 69.2 %copy-start.42 = (f32[64,768]{1,0:T(8,128)S(1)}, f32[64,768]{1,0:T(8,128)}, u32[]{:S(2)}) copy-start(f32[64,768]{1,0:T(8,128)} %copy-done.41) | copy-start | bytes 589828
  466.5 147.9 %all-gather.29.cloned.1.call-start = ((), (), s32[]{:S(2)}) async-start(), calls=%async_computation.19 | async-start | bytes 3932160 | tf_op jit(solution)/shard_map/all_gather | solution.py:480
  571.6 45.3 %copy-start.1 = (bf16[768,1536]{1,0:T(8,128)(2,1)S(1)}, bf16[768,1536]{1,0:T(8,128)(2,1)}, u32[]{:S(2)}) copy-start(bf16[768,1536]{1,0:T(8,128)(2,1)} %copy-done) | copy-start | bytes 7077892
  571.6 125.1 %reduce-scatter.13.cloned.1.call-start = ((), (), s32[]{:S(2)}) async-start(), calls=%async_computation.14 | async-start | bytes 3932160 | tf_op jit(solution)/shard_map/reduce_scatter | solution.py:453
  636.3 122.9 %reduce-scatter.9.cloned.1.call-start = ((), (), s32[]{:S(2)}) async-start(), calls=%async_computation.10 | async-start | bytes 3932160 | tf_op jit(solution)/shard_map/reduce_scatter | solution.py:453
  647.1 235.1 %reduce-scatter.17.cloned.1.call-start = ((), (), s32[]{:S(2)}) async-start(), calls=%async_computation.17 | async-start | bytes 19464192 | tf_op jit(solution)/shard_map/reduce_scatter | solution.py:450
  647.1 9.0 copy-start.64
  678.1 18.6 %copy-start.59 = (f32[2048]{0:T(1024)S(1)}, f32[2048]{0:T(1024)}, u32[]{:S(2)}) copy-start(f32[2048]{0:T(1024)} %param.18) | copy-start | bytes 24580
  678.1 81.1 %copy-start.46 = (bf16[192,2048]{1,0:T(8,128)(2,1)S(1)}, bf16[192,2048]{1,0:T(8,128)(2,1)}, u32[]{:S(2)}) copy-start(bf16[192,2048]{1,0:T(8,128)(2,1)} %reduce-scatter.7.cloned.1.call-done) | copy-start | bytes 2359300
  678.1 81.1 %copy-start.48 = (bf16[192,2048]{1,0:T(8,128)(2,1)S(1)}, bf16[192,2048]{1,0:T(8,128)(2,1)}, u32[]{:S(2)}) copy-start(bf16[192,2048]{1,0:T(8,128)(2,1)} %reduce-scatter.11.cloned.1.call-done) | copy-start | bytes 2359300
  678.1 81.1 %copy-start.57 = (f32[2048]{0:T(1024)S(1)}, f32[2048]{0:T(1024)}, u32[]{:S(2)}) copy-start(f32[2048]{0:T(1024)} %param.19) | copy-start | bytes 24580
  678.1 81.1 %copy-start.63 = (f32[192]{0:T(256)S(1)}, f32[192]{0:T(256)}, u32[]{:S(2)}) copy-start(f32[192]{0:T(256)} %copy-done.62) | copy-start | bytes 2308
  678.1 269.0 %all-gather.21.cloned.1.call-start = ((), (), s32[]{:S(2)}) async-start(), calls=%async_computation.11 | async-start | bytes 3932160 | tf_op jit(solution)/shard_map/all_gather | solution.py:456
  759.2 5.3 copy-start.36
  763.7 247.3 %all-gather.25.cloned.1.call-start = ((), (), s32[]{:S(2)}) async-start(), calls=%async_computation.15 | async-start | bytes 3932160 | tf_op jit(solution)/shard_map/all_gather | solution.py:456
  764.4 4.0 copy-start.30
  764.4 4.0 copy-start.32
  764.4 4.0 copy-start.44
  764.5 321.7 %reduce-scatter.15.cloned.1.call-start = ((), (), s32[]{:S(2)}) async-start(), calls=%async_computation.16 | async-start | bytes 9732096 | tf_op jit(solution)/shard_map/reduce_scatter | solution.py:450
  764.5 3.9 copy-start.52
  884.1 4.1 copy-start.47
  1086.1 4.3 copy-start.49
  (35 other events, 51.7 us)
Sparse Core Ops, SparseCore 0:
  10.5 50.4 all-gather.14
  76.9 44.0 all-gather.26
  122.8 104.7 all-gather.16
  233.2 60.2 reduce-scatter.6
  297.9 63.5 all-gather.18
  401.4 58.8 reduce-scatter.10
  466.6 63.5 all-gather.22
  571.7 42.6 all-gather.28
  636.4 60.2 reduce-scatter.12
  698.9 60.2 reduce-scatter.8
  762.8 119.3 reduce-scatter.16
  883.7 63.4 all-gather.20
  948.8 62.1 all-gather.24
  1014.8 71.2 reduce-scatter.14

commit v2 on v1

--- a/solution.py
+++ b/solution.py
@@ -2,6 +2,7 @@
 import jax.numpy as jnp
 from jax import lax
 from jax.experimental import pallas as pl
+from jax.experimental.layout import Layout, with_layout_constraint
 from jax.experimental.pallas import tpu as pltpu
 from jax.sharding import PartitionSpec as P
 
@@ -75,6 +76,14 @@
 def stack_chunks(array, chunks):
     chunk = chunk_of(*array.shape)
     return jnp.concatenate([jnp.where(chunk == c, array, 0.0) for c in range(1, chunks)], axis=0)
+
+
+def rows_of(ref):
+    return ref[...].reshape(-1, ref.shape[-1])
+
+
+def store_rows(ref, value):
+    ref[...] = value.reshape(ref.shape)
 
 
 def aux_rows(tokens):
@@ -125,8 +134,8 @@
     lev_ref[...] = levels
     tail = jnp.exp(levels[:, tokens - 1 : tokens] - levels + aux_ref[0, base + 2 : base + 3, :])
     tail = split2(tail * one_ref[...])
-    ks_ref[0] = dot2(tail, k_ref[...], 1, 0)
-    vs_ref[0] = dot2(tail, v_ref[...], 1, 0)
+    ks_ref[0] = dot2(tail, rows_of(k_ref), 1, 0)
+    vs_ref[0] = dot2(tail, rows_of(v_ref), 1, 0)
 
 
 def forward_kernel(
@@ -137,7 +146,7 @@
     chunks = tokens // CHUNK
     base, _ = aux_rows(tokens)
     levels, one = lev_ref[...], one_ref[...]
-    q, k, v = q_ref[...], k_ref[...], v_ref[...]
+    q, k, v = rows_of(q_ref), rows_of(k_ref), rows_of(v_ref)
     chunk = chunk_of(SLOTS, tokens)
     kq = dg(k, q, 1, 1)
     d_scr[...] = pick_rows(kq, CHUNK, chunks)
@@ -178,7 +187,7 @@
     out = dot2(split2(mixed_t), v, 0, 0) + dot3(split2(probs * carried), split2(vi_ref[0]), 0, 0)
     mix_ref[...] = out
     unit = out * lax.rsqrt(jnp.mean(out * out, axis=1, keepdims=True) + epsilon)
-    no_ref[...] = (unit * gain_ref[...]).astype(bf16)
+    store_rows(no_ref, (unit * gain_ref[...]).astype(bf16))
 
 
 def backward_kernel(
@@ -189,8 +198,8 @@
     chunks = tokens // CHUNK
     base, _ = aux_rows(tokens)
     levels, one, probs = lev_ref[...], one_ref[...], p_ref[...]
-    q, k, v = q_ref[...], k_ref[...], v_ref[...]
-    out, go = mix_ref[...], go_ref[...]
+    q, k, v = rows_of(q_ref), rows_of(k_ref), rows_of(v_ref)
+    out, go = mix_ref[...], rows_of(go_ref)
     factor = lax.rsqrt(jnp.mean(out * out, axis=1, keepdims=True) + epsilon)
     unit = out * factor
     hg_ref[0] = jnp.sum(go * unit, axis=0, keepdims=True)
@@ -236,7 +245,7 @@
     mz_t += dot3(wst, zst, 0, 0)
     mz = split2(mz_t)
     zc, pc = split2(dz * carried), split2(probs * carried)
-    gq_ref[...] = (dot2(mz, k, 0, 0) + dot3(zc, kin, 0, 0)).astype(bf16)
+    store_rows(gq_ref, (dot2(mz, k, 0, 0) + dot3(zc, kin, 0, 0)).astype(bf16))
     gk_ref[...] = dot2(mz, q, 1, 0)
     gv_ref[...] = dot3(split2(mt_ref[0]), g, 1, 0)
     dk_ref[0] = dot2(zc, q, 1, 0)
@@ -265,14 +274,14 @@
     tokens = lev_ref.shape[1]
     base, _ = aux_rows(tokens)
     levels, one = lev_ref[...], one_ref[...]
-    k, v = k_ref[...], v_ref[...]
+    k, v = rows_of(k_ref), rows_of(v_ref)
     tail = jnp.exp(levels[:, tokens - 1 : tokens] - levels + aux_ref[0, base + 2 : base + 3, :])
     end = jnp.exp(levels[:, tokens - 1 : tokens] + aux_ref[0, base + 1 : base + 2, tokens - 1 : tokens])
     dk, dv = dk_ref[0], dv_ref[0]
     dks, dvs = split2(dk), split2(dv)
     weights = split2(tail * one)
-    gko_ref[...] = (gk_ref[...] + dot3(weights, dks, 0, 0)).astype(bf16)
-    gvo_ref[...] = (gv_ref[...] + dot3(weights, dvs, 0, 0)).astype(bf16)
+    store_rows(gko_ref, (gk_ref[...] + dot3(weights, dks, 0, 0)).astype(bf16))
+    store_rows(gvo_ref, (gv_ref[...] + dot3(weights, dvs, 0, 0)).astype(bf16))
     rows = r_ref[...] + tail * (dot2(dks, k, 1, 1) + dot2(dvs, v, 1, 1))
     final_k = end * ki_ref[0] + ks_ref[0]
     final_v = end * vi_ref[0] + vs_ref[0]
@@ -287,10 +296,11 @@
     gl_ref[...] = (grad * sig_ref[...]).astype(bf16)
 
 
-def seq_specs(tokens):
-    def tok(col, width=HEAD_DIM):
-        return pl.BlockSpec((tokens, width), lambda i: (i, col))
-
+def seq_specs(tokens, members):
+    def own(col):
+        return pl.BlockSpec((members, 1, tokens // members, HEAD_DIM), lambda i: (0, i, 0, col))
+
+    tok = pl.BlockSpec((tokens, HEAD_DIM), lambda i: (i, 0))
     lane = pl.BlockSpec((SLOTS, tokens), lambda i: (0, i))
     _, rows = aux_rows(tokens)
     aux = pl.BlockSpec((1, rows, tokens), lambda i: (i, 0, 0))
@@ -298,7 +308,7 @@
     gain = pl.BlockSpec((1, HEAD_DIM), lambda i: (0, 0))
     square = pl.BlockSpec((1, tokens, tokens), lambda i: (i, 0, 0))
     row = pl.BlockSpec((1, 1, HEAD_DIM), lambda i: (i, 0, 0))
-    return tok, lane, aux, state, gain, square, row
+    return own, tok, lane, aux, state, gain, square, row
 
 
 def params(mib):
@@ -315,11 +325,11 @@
 
 def run_states(qkv, ld, one, aux):
     count, _, tokens = aux.shape
-    tok, lane, auxs, state, _, _, _ = seq_specs(tokens)
+    own, tok, lane, auxs, state, _, _, _ = seq_specs(tokens, qkv.shape[0])
     return pl.pallas_call(
         state_kernel,
         grid=(count,),
-        in_specs=[tok(1), tok(2), lane, lane, auxs],
+        in_specs=[own(1), own(2), lane, lane, auxs],
         out_specs=[lane, state, state],
         out_shape=[
             shape((SLOTS, count * tokens), f32),
@@ -338,15 +348,15 @@
 
 def run_forward(qkv, levels, one, aux, key_in, value_in, gain):
     count, _, tokens = aux.shape
-    tok, lane, auxs, state, gains, square, _ = seq_specs(tokens)
+    own, tok, lane, auxs, state, gains, square, _ = seq_specs(tokens, qkv.shape[0])
     stack = big_scratch(tokens)
     return pl.pallas_call(
         forward_kernel,
         grid=(count,),
-        in_specs=[tok(0), tok(1), tok(2), lane, lane, auxs, state, state, gains],
-        out_specs=[tok(0), tok(0), lane, lane, square],
+        in_specs=[own(0), own(1), own(2), lane, lane, auxs, state, state, gains],
+        out_specs=[own(0), tok, lane, lane, square],
         out_shape=[
-            shape((count * tokens, HEAD_DIM), bf16),
+            shape(qkv.shape[:3] + (HEAD_DIM,), bf16),
             shape((count * tokens, HEAD_DIM), f32),
             shape((SLOTS, count * tokens), f32),
             shape((SLOTS, count * tokens), f32),
@@ -365,15 +375,15 @@
 
 def run_backward(qkv, levels, one, aux, key_in, value_in, gain, mixed, probs, scores, mixed_t, grad_o):
     count, _, tokens = aux.shape
-    tok, lane, auxs, state, gains, square, row = seq_specs(tokens)
+    own, tok, lane, auxs, state, gains, square, row = seq_specs(tokens, qkv.shape[0])
     stack = big_scratch(tokens)
     return pl.pallas_call(
         backward_kernel,
         grid=(count,),
-        in_specs=[tok(0), tok(1), tok(2), lane, lane, auxs, state, state, gains, tok(0), lane, lane, square, tok(0)],
-        out_specs=[tok(0), tok(0), tok(0), lane, lane, state, state, row],
+        in_specs=[own(0), own(1), own(2), lane, lane, auxs, state, state, gains, tok, lane, lane, square, own(0)],
+        out_specs=[own(0), tok, tok, lane, lane, state, state, row],
         out_shape=[
-            shape((count * tokens, HEAD_DIM), bf16),
+            shape(qkv.shape[:3] + (HEAD_DIM,), bf16),
             shape((count * tokens, HEAD_DIM), f32),
             shape((count * tokens, HEAD_DIM), f32),
             shape((SLOTS, count * tokens), f32),
@@ -397,16 +407,16 @@
 
 def run_finish(qkv, levels, one, sig, aux, sums, key_in, value_in, key_own, value_own, gk, gv, rows, acts, dk, dv):
     count, _, tokens = aux.shape
-    tok, lane, auxs, state, _, square, _ = seq_specs(tokens)
+    own, tok, lane, auxs, state, _, square, _ = seq_specs(tokens, qkv.shape[0])
     return pl.pallas_call(
         finish_kernel,
         grid=(count,),
-        in_specs=[tok(1), tok(2), lane, lane, lane, auxs, square, state, state, state, state]
-        + [tok(0), tok(0), lane, lane, state, state],
-        out_specs=[tok(0), tok(0), lane],
+        in_specs=[own(1), own(2), lane, lane, lane, auxs, square, state, state, state, state]
+        + [tok, tok, lane, lane, state, state],
+        out_specs=[own(0), own(0), lane],
         out_shape=[
-            shape((count * tokens, HEAD_DIM), bf16),
-            shape((count * tokens, HEAD_DIM), bf16),
+            shape(qkv.shape[:3] + (HEAD_DIM,), bf16),
+            shape(qkv.shape[:3] + (HEAD_DIM,), bf16),
             shape((SLOTS, count * tokens), bf16),
         ],
         compiler_params=params(40),
@@ -426,6 +436,27 @@
 
 def norm_back(unit_val, factor, grad_unit):
     return factor * (grad_unit - unit_val * jnp.mean(grad_unit * unit_val, axis=-1, keepdims=True))
+
+
+def row_major(array):
+    return with_layout_constraint(array, Layout(major_to_minor=tuple(range(array.ndim))))
+
+
+def after(values, *events):
+    return lax.optimization_barrier((values, events))[0]
+
+
+def line_gather(own, axis, put, buffer):
+    size, here = lax.axis_size(axis), lax.axis_index(axis)
+    for step_to in (1, -1):
+        moving = own
+        for s in range(1, size):
+            sources = range(s - 1, size - 1) if step_to == 1 else range(1, size - s + 1)
+            moving = lax.ppermute(moving, axis, [(i, i + step_to) for i in sources])
+            origin = here - s * step_to
+            valid = (origin >= 0) & (origin < size)
+            buffer = put(buffer, moving, jnp.where(valid, origin, here))
+    return put(buffer, own, here)
 
 
 def per_device(
@@ -437,30 +468,98 @@
     hidden_units = w_gate.shape[1]
     heads = w_query.shape[1]
     tp_place, here = lax.axis_index("tp"), lax.axis_index("ctx")
-    places = lax.axis_size("ctx")
-    shard = rows // lax.axis_size("tp")
+    swap_x = [(0, 1), (1, 0), (2, 3), (3, 2)]
+    places, members = lax.axis_size("ctx"), lax.axis_size("tp")
+    part = tokens // members
+
+    def owner_first(array):
+        array = array.reshape(count, members, part, width).transpose(1, 0, 2, 3)
+        return array.reshape(rows, width)
+
+    def natural(array):
+        return array.reshape(members, count, part, width).transpose(1, 0, 2, 3)
+
+    def lanes(array, order):
+        array = array.reshape(array.shape[0], *order, part).transpose(0, 2, 1, 3)
+        return array.reshape(array.shape[0], rows)
+
+    def blocks_of(array):
+        return array.reshape(members, count, part, -1)
 
     def mine(array):
-        return lax.dynamic_slice_in_dim(array, tp_place * shard, shard, 0)
+        return lax.dynamic_slice_in_dim(array, tp_place * (count * part), count * part, 0)
+
+    def to_shards(array):
+        return lax.psum_scatter(array, "tp", scatter_dimension=0, tiled=True).astype(f32)
+
+    def from_shards(array):
+        return lax.all_gather(array.astype(bf16), "tp", axis=0, tiled=True)
 
     def gather_rows(array):
         return lax.all_gather(array, ("dp", "ctx"), axis=0, tiled=True)
 
-    def scatter_rows(array):
-        return lax.psum_scatter(array, ("dp", "ctx"), scatter_dimension=0, tiled=True).astype(f32)
-
-    def to_shards(array):
-        return lax.psum_scatter(array.astype(bf16), "tp", scatter_dimension=0, tiled=True).astype(f32)
-
-    def from_shards(array):
-        return lax.all_gather(array.astype(bf16), "tp", axis=0, tiled=True)
-
+    def scatter_rows(array, wait=None):
+        if places != 4:
+            return lax.psum_scatter(
+                array, ("dp", "ctx"), scatter_dimension=0, tiled=True
+            ).astype(f32), ()
+        core, y, x = lax.axis_index("dp"), here // 2, here % 2
+        size, cols = array.shape[0] // 8, array.shape[1]
+        half = size // 2
+
+        def pick(value, index, axis):
+            return lax.dynamic_index_in_dim(value, index, axis, keepdims=False)
+
+        def add(a, b, dtype=bf16):
+            return (a.astype(f32) + b.astype(f32)).astype(dtype)
+
+        swap_y = [(0, 2), (2, 0), (1, 3), (3, 1)]
+        array = row_major(array).reshape(2, 2, 2, size, cols)
+        other = lax.ppermute(pick(array, 1 - core, 0), "dp", [(0, 1), (1, 0)])
+        chip = add(pick(array, core, 0), other)
+        over_x = lax.ppermute(pick(chip[:, :, :half], 1 - x, 1), "ctx", swap_x)
+        over_y = lax.ppermute(pick(chip[:, :, half:], 1 - y, 0), "ctx", swap_y)
+        upper = add(pick(chip[:, :, :half], x, 1), over_x)
+        lower = add(pick(chip[:, :, half:], y, 0), over_y)
+        last_y = lax.ppermute(pick(upper, 1 - y, 0), "ctx", swap_y)
+        last_x = lax.ppermute(pick(lower, 1 - x, 0), "ctx", swap_x)
+        upper = add(pick(upper, y, 0), last_y, f32)
+        lower = add(pick(lower, x, 0), last_x, f32)
+        return jnp.concatenate([upper, lower], axis=0), (chip, upper, lower)
+
+    def gather_in_parts(array, parts):
+        buffer = jnp.zeros((members, parts, count * part // parts, width), bf16)
+        for c, block in enumerate(array.astype(bf16).reshape(buffer.shape[1:])):
+
+            def put(buf, value, owner, c=c):
+                return lax.dynamic_update_slice(buf, value[None, None], (owner, c, 0, 0))
+
+            buffer = line_gather(block, "tp", put, buffer)
+        return buffer.reshape(rows, width)
+
+    def from_partner(array, distance):
+        return lax.ppermute(array, "tp", [(i, i ^ distance) for i in range(members)])
+
+    def sum_small(array):
+        if places != 4:
+            return lax.psum(array, ("dp", "ctx", "tp"))
+        array += lax.ppermute(array, "dp", [(0, 1), (1, 0)])
+        for axis in ("ctx", "tp"):
+            for r in (1, 2):
+                array += lax.ppermute(array, axis, [(i, i ^ r) for i in range(4)])
+        return array
+
+    cut = 3 * heads
     w_in = gather_rows(jnp.concatenate([w_query, w_key, w_value, w_decay], axis=1))
-    w_rest = gather_rows(jnp.concatenate([w_out.T, w_gate, w_up, w_down.T], axis=1))
-    w_qkv, w_dec = w_in[:, : 3 * heads], w_in[:, 3 * heads :]
-    w_o = w_rest[:, :heads]
-    w_gu = w_rest[:, heads : heads + 2 * hidden_units]
-    w_d = w_rest[:, heads + 2 * hidden_units :]
+    w_qkv, w_dec = w_in[:, :cut], w_in[:, cut:]
+    w_out_t = w_out.T
+    w_heads = gather_rows(
+        jnp.concatenate([w_out_t] + [from_partner(w_out_t, r) for r in range(1, members)], axis=1)
+    )
+    w_o = w_heads[:, :heads]
+    w_rest = gather_rows(jnp.concatenate([w_gate, w_up, w_down.T], axis=1))
+    w_gu = w_rest[:, : 2 * hidden_units]
+    w_d = w_rest[:, 2 * hidden_units :]
 
     edges = lax.all_gather(jnp.stack([segments[:, 0], segments[:, -1]]), "ctx")
     prev_doc = jnp.where(here > 0, edges[jnp.maximum(here - 1, 0), 1], -1)
@@ -476,97 +575,148 @@
         index[None, :] < jnp.maximum(index[:, None], here)
     )
 
-    def exchange(keys, values, coefs):
-        every = lax.all_gather(jnp.concatenate([keys, values], axis=2), "ctx")
-        total = jnp.sum(every * coefs[..., None], axis=0)
-        return total[..., :HEAD_DIM], total[..., HEAD_DIM:]
-
-    x = layer_input.reshape(rows, width)
+    square = places == 4
+    if square:
+        low = 2 * (here // 2)
+        is_low = here == low
+
+        def exchange(keys, values, coefs, forward, own_end, near_end):
+            own = jnp.concatenate([keys, values], axis=2)
+            near = lax.ppermute(own.astype(bf16), "ctx", swap_x).astype(f32)
+            first, second = jnp.where(is_low, own, near), jnp.where(is_low, near, own)
+            low_end, high_end = jnp.where(is_low, own_end, near_end), jnp.where(is_low, near_end, own_end)
+            if forward:
+                link = lax.dynamic_index_in_dim(edges, low, 0, False)[1] == lax.dynamic_index_in_dim(edges, low + 1, 0, False)[1]
+                joined = second + jnp.where(link[:, None], jnp.exp(high_end), 0.0)[..., None] * first
+                pairs, origin = [(0, 2), (1, 3)], 1
+            else:
+                link = lax.dynamic_index_in_dim(edges, low, 0, False)[0] == lax.dynamic_index_in_dim(edges, low + 1, 0, False)[0]
+                joined = first + jnp.where(link[:, None], jnp.exp(low_end), 0.0)[..., None] * second
+                pairs, origin = [(2, 0), (3, 1)], 2
+            far = lax.ppermute(joined.astype(bf16), "ctx", pairs).astype(f32)
+            beside = lax.dynamic_index_in_dim(coefs, here + jnp.where(is_low, 1, -1), 0, False)
+            total = beside[..., None] * near + coefs[origin][..., None] * far
+            return total[..., :HEAD_DIM], total[..., HEAD_DIM:]
+
+        def level_ends(own_end):
+            near_end = lax.ppermute(own_end, "ctx", swap_x)
+            slot = (index == here)[:, None, None]
+            beside = (index == here + jnp.where(is_low, 1, -1))[:, None, None]
+            return jnp.where(slot, own_end, 0.0) + jnp.where(beside, near_end, 0.0), near_end
+
+    else:
+
+        def exchange(keys, values, coefs, forward, own_end, near_end):
+            every = lax.all_gather(jnp.concatenate([keys, values], axis=2), "ctx")
+            total = jnp.sum(every * coefs[..., None], axis=0)
+            return total[..., :HEAD_DIM], total[..., HEAD_DIM:]
+
+        def level_ends(own_end):
+            return lax.all_gather(own_end, "ctx"), own_end
+
+    x = owner_first(layer_input)
     unit_one, factor_one, scaled_one = rms_parts(x.astype(f32), norm1_gain)
     normed1 = scaled_one.astype(bf16)
-    qkv = matmul(normed1, w_qkv).astype(bf16)
+    qkv = blocks_of(matmul(normed1, w_qkv).astype(bf16))
     bias_here = lax.dynamic_slice_in_dim(decay_bias, tp_place * SLOTS, SLOTS)
-    logits = matmul(w_dec, normed1, 0, 1) + bias_here[:, None]
+    logits = lanes(matmul(w_dec, normed1, 0, 1), (members, count)) + bias_here[:, None]
     log_decay = jax.nn.log_sigmoid(logits) / gate_norm
     one = -jnp.expm1(log_decay)
     sig = jax.nn.sigmoid(-logits) / gate_norm
     levels, key_own, value_own = run_states(qkv, log_decay, one, aux)
-    ends = lax.all_gather(levels[:, tokens - 1 :: tokens].T, "ctx")
+    own_end = levels[:, tokens - 1 :: tokens].T
+    ends, near_end = level_ends(own_end)
     span = jnp.exp(jnp.sum(jnp.where(between[:, :, None, None], ends[None], 0.0), axis=1))
     coef_in = jnp.where(reach_in[..., None], span, 0.0)
     coef_out = jnp.where(reach_out[..., None], span, 0.0)
-    key_in, value_in = exchange(key_own, value_own, coef_in)
+    key_in, value_in = exchange(key_own, value_own, coef_in, True, own_end, near_end)
     gain = head_gain[None, :]
     normed_o, mixed, probs, scores, mixed_t = run_forward(
         qkv, levels, one, aux, key_in, value_in, gain
     )
-    hidden = mine(x).astype(f32) + to_shards(matmul(normed_o, w_o, 1, 1))
+    by_owner = normed_o.reshape(members, count * part, heads)
+
+    def for_partner(r):
+        return lax.dynamic_index_in_dim(by_owner, tp_place ^ r, 0, keepdims=False)
+
+    normed_heads = jnp.concatenate(
+        [for_partner(0)] + [from_partner(for_partner(r), r) for r in range(1, members)], axis=1
+    )
+    hidden = mine(x).astype(f32) + matmul(normed_heads, w_heads, 1, 1)
     unit_two, factor_two, scaled_two = rms_parts(hidden, norm2_gain)
-    normed2 = from_shards(scaled_two)
+    normed2 = gather_in_parts(scaled_two, count)
     pre = matmul(normed2, w_gu)
     gate_pre, up_pre = pre[:, :hidden_units], pre[:, hidden_units:]
     gate_sig = jax.nn.sigmoid(gate_pre)
     gate_silu = gate_pre * gate_sig
     hidden_act = (gate_silu * up_pre).astype(bf16)
-    feed = to_shards(matmul(hidden_act, w_d, 1, 1))
-    output = from_shards(hidden + feed)
-
-    grad_feed = cotangent.reshape(rows, width)
+
+    grad_feed = owner_first(cotangent)
     grad_act = matmul(grad_feed, w_d)
     grad_gate = (grad_act * up_pre * gate_sig * (1.0 + gate_pre * (1.0 - gate_sig))).astype(bf16)
     grad_up = (grad_act * gate_silu).astype(bf16)
     grad_gu = jnp.concatenate([grad_gate, grad_up], axis=1)
-    grad_n2 = to_shards(matmul(grad_gu, w_gu, 1, 1))
-    grad_wgu = matmul(normed2, grad_gu, 0, 0).astype(bf16)
-    grad_wd = matmul(grad_feed, hidden_act, 0, 0).astype(bf16)
-    ffn_rows = scatter_rows(jnp.concatenate([grad_wgu, grad_wd], axis=1))
+    part_n2 = matmul(grad_gu, w_gu, 1, 1).astype(bf16)
+    grad_n2 = to_shards(part_n2)
+    begun = lax.ppermute(part_n2[:16, :128], "dp", [(0, 1), (1, 0)])
+    normed2, grad_gu, hidden_act = after((normed2, grad_gu, hidden_act), begun)
+    rows_wgu, stages_wgu = scatter_rows(matmul(normed2, grad_gu, 0, 0).astype(bf16))
+    feed_part = matmul(hidden_act, w_d, 1, 1).astype(bf16)
+    rows_wd, stages_wd = scatter_rows(matmul(grad_feed, hidden_act, 0, 0).astype(bf16))
     gain_two_part = jnp.sum(grad_n2 * unit_two, axis=0)
     grad_hidden = mine(grad_feed).astype(f32) + norm_back(unit_two, factor_two, grad_n2 * norm2_gain)
-    grad_attn = from_shards(grad_hidden)
+    grad_attn = gather_in_parts(grad_hidden, count)
+    feed = to_shards(after(feed_part, grad_n2))
     grad_o = matmul(grad_attn, w_o)
-    grad_wo = matmul(grad_attn, normed_o, 0, 0).astype(bf16)
+    grad_o, feed = after((grad_o, feed), stages_wgu[:1], stages_wd[:1])
+    output = from_shards(hidden + feed)
     grad_q, gk, gv, row_sums, acts, dk, dv, head_part = run_backward(
-        qkv, levels, one, aux, key_in, value_in, gain, mixed, probs, scores, mixed_t, grad_o
-    )
-    dk_later, dv_later = exchange(dk, dv, coef_out)
+        qkv, levels, one, aux, key_in, value_in, gain, mixed, probs, scores, mixed_t, blocks_of(grad_o)
+    )
+    dk_later, dv_later = exchange(dk, dv, coef_out, False, own_end, near_end)
+    grad_wo = matmul(grad_attn, normed_o.reshape(rows, heads), 0, 0).astype(bf16)
+    dk_later = after(dk_later, stages_wgu, stages_wd, grad_wo, output)
     grad_k, grad_v, grad_logits = run_finish(
         qkv, levels, one, sig, aux, sums, key_in, value_in, key_own, value_own,
         gk, gv, row_sums, acts, dk_later, dv_later,
     )
-    grad_all = jnp.concatenate([grad_q, grad_k, grad_v, grad_logits.T], axis=1)
-    grad_n1 = to_shards(matmul(grad_all, w_in, 1, 1))
-    grad_in = matmul(normed1, grad_all, 0, 0).astype(bf16)
-    att_rows = scatter_rows(jnp.concatenate([grad_in, grad_wo], axis=1))
-    unit_mine, factor_mine = mine(unit_one), mine(factor_one)
-    gain_one_part = jnp.sum(grad_n1 * unit_mine, axis=0)
-    input_grad = grad_hidden + norm_back(unit_mine, factor_mine, grad_n1 * norm1_gain)
-    input_grad = from_shards(input_grad).astype(f32)
+    decay_rows = lanes(grad_logits, (count, members))
+    grad_all = jnp.concatenate(
+        [a.reshape(rows, heads) for a in (grad_q, grad_k, grad_v)] + [decay_rows.T], axis=1
+    )
+    part_n1 = (matmul(grad_all[:, :cut], w_qkv, 1, 1) + matmul(decay_rows, w_dec, 0, 1)).astype(bf16)
+    grad_n1 = to_shards(part_n1)
+    rows_wo, _ = scatter_rows(grad_wo)
+    grad_in = matmul(normed1, after(grad_all, grad_n1), 0, 0).astype(bf16)
+    rows_att, _ = scatter_rows(grad_in)
+    gain_one_part = jnp.sum(part_n1.astype(f32) * unit_one, axis=0)
     bias_part = lax.dynamic_update_slice_in_dim(
         jnp.zeros_like(decay_bias),
         jnp.sum(grad_logits.astype(f32), axis=1),
         tp_place * SLOTS,
         0,
     )
-    small = lax.psum(
-        jnp.concatenate([gain_one_part, gain_two_part, jnp.sum(head_part, axis=(0, 1)), bias_part]),
-        ("dp", "ctx", "tp"),
-    )
-    cut = 3 * heads
+    small = jnp.concatenate(
+        [gain_one_part, gain_two_part, jnp.sum(head_part, axis=(0, 1)), bias_part]
+    )
+    small = sum_small(small)
+    input_grad = grad_hidden + norm_back(mine(unit_one), mine(factor_one), grad_n1 * norm1_gain)
+    input_grad = natural(from_shards(input_grad)).astype(f32)
     return (
-        output.reshape(count, tokens, width),
+        natural(output).reshape(count, tokens, width),
         input_grad.reshape(count, tokens, width),
         small[:width],
         small[width : 2 * width],
         small[2 * width : 2 * width + HEAD_DIM],
         small[2 * width + HEAD_DIM :],
-        att_rows[:, :heads],
-        att_rows[:, heads : 2 * heads],
-        att_rows[:, 2 * heads : cut],
-        att_rows[:, cut : cut + SLOTS],
-        att_rows[:, cut + SLOTS :].T,
-        ffn_rows[:, :hidden_units],
-        ffn_rows[:, hidden_units : 2 * hidden_units],
-        ffn_rows[:, 2 * hidden_units :].T,
+        rows_att[:, :heads],
+        rows_att[:, heads : 2 * heads],
+        rows_att[:, 2 * heads : cut],
+        rows_att[:, cut:],
+        rows_wo.T,
+        rows_wgu[:, :hidden_units],
+        rows_wgu[:, hidden_units:],
+        rows_wd.T,
     )
 
 

time: 1110 us -> 713 us (0.64)
  waiting for transfers between devices: 752 us -> 216 us
  starting transfers between devices: 1.29 us -> 100 us
  local copies, waits for them, and re-layouts: 47.3 us -> 127 us
  blocking collectives: 58.3 us -> 8.09 us
    reduce_scatter x6 -> x3, waiting for transfers between devices: 327 us -> 19.1 us  [to_shards(): lax.psum_scatter(array, 'tp', scatter_dimension=0, tiled=True).astype(f32)]
    all_gather x4 -> x2, waiting for transfers between devices: 248 us -> 18.6 us  [from_shards(): return lax.all_gather(array.astype(bf16), 'tp', axis=0, tiled=True)]
    ppermute x0 -> x72, waiting for transfers between devices: none -> 178 us  [the longest x36 51.3 us: line_gather(): moving = lax.ppermute(moving, axis, [(i, i + step_to) for i in sources])]
    all_gather x2 -> x3, waiting for transfers between devices: 108 us -> 0.01 us  [gather_rows(): return lax.all_gather(array, ('dp', 'ctx'), axis=0, tiled=True)]
    ppermute x0 -> x72, starting transfers between devices: none -> 98.9 us  [the longest x36 55 us: line_gather(): moving = lax.ppermute(moving, axis, [(i, i + step_to) for i in sources])]
    all_gather x2 -> x0, waiting for transfers between devices: 68.8 us -> none  [exchange(): every = lax.all_gather(jnp.concatenate([keys, values], axis=2), 'ctx')]
    psum x1 -> x0, blocking collectives: 40.8 us -> none  [per_device(): lax.psum(jnp.concatenate([gain_one_part, gain_two_part, jnp.sum(head_part...]
    convert_element_type x2 -> x19, other arithmetic: 2.05 us -> 27.3 us  [the longest x12 20.2 us: add(): return (a.astype(f32) + b.astype(f32)).astype(dtype)]
  transfers between devices with their start and end apart: 14 -> 80, of which waited for: 14 -> 35; matrix products, arithmetic and copies ran while one was open for 9% -> 31% of each run, Pallas kernels for 1% -> 7%
where the time goes in v2:
time: 713 us; the launch traced here: 704 us
  waiting for transfers between devices  216 us (30%)
  local copies, waits for them, and re-layouts  127 us (18%)
  matrix products  113 us (16%)
  starting transfers between devices  100 us (14%)
  other arithmetic  68.6 us (10%)
  Pallas kernels  54.7 us (8%)
  between operations  16.4 us (2%)
  blocking collectives  8.09 us (1%)
    dot_general x14, matrix products, matmul(): lax.dot_general(a, b, (((ca,), (cb,)), ((), ())), preferred_element_type=...  113 us
    ppermute x36, starting transfers between devices, line_gather(): moving = lax.ppermute(moving, axis, [(i, i + step_to) for i in sources])  55 us
    ppermute x36, waiting for transfers between devices, line_gather(): moving = lax.ppermute(moving, axis, [(i, i + step_to) for i in sources])  51.3 us
    unnamed x200, local copies, waits for them, and re-layouts  48.4 us
    ppermute x6, waiting for transfers between devices, from_partner(): lax.ppermute(array, 'tp', [(i, i ^ distance) for i in range(members)])  34.3 us
    pallas_call x1, Pallas kernels, run_backward(): pl.pallas_call(backward_kernel, grid=(count,), in_specs=[own(0), own(1),...  32.7 us
    ppermute x2, waiting for transfers between devices, exchange(): far = lax.ppermute(joined.astype(bf16), 'ctx', pairs).astype(f32)  29 us
    dynamic_slice x6, local copies, waits for them, and re-layouts, pick(): return lax.dynamic_index_in_dim(value, index, axis, keepdims=False)  21.2 us
  transfers between devices with their start and end apart: 80, of which 35 were waited for; matrix products, arithmetic and copies ran while one was open for 31% of the time, Pallas kernels for 7%

profile of v2, /device:TPU:0, one launch (start us, length us, event | category | flops | bytes accessed | tf_op | source)
XLA Modules:
  0.0 703.6 jit_solution(11525451818270423519)
XLA Ops:
  12.5 5.1 collective-permute-start.8
  18.3 6.6 collective-permute-done.8
  24.9 15.0 %collective-permute-done.7 = bf16[256,512]{0,1:T(8,128)(2,1)S(1)} collective-permute-done((bf16[256,512]{0,1:T(8,128)(2,1)S(1)}, bf16[256,512]{0,1:T(8,128)(2,1)S(1)}, u32[]{:S(2)}, u32[]{:S(2)}) %collective-permute-start.7) | collective-permute-done | bytes 262176 | tf_op jit(solution)/shard_map/ppermute | solution.py:541
  43.4 8.1 %all-gather.1 = s32[4,2,3]{2,1,0:T(2,128)S(1)} all-gather(s32[1,2,3]{2,1,0:T(2,128)S(1)} %add_bitcast_fusion), channel_id=2, replica_groups=mesh['dp'=2,'ctx'=4,'tp'=4] {'ctx'}, dimensions={0}, use_global_device_ids=true | all-gather | bytes 120 | tf_op jit(solution)/shard_map/all_gather | solution.py:564
  59.6 5.4 convert_multiply_fusion.2
  70.2 9.9 %fusion.23 = bf16[768,1536]{1,0:T(8,128)(2,1)S(1)} fusion(bf16[2048,1600]{0,1:T(8,128)(2,1)} %all-gather.8.cloned.1.call-done, f32[768,2048]{1,0:T(8,128)} %convert_multiply_fusion.2, f32[2048]{0:T(1024)S(1)} %copy-done.83), kind=kOutput, calls=%fused_computation.43 | convolution fusion | flops 4836163584 | bytes 14950400 | tf_op jit(solution)/shard_map/dot_general | solution.py:428
  91.1 9.5 %collective-permute-done.1 = bf16[3,64,1024]{2,1,0:T(8,128)(2,1)} collective-permute-done((bf16[3,64,1024]{2,1,0:T(8,128)(2,1)}, bf16[3,64,1024]{2,1,0:T(8,128)(2,1)}, u32[]{:S(2)}, u32[]{:S(2)}) %collective-permute-start.1) | collective-permute-done | bytes 393248 | tf_op jit(solution)/shard_map/ppermute | solution.py:585
  103.5 15.7 %collective-permute-done.2 = bf16[3,64,1024]{2,1,0:T(8,128)(2,1)S(1)} collective-permute-done((bf16[3,64,1024]{2,1,0:T(8,128)(2,1)S(1)}, bf16[3,64,1024]{2,1,0:T(8,128)(2,1)S(1)}, u32[]{:S(2)}, u32[]{:S(2)}) %collective-permute-start.2) | collective-permute-done | bytes 393248 | tf_op jit(solution)/shard_map/ppermute | solution.py:596
  120.6 16.1 %shard_map.255 = (bf16[4,3,64,512]{3,2,1,0:T(8,128)(2,1)S(1)}, f32[768,512]{1,0:T(8,128)S(1)}, f32[64,768]{1,0:T(8,128)S(1)}, f32[64,768]{1,0:T(8,128)S(1)}, f32[3,256,256]{2,1,0:T(8,128)S(1)}) custom-call(bf16[4,3,64,1536]{3,2,1,0:T(8,128)(2,1)S(1)} %bitcast.313, bf16[4,3,64,1536]{3,2,1,0:T(8,128)(2,1)S(1)} %bitcast.314, ...), custom_call_target="tpu_custom_call" | custom-call | flops 3000000000 | bytes 9000000 | tf_op jit(solution)/shard_map/pallas_call | solution.py:353
  144.8 5.0 collective-permute-done.5
  149.7 7.6 %collective-permute-done.4 = bf16[192,512]{1,0:T(8,128)(2,1)S(1)} collective-permute-done((bf16[192,512]{1,0:T(8,128)(2,1)S(1)}, bf16[192,512]{1,0:T(8,128)(2,1)S(1)}, u32[]{:S(2)}, u32[]{:S(2)}) %collective-permute-start.4) | collective-permute-done | bytes 196640 | tf_op jit(solution)/shard_map/ppermute | solution.py:541
  157.4 5.5 multiply_reduce_fusion.4
  168.5 4.6 collective-permute-start.15
  173.1 4.9 copy.138
  179.3 4.7 collective-permute-start.21
  200.9 7.2 %collective-permute-done.19 = bf16[64,2048]{1,0:T(8,128)(2,1)S(1)} collective-permute-done((bf16[64,2048]{1,0:T(8,128)(2,1)S(1)}, bf16[64,2048]{1,0:T(8,128)(2,1)S(1)}, u32[]{:S(2)}, u32[]{:S(2)}) %collective-permute-start.19) | collective-permute-done | bytes 262176 | tf_op jit(solution)/shard_map/ppermute | solution.py:455
  210.0 5.6 collective-permute-done.25
  233.2 13.3 %fusion.3 = f32[768,2816]{0,1:T(8,128)S(1)} fusion(bf16[768,2048]{1,0:T(8,128)(2,1)} %bitcast.54, bf16[2048,4224]{0,1:T(8,128)(2,1)} %all-gather.12.cloned.1.call-done), kind=kOutput, calls=%fused_computation.5 | convolution fusion | flops 8858370048 | bytes 23330816 | tf_op jit(solution)/shard_map/dot_general | solution.py:428
  246.5 9.3 %fusion.20 = (bf16[768,1408]{0,1:T(8,128)(2,1)S(1)}, bf16[768,1408]{0,1:T(8,128)(2,1)S(1)}, bf16[768,1408]{0,1:T(8,128)(2,1)}) fusion(f32[768,2816]{0,1:T(8,128)S(1)} %fusion.3, bf16[768,2048]{1,0:T(8,128)(2,1)S(1)} %bitcast.339, bf16[2048,4224]{0,1:T(8,128)(2,1)} %all-gather.12.cloned.1.call-done), kind=kOutput, calls=%fused_computation.37 | convolution fusion | flops 4445405184 | bytes 24051712 | tf_op jit(solution)/shard_map/dot_general | solution.py:428
  258.1 13.5 %fusion.29 = bf16[768,2048]{1,0:T(8,128)(2,1)} fusion(bf16[2048,4224]{0,1:T(8,128)(2,1)} %all-gather.12.cloned.1.call-done, bf16[768,1408]{0,1:T(8,128)(2,1)S(1)} %get-tuple-element.133, bf16[768,1408]{0,1:T(8,128)(2,1)S(1)} %get-tuple-element.132), kind=kOutput, calls=%fused_computation.45 | convolution fusion | flops 8868593664 | bytes 19005440 | tf_op jit(solution)/shard_map/dot_general | solution.py:428
  272.1 7.5 %convolution_convert_fusion.2 = bf16[1408,2048]{0,1:T(8,128)(2,1)S(1)} fusion(bf16[768,1408]{0,1:T(8,128)(2,1)} %get-tuple-element.45, bf16[768,2048]{1,0:T(8,128)(2,1)} %bitcast.336), kind=kOutput, calls=%fused_computation.10 | convolution fusion | flops 4432068608 | bytes 11075584 | tf_op jit(solution)/shard_map/dot_general | solution.py:428
  282.6 4.6 copy.144
  287.2 12.2 %convolution_convert_fusion = bf16[2048,2816]{1,0:T(8,128)(2,1)S(1)} fusion(bf16[768,2048]{1,0:T(8,128)(2,1)} %bitcast.54, bf16[768,2816]{0,1:T(8,128)(2,1)} %pad_maximum_fusion), kind=kOutput, calls=%fused_computation.2 | convolution fusion | flops 8864137216 | bytes 19005440 | tf_op jit(solution)/shard_map/dot_general | solution.py:428
  306.2 4.6 copy.161
  317.8 9.3 %fusion.26 = bf16[768,2048]{1,0:T(8,128)(2,1)} fusion(bf16[768,1408]{0,1:T(8,128)(2,1)S(1)} %copy-done.92, bf16[2048,4224]{0,1:T(8,128)(2,1)} %all-gather.12.cloned.1.call-done), kind=kOutput, calls=%fused_computation.44 | convolution fusion | flops 4430757888 | bytes 11075584 | tf_op jit(solution)/shard_map/dot_general | solution.py:428
  330.9 5.3 collective-permute-done.53
  339.7 8.2 %collective-permute-done.55 = bf16[2,128,1408]{1,2,0:T(8,128)(2,1)S(1)} collective-permute-done((bf16[2,128,1408]{1,2,0:T(8,128)(2,1)S(1)}, bf16[2,128,1408]{1,2,0:T(8,128)(2,1)S(1)}, u32[]{:S(2)}, u32[]{:S(2)}) %collective-permute-start.55) | collective-permute-done | bytes 720928 | tf_op jit(solution)/shard_map/ppermute | solution.py:521
  349.9 4.8 collective-permute-done.54
  357.8 5.7 fusion
  379.3 4.5 collective-permute-start.33
  385.1 4.6 collective-permute-start.39
  389.7 14.6 %reduce-scatter.6.cloned.1.call-done = bf16[192,2048]{1,0:T(8,128)(2,1)} async-done(((bf16[768,2048]{1,0:T(8,128)(2,1)}), bf16[192,2048]{1,0:T(8,128)(2,1)}) %reduce-scatter.6.cloned.1.call-update) | async-done | bytes 786448 | tf_op jit(solution)/shard_map/reduce_scatter | solution.py:493
  410.1 8.5 %collective-permute-done.31 = bf16[64,2048]{1,0:T(8,128)(2,1)S(1)} collective-permute-done((bf16[64,2048]{1,0:T(8,128)(2,1)S(1)}, bf16[64,2048]{1,0:T(8,128)(2,1)S(1)}, u32[]{:S(2)}, u32[]{:S(2)}) %collective-permute-start.31) | collective-permute-done | bytes 262176 | tf_op jit(solution)/shard_map/ppermute | solution.py:455
  426.5 8.9 %collective-permute-done.32 = bf16[64,2048]{1,0:T(8,128)(2,1)S(1)} collective-permute-done((bf16[64,2048]{1,0:T(8,128)(2,1)S(1)}, bf16[64,2048]{1,0:T(8,128)(2,1)S(1)}, u32[]{:S(2)}, u32[]{:S(2)}) %collective-permute-start.32) | collective-permute-done | bytes 262176 | tf_op jit(solution)/shard_map/ppermute | solution.py:455
  436.2 4.8 collective-permute-done.37
  456.0 5.7 fusion.44
  465.5 32.7 %shard_map.256 = (bf16[4,3,64,512]{3,2,1,0:T(8,128)(2,1)S(1)}, f32[768,512]{1,0:T(8,128)S(1)}, f32[768,512]{1,0:T(8,128)}, f32[64,768]{1,0:T(8,128)S(1)}, f32[64...) custom-call(bf16[4,3,64,1536]{3,2,1,0:T(8,128)(2,1)} %bitcast.316, ...), custom_call_target="tpu_custom_call" | custom-call | flops 8999999488 | bytes 15000000 | tf_op jit(solution)/shard_map/pallas_call | solution.py:380
  514.0 13.2 %collective-permute-done.48 = bf16[3,64,1024]{2,1,0:T(8,128)(2,1)S(1)} collective-permute-done((bf16[3,64,1024]{2,1,0:T(8,128)(2,1)S(1)}, bf16[3,64,1024]{2,1,0:T(8,128)(2,1)S(1)}, u32[]{:S(2)}, u32[]{:S(2)}) %collective-permute-start.48) | collective-permute-done | bytes 393248 | tf_op jit(solution)/shard_map/ppermute | solution.py:596
  551.1 8.0 %fusion.10 = f32[768,2048]{1,0:T(8,128)S(1)} fusion(bf16[2048,1600]{0,1:T(8,128)(2,1)} %all-gather.8.cloned.1.call-done, bf16[768,512]{1,0:T(8,128)(2,1)} %bitcast.325, bf16[768,512]{1,0:T(8,128)(2,1)} %bitcast.323, bf16[768,512]{1,0:T(8,128)(2,1)} %bitcast.321), kind=kOutput, calls=%fused_computation.24 | convolution fusion | flops 4838916096 | bytes 14942208 | tf_op jit(solution)/shard_map/dot_general | solution.py:428
  573.9 8.2 %convolution_convert_fusion.1 = bf16[2048,1600]{1,0:T(8,128)(2,1)S(1)} fusion(bf16[768,1600]{1,0:T(8,128)(2,1)S(1)} %pad_maximum_fusion.1, f32[768,2048]{1,0:T(8,128)} %convert_multiply_fusion.2, f32[2048]{0:T(1024)S(1)} %copy-done.84), kind=kOutput, calls=%fused_computation.9 | convolution fusion | flops 5039587328 | bytes 15310848 | tf_op jit(solution)/shard_map/dot_general | solution.py:428
  585.6 5.5 copy.151
  597.0 4.8 collective-permute-done.70
  610.9 5.8 copy.162
  616.9 4.6 reduce-scatter.8.cloned.1.call-done
  641.7 9.5 %collective-permute-done.63 = bf16[2,128,1600]{1,2,0:T(8,128)(2,1)S(1)} collective-permute-done((bf16[2,128,1600]{1,2,0:T(8,128)(2,1)S(1)}, bf16[2,128,1600]{1,2,0:T(8,128)(2,1)S(1)}, u32[]{:S(2)}, u32[]{:S(2)}) %collective-permute-start.63) | collective-permute-done | bytes 819232 | tf_op jit(solution)/shard_map/ppermute | solution.py:520
  653.0 6.7 collective-permute-done.65
  660.6 6.2 collective-permute-done.64
  672.1 18.6 %all-gather.16.cloned.1.call-done = bf16[768,2048]{1,0:T(8,128)(2,1)} async-done(((bf16[192,2048]{1,0:T(8,128)(2,1)}), bf16[768,2048]{1,0:T(8,128)(2,1)}) %all-gather.16.cloned.1.call-update) | async-done | bytes 3145744 | tf_op jit(solution)/shard_map/all_gather | solution.py:496
  (547 shorter events, 276.9 us)
Async XLA Ops:
  7.2 57.9 %all-gather.8.cloned.1.call-start = ((), (), s32[]{:S(2)}) async-start(), calls=%async_computation.3 | async-start | bytes 7372800 | tf_op jit(solution)/shard_map/all_gather | solution.py:499
  12.4 144.9 %all-gather.10.cloned.1.call-start = ((), (), s32[]{:S(2)}) async-start(), calls=%async_computation.4 | async-start | bytes 9437184 | tf_op jit(solution)/shard_map/all_gather | solution.py:499
  17.6 22.3 %collective-permute-start.7 = (bf16[256,512]{0,1:T(8,128)(2,1)S(1)}, bf16[256,512]{0,1:T(8,128)(2,1)S(1)}, u32[]{:S(2)}, u32[]{:S(2)}) collective-permute-start(bf16[256,512]{0,1:T(8,128)(2,1)S(1)} %bitcast.359), channel_id=1, source_target_pairs={{0,2},{1,3},{2,0},{3,1},{4,6},{5,7},{6,4},{7,5},{8,10},{9,11},{10,... | collective-permute-start | bytes 786440 | tf_op jit(solution)/shard_map/ppermute | solution.py:541
  17.6 22.3 %collective-permute-start.6 = (bf16[256,512]{0,1:T(8,128)(2,1)S(1)}, bf16[256,512]{0,1:T(8,128)(2,1)S(1)}, u32[]{:S(2)}, u32[]{:S(2)}) collective-permute-start(bf16[256,512]{0,1:T(8,128)(2,1)S(1)} %bitcast.360), channel_id=1, source_target_pairs={{0,1},{1,0},{2,3},{3,2},{4,5},{5,4},{6,7},{7,6},{8,9},{9,8},{10,11... | collective-permute-start | bytes 786440 | tf_op jit(solution)/shard_map/ppermute | solution.py:541
  41.0 192.2 %all-gather.12.cloned.1.call-start = ((), (), s32[]{:S(2)}) async-start(), calls=%async_computation.5 | async-start | bytes 19464192 | tf_op jit(solution)/shard_map/all_gather | solution.py:499
  43.2 325.2 %reduce-scatter.4.cloned.1.call-start = ((), (), s32[]{:S(2)}) async-start(), calls=%async_computation.6 | async-start | bytes 3932160 | tf_op jit(solution)/shard_map/reduce_scatter | solution.py:493
  101.9 17.3 %collective-permute-start.2 = (bf16[3,64,1024]{2,1,0:T(8,128)(2,1)S(1)}, bf16[3,64,1024]{2,1,0:T(8,128)(2,1)S(1)}, u32[]{:S(2)}, u32[]{:S(2)}) collective-permute-start(bf16[3,64,1024]{2,1,0:T(8,128)(2,1)S(1)} %fusion.57), channel_id=1, source_target_pairs={{0,8},{4,12},{1,9},{5,13},{2,10},{6,14},{3,11},{7,15},{16,24},{20,... | collective-permute-start | bytes 1179656 | tf_op jit(solution)/shard_map/ppermute | solution.py:596
  165.1 18.9 %collective-permute-start.9 = (bf16[64,2048]{1,0:T(8,128)(2,1)}, bf16[64,2048]{1,0:T(8,128)(2,1)S(1)}, u32[]{:S(2)}, u32[]{:S(2)}) collective-permute-start(bf16[64,2048]{1,0:T(8,128)(2,1)} %get-tuple-element.161), channel_id=1, source_target_pairs={{0,1},{1,2},{2,3},{4,5},{5,6},{6,7},{8,9},{9,10},{10,11},{12,13},{... | collective-permute-start | bytes 786440 | tf_op jit(solution)/shard_map/ppermute | solution.py:455
  167.2 18.2 %collective-permute-start.12 = (bf16[64,2048]{1,0:T(8,128)(2,1)}, bf16[64,2048]{1,0:T(8,128)(2,1)S(1)}, u32[]{:S(2)}, u32[]{:S(2)}) collective-permute-start(bf16[64,2048]{1,0:T(8,128)(2,1)} %get-tuple-element.161), channel_id=1, source_target_pairs={{1,0},{2,1},{3,2},{5,4},{6,5},{7,6},{9,8},{10,9},{11,10},{13,12},{... | collective-permute-start | bytes 786440 | tf_op jit(solution)/shard_map/ppermute | solution.py:455
  168.5 17.6 %collective-permute-start.15 = (bf16[64,2048]{1,0:T(8,128)(2,1)}, bf16[64,2048]{1,0:T(8,128)(2,1)S(1)}, u32[]{:S(2)}, u32[]{:S(2)}) collective-permute-start(bf16[64,2048]{1,0:T(8,128)(2,1)} %get-tuple-element.160), channel_id=1, source_target_pairs={{0,1},{1,2},{2,3},{4,5},{5,6},{6,7},{8,9},{9,10},{10,11},{12,13},{... | collective-permute-start | bytes 786440 | tf_op jit(solution)/shard_map/ppermute | solution.py:455
  190.9 17.1 %collective-permute-start.19 = (bf16[64,2048]{1,0:T(8,128)(2,1)S(1)}, bf16[64,2048]{1,0:T(8,128)(2,1)S(1)}, u32[]{:S(2)}, u32[]{:S(2)}) collective-permute-start(bf16[64,2048]{1,0:T(8,128)(2,1)S(1)} %collective-permute-done.18), channel_id=1, source_target_pairs={{1,0},{2,1},{5,4},{6,5},{9,8},{10,9},{13,12},{14,13},{17,16},{18,1... | collective-permute-start | bytes 786440 | tf_op jit(solution)/shard_map/ppermute | solution.py:455
  193.0 15.7 %collective-permute-start.22 = (bf16[64,2048]{1,0:T(8,128)(2,1)S(1)}, bf16[64,2048]{1,0:T(8,128)(2,1)S(1)}, u32[]{:S(2)}, u32[]{:S(2)}) collective-permute-start(bf16[64,2048]{1,0:T(8,128)(2,1)S(1)} %collective-permute-done.21), channel_id=1, source_target_pairs={{1,2},{2,3},{5,6},{6,7},{9,10},{10,11},{13,14},{14,15},{17,18},{18... | collective-permute-start | bytes 786440 | tf_op jit(solution)/shard_map/ppermute | solution.py:455
  193.7 21.9 %collective-permute-start.25 = (bf16[64,2048]{1,0:T(8,128)(2,1)S(1)}, bf16[64,2048]{1,0:T(8,128)(2,1)S(1)}, u32[]{:S(2)}, u32[]{:S(2)}) collective-permute-start(bf16[64,2048]{1,0:T(8,128)(2,1)S(1)} %collective-permute-done.24), channel_id=1, source_target_pairs={{1,0},{2,1},{5,4},{6,5},{9,8},{10,9},{13,12},{14,13},{17,16},{18,1... | collective-permute-start | bytes 786440 | tf_op jit(solution)/shard_map/ppermute | solution.py:455
  198.2 18.1 %collective-permute-start.11 = (bf16[64,2048]{1,0:T(8,128)(2,1)S(1)}, bf16[64,2048]{1,0:T(8,128)(2,1)S(1)}, u32[]{:S(2)}, u32[]{:S(2)}) collective-permute-start(bf16[64,2048]{1,0:T(8,128)(2,1)S(1)} %collective-permute-done.10), channel_id=1, source_target_pairs={{2,3},{6,7},{10,11},{14,15},{18,19},{22,23},{26,27},{30,31}} | collective-permute-start | bytes 786440 | tf_op jit(solution)/shard_map/ppermute | solution.py:455
  199.6 21.6 %collective-permute-start.14 = (bf16[64,2048]{1,0:T(8,128)(2,1)S(1)}, bf16[64,2048]{1,0:T(8,128)(2,1)S(1)}, u32[]{:S(2)}, u32[]{:S(2)}) collective-permute-start(bf16[64,2048]{1,0:T(8,128)(2,1)S(1)} %collective-permute-done.13), channel_id=1, source_target_pairs={{1,0},{5,4},{9,8},{13,12},{17,16},{21,20},{25,24},{29,28}} | collective-permute-start | bytes 786440 | tf_op jit(solution)/shard_map/ppermute | solution.py:455
  208.0 16.1 %collective-permute-start.17 = (bf16[64,2048]{1,0:T(8,128)(2,1)S(1)}, bf16[64,2048]{1,0:T(8,128)(2,1)S(1)}, u32[]{:S(2)}, u32[]{:S(2)}) collective-permute-start(bf16[64,2048]{1,0:T(8,128)(2,1)S(1)} %collective-permute-done.16), channel_id=1, source_target_pairs={{2,3},{6,7},{10,11},{14,15},{18,19},{22,23},{26,27},{30,31}} | collective-permute-start | bytes 786440 | tf_op jit(solution)/shard_map/ppermute | solution.py:455
  208.7 17.8 %collective-permute-start.20 = (bf16[64,2048]{1,0:T(8,128)(2,1)S(1)}, bf16[64,2048]{1,0:T(8,128)(2,1)S(1)}, u32[]{:S(2)}, u32[]{:S(2)}) collective-permute-start(bf16[64,2048]{1,0:T(8,128)(2,1)S(1)} %collective-permute-done.19), channel_id=1, source_target_pairs={{1,0},{5,4},{9,8},{13,12},{17,16},{21,20},{25,24},{29,28}} | collective-permute-start | bytes 786440 | tf_op jit(solution)/shard_map/ppermute | solution.py:455
  216.3 15.4 %collective-permute-start.26 = (bf16[64,2048]{1,0:T(8,128)(2,1)S(1)}, bf16[64,2048]{1,0:T(8,128)(2,1)S(1)}, u32[]{:S(2)}, u32[]{:S(2)}) collective-permute-start(bf16[64,2048]{1,0:T(8,128)(2,1)S(1)} %collective-permute-done.25), channel_id=1, source_target_pairs={{1,0},{5,4},{9,8},{13,12},{17,16},{21,20},{25,24},{29,28}} | collective-permute-start | bytes 786440 | tf_op jit(solution)/shard_map/ppermute | solution.py:455
  271.6 132.6 %reduce-scatter.6.cloned.1.call-start = ((), (), s32[]{:S(2)}) async-start(), calls=%async_computation.7 | async-start | bytes 3932160 | tf_op jit(solution)/shard_map/reduce_scatter | solution.py:493
  287.2 23.6 %collective-permute-start.46 = (bf16[2,2,256,1408]{2,3,1,0:T(8,128)(2,1)}, bf16[2,2,256,1408]{2,3,1,0:T(8,128)(2,1)}, u32[]{:S(2)}, u32[]{:S(2)}) collective-permute-start(bf16[2,2,256,1408]{2,3,1,0:T(8,128)(2,1)} %bitcast.349), channel_id=1, source_target_pairs={{0,16},{16,0},{1,17},{17,1},{2,18},{18,2},{3,19},{19,3},{4,20},{20... | collective-permute-start | bytes 8650760 | tf_op jit(solution)/shard_map/ppermute | solution.py:518
  305.5 52.4 %collective-permute-start.45 = (bf16[2,2,256,2816]{3,2,1,0:T(8,128)(2,1)}, bf16[2,2,256,2816]{3,2,1,0:T(8,128)(2,1)}, u32[]{:S(2)}, u32[]{:S(2)}) collective-permute-start(bf16[2,2,256,2816]{3,2,1,0:T(8,128)(2,1)} %dynamic-slice_bitcast_fusion), channel_id=1, source_target_pairs={{0,16},{16,0},{1,17},{17,1},{2,18},{18,2},{3,19},{19,3},{4,20},{20... | collective-permute-start | bytes 17301512 | tf_op jit(solution)/shard_map/ppermute | solution.py:518
  317.8 18.4 %collective-permute-start.53 = (bf16[2,128,1408]{1,2,0:T(8,128)(2,1)}, bf16[2,128,1408]{1,2,0:T(8,128)(2,1)}, u32[]{:S(2)}, u32[]{:S(2)}) collective-permute-start(bf16[2,128,1408]{1,2,0:T(8,128)(2,1)} %dynamic-slice_bitcast_fusion.6), channel_id=1, source_target_pairs={{0,4},{4,0},{8,12},{12,8},{1,5},{5,1},{9,13},{13,9},{2,6},{6,2},{1... | collective-permute-start | bytes 2162696 | tf_op jit(solution)/shard_map/ppermute | solution.py:520
  327.1 203.8 %all-gather.14.cloned.1.call-start = ((), (), s32[]{:S(2)}) async-start(), calls=%async_computation.8 | async-start | bytes 3932160 | tf_op jit(solution)/shard_map/all_gather | solution.py:496
  328.5 19.5 %collective-permute-start.55 = (bf16[2,128,1408]{1,2,0:T(8,128)(2,1)S(1)}, bf16[2,128,1408]{1,2,0:T(8,128)(2,1)S(1)}, u32[]{:S(2)}, u32[]{:S(2)}) collective-permute-start(bf16[2,128,1408]{1,2,0:T(8,128)(2,1)S(1)} %dynamic-slice_bitcast_fusion.5), channel_id=1, source_target_pairs={{0,8},{8,0},{4,12},{12,4},{1,9},{9,1},{5,13},{13,5},{2,10},{10,2},... | collective-permute-start | bytes 2162696 | tf_op jit(solution)/shard_map/ppermute | solution.py:521
  337.7 17.0 %collective-permute-start.54 = (bf16[128,1408]{0,1:T(8,128)(2,1)S(1)}, bf16[128,1408]{0,1:T(8,128)(2,1)S(1)}, u32[]{:S(2)}, u32[]{:S(2)}) collective-permute-start(bf16[128,1408]{0,1:T(8,128)(2,1)S(1)} %dynamic-slice_bitcast_fusion.12), channel_id=1, source_target_pairs={{0,8},{8,0},{4,12},{12,4},{1,9},{9,1},{5,13},{13,5},{2,10},{10,2},... | collective-permute-start | bytes 1081352 | tf_op jit(solution)/shard_map/ppermute | solution.py:524
  373.7 31.8 %collective-permute-start.27 = (bf16[64,2048]{1,0:T(8,128)(2,1)}, bf16[64,2048]{1,0:T(8,128)(2,1)S(1)}, u32[]{:S(2)}, u32[]{:S(2)}) collective-permute-start(bf16[64,2048]{1,0:T(8,128)(2,1)} %get-tuple-element.158), channel_id=1, source_target_pairs={{0,1},{1,2},{2,3},{4,5},{5,6},{6,7},{8,9},{9,10},{10,11},{12,13},{... | collective-permute-start | bytes 786440 | tf_op jit(solution)/shard_map/ppermute | solution.py:455
  376.7 29.6 %collective-permute-start.30 = (bf16[64,2048]{1,0:T(8,128)(2,1)}, bf16[64,2048]{1,0:T(8,128)(2,1)S(1)}, u32[]{:S(2)}, u32[]{:S(2)}) collective-permute-start(bf16[64,2048]{1,0:T(8,128)(2,1)} %get-tuple-element.158), channel_id=1, source_target_pairs={{1,0},{2,1},{3,2},{5,4},{6,5},{7,6},{9,8},{10,9},{11,10},{13,12},{... | collective-permute-start | bytes 786440 | tf_op jit(solution)/shard_map/ppermute | solution.py:455
  379.3 29.6 %collective-permute-start.33 = (bf16[64,2048]{1,0:T(8,128)(2,1)}, bf16[64,2048]{1,0:T(8,128)(2,1)S(1)}, u32[]{:S(2)}, u32[]{:S(2)}) collective-permute-start(bf16[64,2048]{1,0:T(8,128)(2,1)} %get-tuple-element.157), channel_id=1, source_target_pairs={{0,1},{1,2},{2,3},{4,5},{5,6},{6,7},{8,9},{9,10},{10,11},{12,13},{... | collective-permute-start | bytes 786440 | tf_op jit(solution)/shard_map/ppermute | solution.py:455
  383.8 36.9 %collective-permute-start.36 = (bf16[64,2048]{1,0:T(8,128)(2,1)}, bf16[64,2048]{1,0:T(8,128)(2,1)S(1)}, u32[]{:S(2)}, u32[]{:S(2)}) collective-permute-start(bf16[64,2048]{1,0:T(8,128)(2,1)} %get-tuple-element.157), channel_id=1, source_target_pairs={{1,0},{2,1},{3,2},{5,4},{6,5},{7,6},{9,8},{10,9},{11,10},{13,12},{... | collective-permute-start | bytes 786440 | tf_op jit(solution)/shard_map/ppermute | solution.py:455
  385.1 37.1 %collective-permute-start.39 = (bf16[64,2048]{1,0:T(8,128)(2,1)}, bf16[64,2048]{1,0:T(8,128)(2,1)S(1)}, u32[]{:S(2)}, u32[]{:S(2)}) collective-permute-start(bf16[64,2048]{1,0:T(8,128)(2,1)} %get-tuple-element.156), channel_id=1, source_target_pairs={{0,1},{1,2},{2,3},{4,5},{5,6},{6,7},{8,9},{9,10},{10,11},{12,13},{... | collective-permute-start | bytes 786440 | tf_op jit(solution)/shard_map/ppermute | solution.py:455
  408.8 15.7 %collective-permute-start.42 = (bf16[64,2048]{1,0:T(8,128)(2,1)}, bf16[64,2048]{1,0:T(8,128)(2,1)S(1)}, u32[]{:S(2)}, u32[]{:S(2)}) collective-permute-start(bf16[64,2048]{1,0:T(8,128)(2,1)} %get-tuple-element.156), channel_id=1, source_target_pairs={{1,0},{2,1},{3,2},{5,4},{6,5},{7,6},{9,8},{10,9},{11,10},{13,12},{... | collective-permute-start | bytes 786440 | tf_op jit(solution)/shard_map/ppermute | solution.py:455
  419.3 16.1 %collective-permute-start.32 = (bf16[64,2048]{1,0:T(8,128)(2,1)S(1)}, bf16[64,2048]{1,0:T(8,128)(2,1)S(1)}, u32[]{:S(2)}, u32[]{:S(2)}) collective-permute-start(bf16[64,2048]{1,0:T(8,128)(2,1)S(1)} %collective-permute-done.31), channel_id=1, source_target_pairs={{1,0},{5,4},{9,8},{13,12},{17,16},{21,20},{25,24},{29,28}} | collective-permute-start | bytes 786440 | tf_op jit(solution)/shard_map/ppermute | solution.py:455
  420.7 82.2 %collective-permute-start.49 = (bf16[2,128,2816]{2,1,0:T(8,128)(2,1)}, bf16[2,128,2816]{2,1,0:T(8,128)(2,1)}, u32[]{:S(2)}, u32[]{:S(2)}) collective-permute-start(bf16[2,128,2816]{2,1,0:T(8,128)(2,1)} %dynamic-slice_bitcast_fusion.2), channel_id=1, source_target_pairs={{0,4},{4,0},{8,12},{12,8},{1,5},{5,1},{9,13},{13,9},{2,6},{6,2},{1... | collective-permute-start | bytes 4325384 | tf_op jit(solution)/shard_map/ppermute | solution.py:520
  422.2 18.8 %collective-permute-start.37 = (bf16[64,2048]{1,0:T(8,128)(2,1)S(1)}, bf16[64,2048]{1,0:T(8,128)(2,1)S(1)}, u32[]{:S(2)}, u32[]{:S(2)}) collective-permute-start(bf16[64,2048]{1,0:T(8,128)(2,1)S(1)} %collective-permute-done.36), channel_id=1, source_target_pairs={{1,0},{2,1},{5,4},{6,5},{9,8},{10,9},{13,12},{14,13},{17,16},{18,1... | collective-permute-start | bytes 786440 | tf_op jit(solution)/shard_map/ppermute | solution.py:455
  424.5 17.9 %collective-permute-start.40 = (bf16[64,2048]{1,0:T(8,128)(2,1)S(1)}, bf16[64,2048]{1,0:T(8,128)(2,1)S(1)}, u32[]{:S(2)}, u32[]{:S(2)}) collective-permute-start(bf16[64,2048]{1,0:T(8,128)(2,1)S(1)} %collective-permute-done.39), channel_id=1, source_target_pairs={{1,2},{2,3},{5,6},{6,7},{9,10},{10,11},{13,14},{14,15},{17,18},{18... | collective-permute-start | bytes 786440 | tf_op jit(solution)/shard_map/ppermute | solution.py:455
  425.2 21.5 %collective-permute-start.43 = (bf16[64,2048]{1,0:T(8,128)(2,1)S(1)}, bf16[64,2048]{1,0:T(8,128)(2,1)S(1)}, u32[]{:S(2)}, u32[]{:S(2)}) collective-permute-start(bf16[64,2048]{1,0:T(8,128)(2,1)S(1)} %collective-permute-done.42), channel_id=1, source_target_pairs={{1,0},{2,1},{5,4},{6,5},{9,8},{10,9},{13,12},{14,13},{17,16},{18,1... | collective-permute-start | bytes 786440 | tf_op jit(solution)/shard_map/ppermute | solution.py:455
  441.0 70.2 %collective-permute-start.51 = (bf16[2,128,2816]{2,1,0:T(8,128)(2,1)}, bf16[2,128,2816]{2,1,0:T(8,128)(2,1)}, u32[]{:S(2)}, u32[]{:S(2)}) collective-permute-start(bf16[2,128,2816]{2,1,0:T(8,128)(2,1)} %dynamic-slice_bitcast_fusion.1), channel_id=1, source_target_pairs={{0,8},{8,0},{4,12},{12,4},{1,9},{9,1},{5,13},{13,5},{2,10},{10,2},... | collective-permute-start | bytes 4325384 | tf_op jit(solution)/shard_map/ppermute | solution.py:521
  463.0 158.5 %reduce-scatter.8.cloned.1.call-start = ((), (), s32[]{:S(2)}) async-start(), calls=%async_computation.9 | async-start | bytes 3932160 | tf_op jit(solution)/shard_map/reduce_scatter | solution.py:493
  504.6 23.8 %collective-permute-start.50 = (bf16[128,2816]{1,0:T(8,128)(2,1)S(1)}, bf16[128,2816]{1,0:T(8,128)(2,1)S(1)}, u32[]{:S(2)}, u32[]{:S(2)}) collective-permute-start(bf16[128,2816]{1,0:T(8,128)(2,1)S(1)} %dynamic-slice_bitcast_fusion.8), channel_id=1, source_target_pairs={{0,8},{8,0},{4,12},{12,4},{1,9},{9,1},{5,13},{13,5},{2,10},{10,2},... | collective-permute-start | bytes 2162696 | tf_op jit(solution)/shard_map/ppermute | solution.py:524
  510.0 17.3 %collective-permute-start.48 = (bf16[3,64,1024]{2,1,0:T(8,128)(2,1)S(1)}, bf16[3,64,1024]{2,1,0:T(8,128)(2,1)S(1)}, u32[]{:S(2)}, u32[]{:S(2)}) collective-permute-start(bf16[3,64,1024]{2,1,0:T(8,128)(2,1)S(1)} %fusion.61), channel_id=1, source_target_pairs={{8,0},{12,4},{9,1},{13,5},{10,2},{14,6},{11,3},{15,7},{24,16},{28,... | collective-permute-start | bytes 1179656 | tf_op jit(solution)/shard_map/ppermute | solution.py:596
  513.1 16.6 %collective-permute-start.52 = (bf16[128,2816]{1,0:T(8,128)(2,1)S(1)}, bf16[128,2816]{1,0:T(8,128)(2,1)S(1)}, u32[]{:S(2)}, u32[]{:S(2)}) collective-permute-start(bf16[128,2816]{1,0:T(8,128)(2,1)S(1)} %dynamic-slice_bitcast_fusion.7), channel_id=1, source_target_pairs={{0,4},{4,0},{8,12},{12,8},{1,5},{5,1},{9,13},{13,9},{2,6},{6,2},{1... | collective-permute-start | bytes 2162696 | tf_op jit(solution)/shard_map/ppermute | solution.py:525
  563.3 127.4 %all-gather.16.cloned.1.call-start = ((), (), s32[]{:S(2)}) async-start(), calls=%async_computation.10 | async-start | bytes 3932160 | tf_op jit(solution)/shard_map/all_gather | solution.py:496
  570.4 21.1 %collective-permute-start.67 = (bf16[2,2,256,512]{2,3,1,0:T(8,128)(2,1)}, bf16[2,2,256,512]{2,3,1,0:T(8,128)(2,1)}, u32[]{:S(2)}, u32[]{:S(2)}) collective-permute-start(bf16[2,2,256,512]{2,3,1,0:T(8,128)(2,1)} %bitcast.352), channel_id=1, source_target_pairs={{0,16},{16,0},{1,17},{17,1},{2,18},{18,2},{3,19},{19,3},{4,20},{20... | collective-permute-start | bytes 3145736 | tf_op jit(solution)/shard_map/ppermute | solution.py:518
  591.1 35.9 %collective-permute-start.62 = (bf16[2,2,256,1600]{2,3,1,0:T(8,128)(2,1)}, bf16[2,2,256,1600]{2,3,1,0:T(8,128)(2,1)}, u32[]{:S(2)}, u32[]{:S(2)}) collective-permute-start(bf16[2,2,256,1600]{2,3,1,0:T(8,128)(2,1)} %bitcast.343), channel_id=1, source_target_pairs={{0,16},{16,0},{1,17},{17,1},{2,18},{18,2},{3,19},{19,3},{4,20},{20... | collective-permute-start | bytes 9830408 | tf_op jit(solution)/shard_map/ppermute | solution.py:518
  606.3 26.6 %collective-permute-start.69 = (bf16[128,512]{0,1:T(8,128)(2,1)S(1)}, bf16[128,512]{0,1:T(8,128)(2,1)S(1)}, u32[]{:S(2)}, u32[]{:S(2)}) collective-permute-start(bf16[128,512]{0,1:T(8,128)(2,1)S(1)} %dynamic-slice_bitcast_fusion.20), channel_id=1, source_target_pairs={{0,8},{8,0},{4,12},{12,4},{1,9},{9,1},{5,13},{13,5},{2,10},{10,2},... | collective-permute-start | bytes 393224 | tf_op jit(solution)/shard_map/ppermute | solution.py:524
  616.8 16.2 %collective-permute-start.60 = (f32[4864]{0:T(1024)S(1)}, f32[4864]{0:T(1024)S(1)}, u32[]{:S(2)}, u32[]{:S(2)}) collective-permute-start(f32[4864]{0:T(1024)S(1)} %add.426), channel_id=1, source_target_pairs={{0,1},{1,0},{2,3},{3,2},{4,5},{5,4},{6,7},{7,6},{8,9},{9,8},{10,11... | collective-permute-start | bytes 58376 | tf_op jit(solution)/shard_map/ppermute | solution.py:549
  631.3 19.9 %collective-permute-start.63 = (bf16[2,128,1600]{1,2,0:T(8,128)(2,1)S(1)}, bf16[2,128,1600]{1,2,0:T(8,128)(2,1)S(1)}, u32[]{:S(2)}, u32[]{:S(2)}) collective-permute-start(bf16[2,128,1600]{1,2,0:T(8,128)(2,1)S(1)} %dynamic-slice_bitcast_fusion.4), channel_id=1, source_target_pairs={{0,4},{4,0},{8,12},{12,8},{1,5},{5,1},{9,13},{13,9},{2,6},{6,2},{1... | collective-permute-start | bytes 2457608 | tf_op jit(solution)/shard_map/ppermute | solution.py:520
  638.5 21.2 %collective-permute-start.65 = (bf16[2,128,1600]{1,2,0:T(8,128)(2,1)S(1)}, bf16[2,128,1600]{1,2,0:T(8,128)(2,1)S(1)}, u32[]{:S(2)}, u32[]{:S(2)}) collective-permute-start(bf16[2,128,1600]{1,2,0:T(8,128)(2,1)S(1)} %dynamic-slice_bitcast_fusion.3), channel_id=1, source_target_pairs={{0,8},{8,0},{4,12},{12,4},{1,9},{9,1},{5,13},{13,5},{2,10},{10,2},... | collective-permute-start | bytes 2457608 | tf_op jit(solution)/shard_map/ppermute | solution.py:521
  (125 other events, 1527.1 us)
Sparse Core Ops, SparseCore 0:
  12.5 50.5 all-gather.7
  65.6 58.9 all-gather.9
  126.4 101.2 all-gather.11
  271.7 58.8 reduce-scatter.3
  332.8 71.3 reduce-scatter.5
  463.1 61.4 all-gather.13
  563.4 57.9 reduce-scatter.7
  627.1 63.5 all-gather.15

commit v3 on v2

--- a/solution.py
+++ b/solution.py
@@ -84,6 +84,11 @@
 
 def store_rows(ref, value):
     ref[...] = value.reshape(ref.shape)
+
+
+def store_state(ref, key_part, value_part):
+    ref[0, :, :HEAD_DIM] = key_part.astype(ref.dtype)
+    ref[0, :, HEAD_DIM:] = value_part.astype(ref.dtype)
 
 
 def aux_rows(tokens):
@@ -120,7 +125,7 @@
     return jnp.concatenate([bias, keeps, pad], axis=1)
 
 
-def state_kernel(k_ref, v_ref, ld_ref, one_ref, aux_ref, lev_ref, ks_ref, vs_ref):
+def state_kernel(k_ref, v_ref, ld_ref, one_ref, aux_ref, lev_ref, st_ref, low_ref, end_ref):
     tokens = ld_ref.shape[1]
     base, _ = aux_rows(tokens)
     earlier = lax.broadcasted_iota(jnp.int32, (tokens, tokens), 0)
@@ -134,8 +139,10 @@
     lev_ref[...] = levels
     tail = jnp.exp(levels[:, tokens - 1 : tokens] - levels + aux_ref[0, base + 2 : base + 3, :])
     tail = split2(tail * one_ref[...])
-    ks_ref[0] = dot2(tail, rows_of(k_ref), 1, 0)
-    vs_ref[0] = dot2(tail, rows_of(v_ref), 1, 0)
+    state_k, state_v = dot2(tail, rows_of(k_ref), 1, 0), dot2(tail, rows_of(v_ref), 1, 0)
+    store_state(st_ref, state_k, state_v)
+    store_state(low_ref, state_k, state_v)
+    end_ref[0] = jnp.broadcast_to(levels[:, tokens - 1 : tokens], (SLOTS, 128))
 
 
 def forward_kernel(
@@ -157,7 +164,7 @@
         w_scr[j] = w
         return scores + w * d_scr[pl.ds(j, 1), :]
 
-    scores = lax.fori_loop(0, CHUNK, inside, jnp.zeros_like(levels), unroll=2)
+    scores = lax.fori_loop(0, CHUNK, inside, jnp.zeros_like(levels), unroll=4)
     decay = jnp.exp(levels - level_refs(levels) + aux_ref[0, base : base + 1, :])
     for c in range(1, chunks):
         w = levels[:, c * CHUNK - 1 : c * CHUNK] - levels + aux_ref[0, 2 * CHUNK + c : 2 * CHUNK + c + 1, :]
@@ -178,7 +185,7 @@
         d_scr[pl.ds(j, 1), :] = jnp.sum(w_scr[j] * probs, axis=0, keepdims=True)
         return carry
 
-    lax.fori_loop(0, CHUNK, mixing, 0, unroll=2)
+    lax.fori_loop(0, CHUNK, mixing, 0, unroll=4)
     row = lax.broadcasted_iota(jnp.int32, (tokens, tokens), 0) // CHUNK
     col = lax.broadcasted_iota(jnp.int32, (tokens, tokens), 1) // CHUNK
     mixed_t = jnp.where(row == col, jnp.concatenate([d_scr[...]] * chunks, axis=0), 0.0)
@@ -192,14 +199,14 @@
 
 def backward_kernel(
     q_ref, k_ref, v_ref, lev_ref, one_ref, aux_ref, ki_ref, vi_ref, gain_ref, mix_ref, p_ref, sc_ref, mt_ref, go_ref,
-    gq_ref, gk_ref, gv_ref, r_ref, a_ref, dk_ref, dv_ref, hg_ref, w_scr, d_scr, e_scr, x_scr, wh_scr, wl_scr,
+    gq_ref, gk_ref, gv_ref, r_ref, a_ref, d_ref, low_ref, hg_ref, w_scr, d_scr, e_scr, x_scr, wh_scr, wl_scr,
 ):
     tokens = lev_ref.shape[1]
     chunks = tokens // CHUNK
     base, _ = aux_rows(tokens)
     levels, one, probs = lev_ref[...], one_ref[...], p_ref[...]
     q, k, v = rows_of(q_ref), rows_of(k_ref), rows_of(v_ref)
-    out, go = mix_ref[...], rows_of(go_ref)
+    out, go = mix_ref[...], rows_of(go_ref).astype(f32)
     factor = lax.rsqrt(jnp.mean(out * out, axis=1, keepdims=True) + epsilon)
     unit = out * factor
     hg_ref[0] = jnp.sum(go * unit, axis=0, keepdims=True)
@@ -216,7 +223,7 @@
         w_scr[j] = w
         return dp + w * d_scr[pl.ds(j, 1), :]
 
-    dp = lax.fori_loop(0, CHUNK, inside, jnp.zeros_like(levels), unroll=2)
+    dp = lax.fori_loop(0, CHUNK, inside, jnp.zeros_like(levels), unroll=4)
     decay = jnp.exp(levels - level_refs(levels) + aux_ref[0, base : base + 1, :])
     for c in range(1, chunks):
         w = levels[:, c * CHUNK - 1 : c * CHUNK] - levels + aux_ref[0, 2 * CHUNK + c : 2 * CHUNK + c + 1, :]
@@ -236,7 +243,7 @@
         d_scr[pl.ds(j, 1), :] = jnp.sum(w_scr[j] * dz, axis=0, keepdims=True)
         return carry
 
-    lax.fori_loop(0, CHUNK, mixing, 0, unroll=2)
+    lax.fori_loop(0, CHUNK, mixing, 0, unroll=4)
     row = lax.broadcasted_iota(jnp.int32, (tokens, tokens), 0) // CHUNK
     col = lax.broadcasted_iota(jnp.int32, (tokens, tokens), 1) // CHUNK
     mz_t = jnp.where(row == col, jnp.concatenate([d_scr[...]] * chunks, axis=0), 0.0)
@@ -248,8 +255,9 @@
     store_rows(gq_ref, (dot2(mz, k, 0, 0) + dot3(zc, kin, 0, 0)).astype(bf16))
     gk_ref[...] = dot2(mz, q, 1, 0)
     gv_ref[...] = dot3(split2(mt_ref[0]), g, 1, 0)
-    dk_ref[0] = dot2(zc, q, 1, 0)
-    dv_ref[0] = dot3(pc, g, 1, 0)
+    grad_ks, grad_vs = dot2(zc, q, 1, 0), dot3(pc, g, 1, 0)
+    store_state(d_ref, grad_ks, grad_vs)
+    store_state(low_ref, grad_ks, grad_vs)
     qk = dg(q, k, 1, 1)
     gv_n = dot2(g, v, 1, 1)
     d_scr[...] = pick_rows(qk, CHUNK, chunks)
@@ -260,7 +268,7 @@
         term = group_lane(dz, i) * d_scr[pl.ds(i, 1), :] + group_lane(probs, i) * e_scr[pl.ds(i, 1), :]
         return total + jnp.exp(gap) * term
 
-    total = lax.fori_loop(0, CHUNK, onward, jnp.zeros_like(levels), unroll=2)
+    total = lax.fori_loop(0, CHUNK, onward, jnp.zeros_like(levels), unroll=4)
     cross = dot3(zst, split2(qk), 1, 0) + dot3(pst, split2(gv_n), 1, 0)
     for c in range(1, chunks):
         total += x_scr[(c - 1) * SLOTS : c * SLOTS] * cross[(c - 1) * SLOTS : c * SLOTS]
@@ -304,11 +312,14 @@
     lane = pl.BlockSpec((SLOTS, tokens), lambda i: (0, i))
     _, rows = aux_rows(tokens)
     aux = pl.BlockSpec((1, rows, tokens), lambda i: (i, 0, 0))
-    state = pl.BlockSpec((1, SLOTS, HEAD_DIM), lambda i: (i, 0, 0))
+    state = pl.BlockSpec((1, SLOTS, 2 * HEAD_DIM), lambda i: (i, 0, 0))
+    key_half = pl.BlockSpec((1, SLOTS, HEAD_DIM), lambda i: (i, 0, 0))
+    value_half = pl.BlockSpec((1, SLOTS, HEAD_DIM), lambda i: (i, 0, 1))
+    halves = [key_half, value_half]
     gain = pl.BlockSpec((1, HEAD_DIM), lambda i: (0, 0))
     square = pl.BlockSpec((1, tokens, tokens), lambda i: (i, 0, 0))
     row = pl.BlockSpec((1, 1, HEAD_DIM), lambda i: (i, 0, 0))
-    return own, tok, lane, aux, state, gain, square, row
+    return own, tok, lane, aux, state, halves, gain, square, row
 
 
 def params(mib):
@@ -325,16 +336,17 @@
 
 def run_states(qkv, ld, one, aux):
     count, _, tokens = aux.shape
-    own, tok, lane, auxs, state, _, _, _ = seq_specs(tokens, qkv.shape[0])
+    own, tok, lane, auxs, state, _, _, _, _ = seq_specs(tokens, qkv.shape[0])
     return pl.pallas_call(
         state_kernel,
         grid=(count,),
         in_specs=[own(1), own(2), lane, lane, auxs],
-        out_specs=[lane, state, state],
+        out_specs=[lane, state, state, pl.BlockSpec((1, SLOTS, 128), lambda i: (i, 0, 0))],
         out_shape=[
             shape((SLOTS, count * tokens), f32),
-            shape((count, SLOTS, HEAD_DIM), f32),
-            shape((count, SLOTS, HEAD_DIM), f32),
+            shape((count, SLOTS, 2 * HEAD_DIM), f32),
+            shape((count, SLOTS, 2 * HEAD_DIM), bf16),
+            shape((count, SLOTS, 128), f32),
         ],
         compiler_params=params(24),
         cost_estimate=cost(count, 100000000, 1500000),
@@ -346,14 +358,14 @@
     return stack
 
 
-def run_forward(qkv, levels, one, aux, key_in, value_in, gain):
+def run_forward(qkv, levels, one, aux, state_in, gain):
     count, _, tokens = aux.shape
-    own, tok, lane, auxs, state, gains, square, _ = seq_specs(tokens, qkv.shape[0])
+    own, tok, lane, auxs, state, halves, gains, square, _ = seq_specs(tokens, qkv.shape[0])
     stack = big_scratch(tokens)
     return pl.pallas_call(
         forward_kernel,
         grid=(count,),
-        in_specs=[own(0), own(1), own(2), lane, lane, auxs, state, state, gains],
+        in_specs=[own(0), own(1), own(2), lane, lane, auxs, *halves, gains],
         out_specs=[own(0), tok, lane, lane, square],
         out_shape=[
             shape(qkv.shape[:3] + (HEAD_DIM,), bf16),
@@ -370,17 +382,17 @@
         ],
         compiler_params=params(40),
         cost_estimate=cost(count, 1000000000, 3000000),
-    )(qkv, qkv, qkv, levels, one, aux, key_in, value_in, gain)
-
-
-def run_backward(qkv, levels, one, aux, key_in, value_in, gain, mixed, probs, scores, mixed_t, grad_o):
+    )(qkv, qkv, qkv, levels, one, aux, state_in, state_in, gain)
+
+
+def run_backward(qkv, levels, one, aux, state_in, gain, mixed, probs, scores, mixed_t, grad_o):
     count, _, tokens = aux.shape
-    own, tok, lane, auxs, state, gains, square, row = seq_specs(tokens, qkv.shape[0])
+    own, tok, lane, auxs, state, halves, gains, square, row = seq_specs(tokens, qkv.shape[0])
     stack = big_scratch(tokens)
     return pl.pallas_call(
         backward_kernel,
         grid=(count,),
-        in_specs=[own(0), own(1), own(2), lane, lane, auxs, state, state, gains, tok, lane, lane, square, own(0)],
+        in_specs=[own(0), own(1), own(2), lane, lane, auxs, *halves, gains, tok, lane, lane, square, own(0)],
         out_specs=[own(0), tok, tok, lane, lane, state, state, row],
         out_shape=[
             shape(qkv.shape[:3] + (HEAD_DIM,), bf16),
@@ -388,8 +400,8 @@
             shape((count * tokens, HEAD_DIM), f32),
             shape((SLOTS, count * tokens), f32),
             shape((SLOTS, count * tokens), f32),
-            shape((count, SLOTS, HEAD_DIM), f32),
-            shape((count, SLOTS, HEAD_DIM), f32),
+            shape((count, SLOTS, 2 * HEAD_DIM), f32),
+            shape((count, SLOTS, 2 * HEAD_DIM), bf16),
             shape((count, 1, HEAD_DIM), f32),
         ],
         scratch_shapes=[
@@ -402,17 +414,17 @@
         ],
         compiler_params=params(48),
         cost_estimate=cost(count, 3000000000, 5000000),
-    )(qkv, qkv, qkv, levels, one, aux, key_in, value_in, gain, mixed, probs, scores, mixed_t, grad_o)
-
-
-def run_finish(qkv, levels, one, sig, aux, sums, key_in, value_in, key_own, value_own, gk, gv, rows, acts, dk, dv):
+    )(qkv, qkv, qkv, levels, one, aux, state_in, state_in, gain, mixed, probs, scores, mixed_t, grad_o)
+
+
+def run_finish(qkv, levels, one, sig, aux, sums, state_in, state_own, gk, gv, rows, acts, grad_later):
     count, _, tokens = aux.shape
-    own, tok, lane, auxs, state, _, square, _ = seq_specs(tokens, qkv.shape[0])
+    own, tok, lane, auxs, state, halves, _, square, _ = seq_specs(tokens, qkv.shape[0])
     return pl.pallas_call(
         finish_kernel,
         grid=(count,),
-        in_specs=[own(1), own(2), lane, lane, lane, auxs, square, state, state, state, state]
-        + [tok, tok, lane, lane, state, state],
+        in_specs=[own(1), own(2), lane, lane, lane, auxs, square, *halves, *halves]
+        + [tok, tok, lane, lane, *halves],
         out_specs=[own(0), own(0), lane],
         out_shape=[
             shape(qkv.shape[:3] + (HEAD_DIM,), bf16),
@@ -421,7 +433,10 @@
         ],
         compiler_params=params(40),
         cost_estimate=cost(count, 300000000, 4000000),
-    )(qkv, qkv, levels, one, sig, aux, sums, key_in, value_in, key_own, value_own, gk, gv, rows, acts, dk, dv)
+    )(
+        qkv, qkv, levels, one, sig, aux, sums, state_in, state_in, state_own, state_own,
+        gk, gv, rows, acts, grad_later, grad_later,
+    )
 
 
 def matmul(a, b, ca=1, cb=0):
@@ -442,21 +457,25 @@
     return with_layout_constraint(array, Layout(major_to_minor=tuple(range(array.ndim))))
 
 
-def after(values, *events):
-    return lax.optimization_barrier((values, events))[0]
-
-
-def line_gather(own, axis, put, buffer):
+def tie(*values):
+    return lax.optimization_barrier(values)
+
+
+def line_gather(parts, axis, buffer):
     size, here = lax.axis_size(axis), lax.axis_index(axis)
-    for step_to in (1, -1):
-        moving = own
-        for s in range(1, size):
-            sources = range(s - 1, size - 1) if step_to == 1 else range(1, size - s + 1)
-            moving = lax.ppermute(moving, axis, [(i, i + step_to) for i in sources])
-            origin = here - s * step_to
-            valid = (origin >= 0) & (origin < size)
-            buffer = put(buffer, moving, jnp.where(valid, origin, here))
-    return put(buffer, own, here)
+    count = parts.shape[0]
+    moving = {to: [parts[c] for c in range(count)] for to in (1, -1)}
+    for s in range(1, size):
+        for c in range(count):
+            for to in (1, -1):
+                sources = range(s - 1, size - 1) if to == 1 else range(1, size - s + 1)
+                value = lax.ppermute(moving[to][c], axis, [(i, i + to) for i in sources])
+                moving[to][c] = value
+                origin = here - s * to
+                valid = (origin >= 0) & (origin < size)
+                at = (jnp.where(valid, origin, here), c) + (0,) * (parts.ndim - 1)
+                buffer = lax.dynamic_update_slice(buffer, value[None, None], at)
+    return lax.dynamic_update_slice(buffer, parts[None], (here,) + (0,) * parts.ndim)
 
 
 def per_device(
@@ -490,7 +509,7 @@
         return lax.dynamic_slice_in_dim(array, tp_place * (count * part), count * part, 0)
 
     def to_shards(array):
-        return lax.psum_scatter(array, "tp", scatter_dimension=0, tiled=True).astype(f32)
+        return lax.psum_scatter(array, "tp", scatter_dimension=0, tiled=True)
 
     def from_shards(array):
         return lax.all_gather(array.astype(bf16), "tp", axis=0, tiled=True)
@@ -498,56 +517,61 @@
     def gather_rows(array):
         return lax.all_gather(array, ("dp", "ctx"), axis=0, tiled=True)
 
-    def scatter_rows(array, wait=None):
+    core, y, x_at = lax.axis_index("dp"), here // 2, here % 2
+    swap_y = [(0, 2), (2, 0), (1, 3), (3, 1)]
+
+    def pick(value, index, axis):
+        return lax.dynamic_index_in_dim(value, index, axis, keepdims=False)
+
+    def add(a, b, dtype=bf16):
+        return row_major((a.astype(f32) + b.astype(f32)).astype(dtype))
+
+    def scatter_cores(array):
+        if places != 4:
+            return (array,)
+        array = row_major(array).reshape(2, 2, 2, array.shape[0] // 8, array.shape[1])
+        other = lax.ppermute(pick(array, 1 - core, 0), "dp", [(0, 1), (1, 0)])
+        return pick(array, core, 0), other
+
+    def scatter_first(held):
+        if places != 4:
+            return held
+        chip = add(*held)
+        half = chip.shape[2] // 2
+        upper, lower = chip[:, :, :half], chip[:, :, half:]
+        return (
+            pick(upper, x_at, 1),
+            pick(lower, y, 0),
+            lax.ppermute(pick(upper, 1 - x_at, 1), "ctx", swap_x),
+            lax.ppermute(pick(lower, 1 - y, 0), "ctx", swap_y),
+        )
+
+    def scatter_second(held):
+        if places != 4:
+            return held
+        upper, lower, over_x, over_y = held
+        upper, lower = add(upper, over_x), add(lower, over_y)
+        return (
+            pick(upper, y, 0),
+            pick(lower, x_at, 0),
+            lax.ppermute(pick(upper, 1 - y, 0), "ctx", swap_y),
+            lax.ppermute(pick(lower, 1 - x_at, 0), "ctx", swap_x),
+        )
+
+    def scatter_end(held):
         if places != 4:
             return lax.psum_scatter(
-                array, ("dp", "ctx"), scatter_dimension=0, tiled=True
-            ).astype(f32), ()
-        core, y, x = lax.axis_index("dp"), here // 2, here % 2
-        size, cols = array.shape[0] // 8, array.shape[1]
-        half = size // 2
-
-        def pick(value, index, axis):
-            return lax.dynamic_index_in_dim(value, index, axis, keepdims=False)
-
-        def add(a, b, dtype=bf16):
-            return (a.astype(f32) + b.astype(f32)).astype(dtype)
-
-        swap_y = [(0, 2), (2, 0), (1, 3), (3, 1)]
-        array = row_major(array).reshape(2, 2, 2, size, cols)
-        other = lax.ppermute(pick(array, 1 - core, 0), "dp", [(0, 1), (1, 0)])
-        chip = add(pick(array, core, 0), other)
-        over_x = lax.ppermute(pick(chip[:, :, :half], 1 - x, 1), "ctx", swap_x)
-        over_y = lax.ppermute(pick(chip[:, :, half:], 1 - y, 0), "ctx", swap_y)
-        upper = add(pick(chip[:, :, :half], x, 1), over_x)
-        lower = add(pick(chip[:, :, half:], y, 0), over_y)
-        last_y = lax.ppermute(pick(upper, 1 - y, 0), "ctx", swap_y)
-        last_x = lax.ppermute(pick(lower, 1 - x, 0), "ctx", swap_x)
-        upper = add(pick(upper, y, 0), last_y, f32)
-        lower = add(pick(lower, x, 0), last_x, f32)
-        return jnp.concatenate([upper, lower], axis=0), (chip, upper, lower)
+                held[0], ("dp", "ctx"), scatter_dimension=0, tiled=True
+            ).astype(f32)
+        upper, lower, over_y, over_x = held
+        return row_major(jnp.concatenate([add(upper, over_y, f32), add(lower, over_x, f32)], axis=0))
 
     def gather_in_parts(array, parts):
         buffer = jnp.zeros((members, parts, count * part // parts, width), bf16)
-        for c, block in enumerate(array.astype(bf16).reshape(buffer.shape[1:])):
-
-            def put(buf, value, owner, c=c):
-                return lax.dynamic_update_slice(buf, value[None, None], (owner, c, 0, 0))
-
-            buffer = line_gather(block, "tp", put, buffer)
-        return buffer.reshape(rows, width)
+        return line_gather(array.astype(bf16).reshape(buffer.shape[1:]), "tp", buffer).reshape(rows, width)
 
     def from_partner(array, distance):
         return lax.ppermute(array, "tp", [(i, i ^ distance) for i in range(members)])
-
-    def sum_small(array):
-        if places != 4:
-            return lax.psum(array, ("dp", "ctx", "tp"))
-        array += lax.ppermute(array, "dp", [(0, 1), (1, 0)])
-        for axis in ("ctx", "tp"):
-            for r in (1, 2):
-                array += lax.ppermute(array, axis, [(i, i ^ r) for i in range(4)])
-        return array
 
     cut = 3 * heads
     w_in = gather_rows(jnp.concatenate([w_query, w_key, w_value, w_decay], axis=1))
@@ -556,7 +580,6 @@
     w_heads = gather_rows(
         jnp.concatenate([w_out_t] + [from_partner(w_out_t, r) for r in range(1, members)], axis=1)
     )
-    w_o = w_heads[:, :heads]
     w_rest = gather_rows(jnp.concatenate([w_gate, w_up, w_down.T], axis=1))
     w_gu = w_rest[:, : 2 * hidden_units]
     w_d = w_rest[:, 2 * hidden_units :]
@@ -571,48 +594,50 @@
     index = jnp.arange(places)
     reach_in = (index[:, None] < here) & (edges[:, 1] == segments[:, 0])
     reach_out = (index[:, None] > here) & (edges[:, 0] == segments[:, -1])
-    between = (index[None, :] > jnp.minimum(index[:, None], here)) & (
-        index[None, :] < jnp.maximum(index[:, None], here)
-    )
-
-    square = places == 4
-    if square:
-        low = 2 * (here // 2)
-        is_low = here == low
-
-        def exchange(keys, values, coefs, forward, own_end, near_end):
-            own = jnp.concatenate([keys, values], axis=2)
-            near = lax.ppermute(own.astype(bf16), "ctx", swap_x).astype(f32)
-            first, second = jnp.where(is_low, own, near), jnp.where(is_low, near, own)
-            low_end, high_end = jnp.where(is_low, own_end, near_end), jnp.where(is_low, near_end, own_end)
+
+    def flag(array):
+        return array.astype(f32)[:, None, None]
+
+    if places == 4:
+        beside = here ^ 1
+        is_low = x_at == 0
+
+        def level_ends(own_end):
+            return lax.ppermute(own_end, "ctx", swap_x)
+
+        def exchange(own, low, forward, own_end, near_end):
+            row = lax.dynamic_slice_in_dim(edges, 2 * y, 2, 0)
             if forward:
-                link = lax.dynamic_index_in_dim(edges, low, 0, False)[1] == lax.dynamic_index_in_dim(edges, low + 1, 0, False)[1]
-                joined = second + jnp.where(link[:, None], jnp.exp(high_end), 0.0)[..., None] * first
-                pairs, origin = [(0, 2), (1, 3)], 1
+                reach, pairs, origin, side = reach_in, [(0, 2), (1, 3)], 1, 1
+                through = jnp.where(is_low, near_end, own_end)
             else:
-                link = lax.dynamic_index_in_dim(edges, low, 0, False)[0] == lax.dynamic_index_in_dim(edges, low + 1, 0, False)[0]
-                joined = first + jnp.where(link[:, None], jnp.exp(low_end), 0.0)[..., None] * second
-                pairs, origin = [(2, 0), (3, 1)], 2
+                reach, pairs, origin, side = reach_out, [(2, 0), (3, 1)], 2, 0
+                through = jnp.where(is_low, own_end, near_end)
+            near = lax.ppermute(low, "ctx", swap_x).astype(f32)
+            keeps = flag(row[0, side] == row[1, side])
+            keeps = (keeps * jnp.exp(through))[..., :1]
+            outer = is_low if forward else ~is_low
+            joined = jnp.where(outer, near + keeps * own, own + keeps * near)
             far = lax.ppermute(joined.astype(bf16), "ctx", pairs).astype(f32)
-            beside = lax.dynamic_index_in_dim(coefs, here + jnp.where(is_low, 1, -1), 0, False)
-            total = beside[..., None] * near + coefs[origin][..., None] * far
-            return total[..., :HEAD_DIM], total[..., HEAD_DIM:]
+            distant = ~is_low if forward else is_low
+            scale = jnp.where(distant, jnp.exp(near_end), 1.0)[..., :1]
+            near_flag = flag(lax.dynamic_index_in_dim(reach, beside, 0, False))
+            return near_flag * near + (flag(reach[origin]) * scale) * far
+
+    else:
+        between = (index[None, :] > jnp.minimum(index[:, None], here)) & (
+            index[None, :] < jnp.maximum(index[:, None], here)
+        )
 
         def level_ends(own_end):
-            near_end = lax.ppermute(own_end, "ctx", swap_x)
-            slot = (index == here)[:, None, None]
-            beside = (index == here + jnp.where(is_low, 1, -1))[:, None, None]
-            return jnp.where(slot, own_end, 0.0) + jnp.where(beside, near_end, 0.0), near_end
-
-    else:
-
-        def exchange(keys, values, coefs, forward, own_end, near_end):
-            every = lax.all_gather(jnp.concatenate([keys, values], axis=2), "ctx")
-            total = jnp.sum(every * coefs[..., None], axis=0)
-            return total[..., :HEAD_DIM], total[..., HEAD_DIM:]
-
-        def level_ends(own_end):
-            return lax.all_gather(own_end, "ctx"), own_end
+            return own_end
+
+        def exchange(own, low, forward, own_end, near_end):
+            ends = lax.all_gather(own_end[..., :1], "ctx")
+            span = jnp.where(between[:, :, None, None, None], ends[None], 0.0)
+            span = jnp.exp(jnp.sum(span, axis=1))
+            coefs = jnp.where((reach_in if forward else reach_out)[..., None, None], span, 0.0)
+            return jnp.sum(lax.all_gather(own, "ctx") * coefs, axis=0)
 
     x = owner_first(layer_input)
     unit_one, factor_one, scaled_one = rms_parts(x.astype(f32), norm1_gain)
@@ -623,17 +648,11 @@
     log_decay = jax.nn.log_sigmoid(logits) / gate_norm
     one = -jnp.expm1(log_decay)
     sig = jax.nn.sigmoid(-logits) / gate_norm
-    levels, key_own, value_own = run_states(qkv, log_decay, one, aux)
-    own_end = levels[:, tokens - 1 :: tokens].T
-    ends, near_end = level_ends(own_end)
-    span = jnp.exp(jnp.sum(jnp.where(between[:, :, None, None], ends[None], 0.0), axis=1))
-    coef_in = jnp.where(reach_in[..., None], span, 0.0)
-    coef_out = jnp.where(reach_out[..., None], span, 0.0)
-    key_in, value_in = exchange(key_own, value_own, coef_in, True, own_end, near_end)
+    levels, state_own, state_low, own_end = run_states(qkv, log_decay, one, aux)
+    near_end = level_ends(own_end)
+    state_in = exchange(state_own, state_low, True, own_end, near_end)
     gain = head_gain[None, :]
-    normed_o, mixed, probs, scores, mixed_t = run_forward(
-        qkv, levels, one, aux, key_in, value_in, gain
-    )
+    normed_o, mixed, probs, scores, mixed_t = run_forward(qkv, levels, one, aux, state_in, gain)
     by_owner = normed_o.reshape(members, count * part, heads)
 
     def for_partner(r):
@@ -657,38 +676,41 @@
     grad_up = (grad_act * gate_silu).astype(bf16)
     grad_gu = jnp.concatenate([grad_gate, grad_up], axis=1)
     part_n2 = matmul(grad_gu, w_gu, 1, 1).astype(bf16)
-    grad_n2 = to_shards(part_n2)
-    begun = lax.ppermute(part_n2[:16, :128], "dp", [(0, 1), (1, 0)])
-    normed2, grad_gu, hidden_act = after((normed2, grad_gu, hidden_act), begun)
-    rows_wgu, stages_wgu = scatter_rows(matmul(normed2, grad_gu, 0, 0).astype(bf16))
+    grad_n2 = to_shards(part_n2).astype(f32)
+    held_wgu = scatter_cores(matmul(normed2, grad_gu, 0, 0).astype(bf16))
+    held_wd = scatter_cores(matmul(grad_feed, hidden_act, 0, 0).astype(bf16))
     feed_part = matmul(hidden_act, w_d, 1, 1).astype(bf16)
-    rows_wd, stages_wd = scatter_rows(matmul(grad_feed, hidden_act, 0, 0).astype(bf16))
     gain_two_part = jnp.sum(grad_n2 * unit_two, axis=0)
     grad_hidden = mine(grad_feed).astype(f32) + norm_back(unit_two, factor_two, grad_n2 * norm2_gain)
-    grad_attn = gather_in_parts(grad_hidden, count)
-    feed = to_shards(after(feed_part, grad_n2))
-    grad_o = matmul(grad_attn, w_o)
-    grad_o, feed = after((grad_o, feed), stages_wgu[:1], stages_wd[:1])
-    output = from_shards(hidden + feed)
-    grad_q, gk, gv, row_sums, acts, dk, dv, head_part = run_backward(
-        qkv, levels, one, aux, key_in, value_in, gain, mixed, probs, scores, mixed_t, blocks_of(grad_o)
-    )
-    dk_later, dv_later = exchange(dk, dv, coef_out, False, own_end, near_end)
-    grad_wo = matmul(grad_attn, normed_o.reshape(rows, heads), 0, 0).astype(bf16)
-    dk_later = after(dk_later, stages_wgu, stages_wd, grad_wo, output)
+    grad_attn = grad_hidden.astype(bf16)
+    sent = matmul(grad_attn, w_heads).astype(bf16)
+    sent, held_wgu, held_wd = tie(sent, held_wgu, held_wd)
+    feed = to_shards(feed_part)
+    arrived = [sent[:, :heads]] + [
+        from_partner(sent[:, r * heads : (r + 1) * heads], r) for r in range(1, members)
+    ]
+    held_wgu, held_wd = scatter_first(held_wgu), scatter_first(held_wd)
+    grad_o = jnp.zeros((members, count * part, heads), bf16)
+    for r in range(members):
+        grad_o = lax.dynamic_update_slice(grad_o, arrived[r][None], (tp_place ^ r, 0, 0))
+    grad_q, gk, gv, row_sums, acts, grad_state, grad_low, head_part = run_backward(
+        qkv, levels, one, aux, state_in, gain, mixed, probs, scores, mixed_t, blocks_of(grad_o)
+    )
+    grad_low, feed, held_wgu, grad_attn = tie(grad_low, feed, held_wgu, grad_attn)
+    out_shard = (hidden + feed.astype(f32)).astype(bf16)
+    grad_low, out_shard = tie(grad_low, out_shard)
+    output = from_shards(out_shard)
+    grad_later = exchange(grad_state, grad_low, False, own_end, near_end)
     grad_k, grad_v, grad_logits = run_finish(
-        qkv, levels, one, sig, aux, sums, key_in, value_in, key_own, value_own,
-        gk, gv, row_sums, acts, dk_later, dv_later,
+        qkv, levels, one, sig, aux, sums, state_in, state_own, gk, gv, row_sums, acts, grad_later
     )
     decay_rows = lanes(grad_logits, (count, members))
     grad_all = jnp.concatenate(
         [a.reshape(rows, heads) for a in (grad_q, grad_k, grad_v)] + [decay_rows.T], axis=1
     )
     part_n1 = (matmul(grad_all[:, :cut], w_qkv, 1, 1) + matmul(decay_rows, w_dec, 0, 1)).astype(bf16)
+    part_n1, output, grad_all = tie(part_n1, output, grad_all)
     grad_n1 = to_shards(part_n1)
-    rows_wo, _ = scatter_rows(grad_wo)
-    grad_in = matmul(normed1, after(grad_all, grad_n1), 0, 0).astype(bf16)
-    rows_att, _ = scatter_rows(grad_in)
     gain_one_part = jnp.sum(part_n1.astype(f32) * unit_one, axis=0)
     bias_part = lax.dynamic_update_slice_in_dim(
         jnp.zeros_like(decay_bias),
@@ -699,9 +721,29 @@
     small = jnp.concatenate(
         [gain_one_part, gain_two_part, jnp.sum(head_part, axis=(0, 1)), bias_part]
     )
-    small = sum_small(small)
-    input_grad = grad_hidden + norm_back(mine(unit_one), mine(factor_one), grad_n1 * norm1_gain)
-    input_grad = natural(from_shards(input_grad)).astype(f32)
+    held_wo = scatter_first(scatter_cores(matmul(grad_attn, normed_heads, 0, 0).astype(bf16)))
+    grad_in = matmul(normed1, grad_all, 0, 0).astype(bf16)
+    held_in = scatter_cores(grad_in)
+    grad_n1, small, held_in, held_wd = tie(grad_n1, small, held_in, held_wd)
+    held_wgu, held_wo = scatter_second(held_wgu), scatter_second(held_wo)
+    input_grad = grad_hidden + norm_back(mine(unit_one), mine(factor_one), grad_n1.astype(f32) * norm1_gain)
+    input_grad = from_shards(input_grad)
+    held_wd = scatter_second(held_wd)
+    if places != 4:
+        small = lax.psum(small, ("dp", "ctx", "tp"))
+    else:
+        small += lax.ppermute(small, "dp", [(0, 1), (1, 0)])
+        for axis in ("ctx", "tp"):
+            for r in (1, 2):
+                small += lax.ppermute(small, axis, [(i, i ^ r) for i in range(4)])
+    held_in = scatter_first(held_in)
+    rows_wo, rows_wgu, rows_wd = scatter_end(held_wo), scatter_end(held_wgu), scatter_end(held_wd)
+    rows_att = scatter_end(scatter_second(held_in))
+    rows_wo = rows_wo[:, :heads] + sum(
+        from_partner(rows_wo[:, r * heads : (r + 1) * heads].astype(bf16), r).astype(f32)
+        for r in range(1, members)
+    )
+    input_grad = natural(input_grad).astype(f32)
     return (
         natural(output).reshape(count, tokens, width),
         input_grad.reshape(count, tokens, width),

time: 713 us -> 664 us (0.931)
  starting transfers between devices: 100 us -> 76.7 us
  local copies, waits for them, and re-layouts: 127 us -> 110 us
  waiting for transfers between devices: 216 us -> 204 us
    ppermute x6 -> x12, waiting for transfers between devices: 34.3 us -> 86.4 us  [from_partner(): lax.ppermute(array, 'tp', [(i, i ^ distance) for i in range(members)])]
    ppermute x64 -> x46, waiting for transfers between devices: 115 us -> 72.4 us  [the longest x18 22.6 us: line_gather(): value = lax.ppermute(moving[to][c], axis, [(i, i + to) for i in sources])]
    ppermute x64 -> x46, starting transfers between devices: 86 us -> 53.5 us  [the longest x18 27 us: line_gather(): value = lax.ppermute(moving[to][c], axis, [(i, i + to) for i in sources])]
    unnamed x200 -> x178, local copies, waits for them, and re-layouts: 48.4 us -> 27.3 us
    squeeze x17, local copies, waits for them, and re-layouts: 8.07 us -> 23.9 us  [pick(): return lax.dynamic_index_in_dim(value, index, axis, keepdims=False)]
    all_gather x2, waiting for transfers between devices: 18.6 us -> 6 us  [from_shards(): return lax.all_gather(array.astype(bf16), 'tp', axis=0, tiled=True)]
    convert_element_type x15 -> x17, other arithmetic: 23.5 us -> 34.3 us  [the longest x12 29.3 us: add(): return row_major((a.astype(f32) + b.astype(f32)).astype(dtype))]
    dynamic_slice x6 -> x5, local copies, waits for them, and re-layouts: 21.2 us -> 11.7 us  [pick(): return lax.dynamic_index_in_dim(value, index, axis, keepdims=False)]
  transfers between devices with their start and end apart: 80 -> 68, of which waited for: 35 -> 30; matrix products, arithmetic and copies ran while one was open for 31% -> 35% of each run, Pallas kernels for 7% -> 7%
where the time goes in v3:
time: 664 us; the launch traced here: 655 us
  waiting for transfers between devices  204 us (31%)
  matrix products  115 us (17%)
  local copies, waits for them, and re-layouts  110 us (17%)
  starting transfers between devices  76.7 us (12%)
  other arithmetic  75.7 us (11%)
  Pallas kernels  49 us (7%)
  between operations  16.2 us (2%)
  blocking collectives  8.09 us (1%)
    dot_general x14, matrix products, matmul(): lax.dot_general(a, b, (((ca,), (cb,)), ((), ())), preferred_element_type=...  115 us
    ppermute x12, waiting for transfers between devices, from_partner(): lax.ppermute(array, 'tp', [(i, i ^ distance) for i in range(members)])  86.4 us
    convert_element_type x12, other arithmetic, add(): return row_major((a.astype(f32) + b.astype(f32)).astype(dtype))  29.3 us
    pallas_call x1, Pallas kernels, run_backward(): pl.pallas_call(backward_kernel, grid=(count,), in_specs=[own(0), own(1),...  28.7 us
    unnamed x178, local copies, waits for them, and re-layouts  27.3 us
    ppermute x18, starting transfers between devices, line_gather(): value = lax.ppermute(moving[to][c], axis, [(i, i + to) for i in sources])  27 us
    ppermute x2, waiting for transfers between devices, exchange(): far = lax.ppermute(joined.astype(bf16), 'ctx', pairs).astype(f32)  25.1 us
    squeeze x17, local copies, waits for them, and re-layouts, pick(): return lax.dynamic_index_in_dim(value, index, axis, keepdims=False)  23.9 us
  transfers between devices with their start and end apart: 68, of which 30 were waited for; matrix products, arithmetic and copies ran while one was open for 35% of the time, Pallas kernels for 7%

profile of v3, /device:TPU:0, one launch (start us, length us, event | category | flops | bytes accessed | tf_op | source)
XLA Modules:
  0.0 654.7 jit_solution(11641735350886115441)
XLA Ops:
  12.5 5.1 collective-permute-start.8
  18.3 6.6 %collective-permute-done.8 = bf16[256,512]{0,1:T(8,128)(2,1)S(1)} collective-permute-done((bf16[256,512]{0,1:T(8,128)(2,1)S(1)}, bf16[256,512]{0,1:T(8,128)(2,1)S(1)}, u32[]{:S(2)}, u32[]{:S(2)}) %collective-permute-start.8) | collective-permute-done | bytes 262176 | tf_op jit(solution)/shard_map/ppermute | solution.py:574
  24.9 15.0 %collective-permute-done.7 = bf16[256,512]{0,1:T(8,128)(2,1)S(1)} collective-permute-done((bf16[256,512]{0,1:T(8,128)(2,1)S(1)}, bf16[256,512]{0,1:T(8,128)(2,1)S(1)}, u32[]{:S(2)}, u32[]{:S(2)}) %collective-permute-start.7) | collective-permute-done | bytes 262176 | tf_op jit(solution)/shard_map/ppermute | solution.py:574
  43.4 8.1 %all-gather.1 = s32[4,2,3]{2,1,0:T(2,128)S(1)} all-gather(s32[1,2,3]{2,1,0:T(2,128)S(1)} %add_bitcast_fusion), channel_id=2, replica_groups=mesh['dp'=2,'ctx'=4,'tp'=4] {'ctx'}, dimensions={0}, use_global_device_ids=true | all-gather | bytes 120 | tf_op jit(solution)/shard_map/all_gather | solution.py:587
  63.1 3.7 fusion.52
  70.0 9.8 %fusion.21 = bf16[768,1536]{1,0:T(8,128)(2,1)S(1)} fusion(bf16[2048,1600]{0,1:T(8,128)(2,1)} %all-gather.8.cloned.1.call-done, f32[768,2048]{1,0:T(8,128)} %convert_multiply_fusion.2, f32[2048]{0:T(1024)S(1)} %copy-done.75), kind=kOutput, calls=%fused_computation.45 | convolution fusion | flops 4836163584 | bytes 14950400 | tf_op jit(solution)/shard_map/dot_general | solution.py:443
  84.0 13.8 %collective-permute-done.1 = f32[3,64,128]{2,1,0:T(8,128)S(1)} collective-permute-done((f32[3,64,128]{2,1,0:T(8,128)S(1)}, f32[3,64,128]{2,1,0:T(8,128)S(1)}, u32[]{:S(2)}, u32[]{:S(2)}) %collective-permute-start.1) | collective-permute-done | bytes 98336 | tf_op jit(solution)/shard_map/ppermute | solution.py:606
  105.5 16.3 %collective-permute-done.2 = bf16[3,64,1024]{2,1,0:T(8,128)(2,1)S(1)} collective-permute-done((bf16[3,64,1024]{2,1,0:T(8,128)(2,1)}, bf16[3,64,1024]{2,1,0:T(8,128)(2,1)S(1)}, u32[]{:S(2)}, u32[]{:S(2)}) %collective-permute-start.2) | collective-permute-done | bytes 393248 | tf_op jit(solution)/shard_map/ppermute | solution.py:621
  125.7 14.1 %shard_map.255 = (bf16[4,3,64,512]{3,2,1,0:T(8,128)(2,1)S(1)}, f32[768,512]{1,0:T(8,128)S(1)}, f32[64,768]{1,0:T(8,128)S(1)}, f32[64,768]{1,0:T(8,128)S(1)}, f32[3,256,256]{2,1,0:T(8,128)S(1)}) custom-call(bf16[4,3,64,1536]{3,2,1,0:T(8,128)(2,1)S(1)} %bitcast.266, bf16[4,3,64,1536]{3,2,1,0:T(8,128)(2,1)S(1)} %bitcast.267, ...), custom_call_target="tpu_custom_call" | custom-call | flops 3000000000 | bytes 9000000 | tf_op jit(solution)/shard_map/pallas_call | solution.py:365
  147.6 5.3 collective-permute-done.5
  152.9 9.9 %collective-permute-done.4 = bf16[192,512]{1,0:T(8,128)(2,1)S(1)} collective-permute-done((bf16[192,512]{1,0:T(8,128)(2,1)S(1)}, bf16[192,512]{1,0:T(8,128)(2,1)S(1)}, u32[]{:S(2)}, u32[]{:S(2)}) %collective-permute-start.4) | collective-permute-done | bytes 196640 | tf_op jit(solution)/shard_map/ppermute | solution.py:574
  163.5 5.6 multiply_reduce_fusion.2
  172.8 4.1 copy.114
  178.2 4.6 collective-permute-start.13
  184.1 4.8 collective-permute-start.11
  203.8 3.9 collective-permute-done.20
  213.6 10.5 %collective-permute-done.16 = bf16[64,2048]{1,0:T(8,128)(2,1)S(1)} collective-permute-done((bf16[64,2048]{1,0:T(8,128)(2,1)S(1)}, bf16[64,2048]{1,0:T(8,128)(2,1)S(1)}, u32[]{:S(2)}, u32[]{:S(2)}) %collective-permute-start.16) | collective-permute-done | bytes 262176 | tf_op jit(solution)/shard_map/ppermute | solution.py:472
  230.9 5.8 collective-permute-done.22
  241.4 13.3 %fusion.2 = f32[768,2816]{0,1:T(8,128)S(1)} fusion(bf16[768,2048]{1,0:T(8,128)(2,1)} %bitcast.51, bf16[2048,4224]{0,1:T(8,128)(2,1)} %all-gather.12.cloned.1.call-done), kind=kOutput, calls=%fused_computation.4 | convolution fusion | flops 8858370048 | bytes 23330816 | tf_op jit(solution)/shard_map/dot_general | solution.py:443
  254.7 9.3 %fusion.18 = (bf16[768,1408]{0,1:T(8,128)(2,1)S(1)}, bf16[768,1408]{0,1:T(8,128)(2,1)S(1)}, bf16[768,1408]{0,1:T(8,128)(2,1)}) fusion(f32[768,2816]{0,1:T(8,128)S(1)} %fusion.2, bf16[768,2048]{1,0:T(8,128)(2,1)S(1)} %bitcast.295, bf16[2048,4224]{0,1:T(8,128)(2,1)} %all-gather.12.cloned.1.call-done), kind=kOutput, calls=%fused_computation.38 | convolution fusion | flops 4445405184 | bytes 24051712 | tf_op jit(solution)/shard_map/dot_general | solution.py:443
  266.0 13.5 %fusion.27 = bf16[768,2048]{1,0:T(8,128)(2,1)} fusion(bf16[2048,4224]{0,1:T(8,128)(2,1)} %all-gather.12.cloned.1.call-done, bf16[768,1408]{0,1:T(8,128)(2,1)S(1)} %get-tuple-element.173, bf16[768,1408]{0,1:T(8,128)(2,1)S(1)} %get-tuple-element.172), kind=kOutput, calls=%fused_computation.47 | convolution fusion | flops 8868593664 | bytes 19005440 | tf_op jit(solution)/shard_map/dot_general | solution.py:443
  279.7 14.7 %convolution_convert_fusion = bf16[2048,2816]{1,0:T(8,128)(2,1)} fusion(bf16[768,2048]{1,0:T(8,128)(2,1)} %bitcast.51, bf16[768,1408]{0,1:T(8,128)(2,1)} %copy-done.83, bf16[768,1408]{0,1:T(8,128)(2,1)} %copy-done.82), kind=kOutput, calls=%fused_computation.1 | convolution fusion | flops 8872787968 | bytes 19005440 | tf_op jit(solution)/shard_map/dot_general | solution.py:443
  294.4 9.3 %dynamic-slice_bitcast_fusion = (bf16[2,2,256,2816]{3,2,1,0:T(8,128)(2,1)}, bf16[2,2,256,2816]{3,2,1,0:T(8,128)(2,1)}) fusion(bf16[2,2,2,256,2816]{4,3,2,1,0:T(8,128)(2,1)} %bitcast.290, s32[]{:T(128)S(6)} %select_n.289, s32[]{:T(128)S(6)} %select_n.288), kind=kLoop, calls=%fused_computation.23 | loop fusion | bytes 23068680 | tf_op jit(solution)/shard_map/jit(dynamic_index_in_dim)/squeeze | solution.py:524
  303.9 7.5 %convolution_convert_fusion.2 = bf16[1408,2048]{0,1:T(8,128)(2,1)S(1)} fusion(bf16[768,1408]{0,1:T(8,128)(2,1)} %get-tuple-element.176, bf16[768,2048]{1,0:T(8,128)(2,1)} %bitcast.292), kind=kOutput, calls=%fused_computation.11 | convolution fusion | flops 4432068608 | bytes 11075584 | tf_op jit(solution)/shard_map/dot_general | solution.py:443
  315.3 9.2 %fusion.24 = bf16[768,2048]{1,0:T(8,128)(2,1)} fusion(bf16[768,1408]{0,1:T(8,128)(2,1)S(1)} %copy-done.81, bf16[2048,4224]{0,1:T(8,128)(2,1)} %all-gather.12.cloned.1.call-done), kind=kOutput, calls=%fused_computation.46 | convolution fusion | flops 4430757888 | bytes 11075584 | tf_op jit(solution)/shard_map/dot_general | solution.py:443
  324.7 13.2 %reduce-scatter.4.cloned.1.call-done = bf16[192,2048]{1,0:T(8,128)(2,1)} async-done(((bf16[768,2048]{1,0:T(8,128)(2,1)}), bf16[192,2048]{1,0:T(8,128)(2,1)}) %reduce-scatter.4.cloned.1.call-update) | async-done | bytes 786448 | tf_op jit(solution)/shard_map/reduce_scatter | solution.py:512
  341.6 6.6 %convolution_convert_fusion.4 = bf16[192,2048]{1,0:T(8,128)(2,1)S(1)} fusion(bf16[192,2048]{1,0:T(8,128)(2,1)S(1)} %fusion.89, bf16[2048,2048]{0,1:T(8,128)(2,1)} %all-gather.10.cloned.1.call-done), kind=kOutput, calls=%fused_computation.60 | convolution fusion | flops 1611005952 | bytes 9961472 | tf_op jit(solution)/shard_map/dot_general | solution.py:443
  352.7 5.7 add_convert_fusion
  370.3 6.1 collective-permute-done.29
  378.1 10.2 %collective-permute-done.30 = bf16[192,512]{1,0:T(8,128)(2,1)S(1)} collective-permute-done((bf16[192,512]{1,0:T(8,128)(2,1)S(1)}, bf16[192,512]{1,0:T(8,128)(2,1)S(1)}, u32[]{:S(2)}, u32[]{:S(2)}) %collective-permute-start.30) | collective-permute-done | bytes 196640 | tf_op jit(solution)/shard_map/ppermute | solution.py:574
  389.9 28.7 %shard_map.256 = (bf16[4,3,64,512]{3,2,1,0:T(8,128)(2,1)S(1)}, f32[768,512]{1,0:T(8,128)}, f32[768,512]{1,0:T(8,128)}, f32[64,768]{1,0:T(8,128)S(1)}, f32[64,768...) custom-call(bf16[4,3,64,1536]{3,2,1,0:T(8,128)(2,1)} %bitcast.269, ...), custom_call_target="tpu_custom_call" | custom-call | flops 8999999488 | bytes 15000000 | tf_op jit(solution)/shard_map/pallas_call | solution.py:392
  440.4 3.8 collective-permute-done.56
  446.8 8.9 %collective-permute-done.35 = bf16[3,64,1024]{2,1,0:T(8,128)(2,1)S(1)} collective-permute-done((bf16[3,64,1024]{2,1,0:T(8,128)(2,1)S(1)}, bf16[3,64,1024]{2,1,0:T(8,128)(2,1)S(1)}, u32[]{:S(2)}, u32[]{:S(2)}) %collective-permute-start.35) | collective-permute-done | bytes 393248 | tf_op jit(solution)/shard_map/ppermute | solution.py:621
  455.9 4.2 shard_map.257
  464.3 7.2 %fusion.8 = f32[768,2048]{1,0:T(8,128)S(1)} fusion(bf16[2048,1600]{0,1:T(8,128)(2,1)} %all-gather.8.cloned.1.call-done, bf16[768,512]{1,0:T(8,128)(2,1)S(1)} %bitcast.279, bf16[768,512]{1,0:T(8,128)(2,1)S(1)} %bitcast.277, bf16[768,512]{1,0:T(8,128)(2,1)S(1)} %bitcast.275), kind=kOutput, calls=%fused_computation.25 | convolution fusion | flops 4838916096 | bytes 14942208 | tf_op jit(solution)/shard_map/dot_general | solution.py:443
  475.1 5.4 fusion.4
  483.8 4.5 all-gather.14.cloned.1.call-done
  488.4 9.0 %convolution_convert_fusion.1 = bf16[2048,1600]{1,0:T(8,128)(2,1)S(1)} fusion(bf16[768,1600]{1,0:T(8,128)(2,1)} %pad_maximum_fusion.3, f32[768,2048]{1,0:T(8,128)} %convert_multiply_fusion.2, f32[2048]{0:T(1024)S(1)} %copy-done.76), kind=kOutput, calls=%fused_computation.10 | convolution fusion | flops 5039587328 | bytes 15310848 | tf_op jit(solution)/shard_map/dot_general | solution.py:443
  500.9 5.5 copy.122
  514.7 8.2 %collective-permute-done.50 = bf16[128,2048]{1,0:T(8,128)(2,1)S(1)} collective-permute-done((bf16[128,2048]{1,0:T(8,128)(2,1)S(1)}, bf16[128,2048]{1,0:T(8,128)(2,1)S(1)}, u32[]{:S(2)}, u32[]{:S(2)}) %collective-permute-start.50) | collective-permute-done | bytes 524320 | tf_op jit(solution)/shard_map/ppermute | solution.py:557
  531.9 19.9 %collective-permute-done.53 = bf16[256,512]{1,0:T(8,128)(2,1)S(1)} collective-permute-done((bf16[256,512]{1,0:T(8,128)(2,1)S(1)}, bf16[256,512]{1,0:T(8,128)(2,1)S(1)}, u32[]{:S(2)}, u32[]{:S(2)}) %collective-permute-start.53) | collective-permute-done | bytes 262176 | tf_op jit(solution)/shard_map/ppermute | solution.py:574
  551.9 4.1 multiply_reduce_fusion
  557.9 13.3 %collective-permute-done.54 = bf16[256,512]{1,0:T(8,128)(2,1)S(1)} collective-permute-done((bf16[256,512]{1,0:T(8,128)(2,1)S(1)}, bf16[256,512]{1,0:T(8,128)(2,1)S(1)}, u32[]{:S(2)}, u32[]{:S(2)}) %collective-permute-start.54) | collective-permute-done | bytes 262176 | tf_op jit(solution)/shard_map/ppermute | solution.py:574
  574.4 3.9 add_convert_fusion.6
  586.4 5.5 copy.124
  592.5 3.8 add_convert_fusion.1
  616.6 4.5 collective-permute-done.46
  630.5 4.6 collective-permute-done.47
  (468 shorter events, 227.9 us)
Async XLA Ops:
  7.2 55.9 %all-gather.8.cloned.1.call-start = ((), (), s32[]{:S(2)}) async-start(), calls=%async_computation.3 | async-start | bytes 7372800 | tf_op jit(solution)/shard_map/all_gather | solution.py:518
  12.4 150.4 %all-gather.10.cloned.1.call-start = ((), (), s32[]{:S(2)}) async-start(), calls=%async_computation.4 | async-start | bytes 9437184 | tf_op jit(solution)/shard_map/all_gather | solution.py:518
  17.6 22.3 %collective-permute-start.7 = (bf16[256,512]{0,1:T(8,128)(2,1)S(1)}, bf16[256,512]{0,1:T(8,128)(2,1)S(1)}, u32[]{:S(2)}, u32[]{:S(2)}) collective-permute-start(bf16[256,512]{0,1:T(8,128)(2,1)S(1)} %bitcast.311), channel_id=1, source_target_pairs={{0,2},{1,3},{2,0},{3,1},{4,6},{5,7},{6,4},{7,5},{8,10},{9,11},{10,... | collective-permute-start | bytes 786440 | tf_op jit(solution)/shard_map/ppermute | solution.py:574
  17.6 22.3 %collective-permute-start.6 = (bf16[256,512]{0,1:T(8,128)(2,1)S(1)}, bf16[256,512]{0,1:T(8,128)(2,1)S(1)}, u32[]{:S(2)}, u32[]{:S(2)}) collective-permute-start(bf16[256,512]{0,1:T(8,128)(2,1)S(1)} %bitcast.312), channel_id=1, source_target_pairs={{0,1},{1,0},{2,3},{3,2},{4,5},{5,4},{6,7},{7,6},{8,9},{9,8},{10,11... | collective-permute-start | bytes 786440 | tf_op jit(solution)/shard_map/ppermute | solution.py:574
  41.0 200.4 %all-gather.12.cloned.1.call-start = ((), (), s32[]{:S(2)}) async-start(), calls=%async_computation.5 | async-start | bytes 19464192 | tf_op jit(solution)/shard_map/all_gather | solution.py:518
  43.2 294.8 %reduce-scatter.4.cloned.1.call-start = ((), (), s32[]{:S(2)}) async-start(), calls=%async_computation.6 | async-start | bytes 3932160 | tf_op jit(solution)/shard_map/reduce_scatter | solution.py:512
  81.8 16.8 %collective-permute-start = (bf16[3,64,1024]{2,1,0:T(8,128)(2,1)S(1)}, bf16[3,64,1024]{2,1,0:T(8,128)(2,1)S(1)}, u32[]{:S(2)}, u32[]{:S(2)}) collective-permute-start(bf16[3,64,1024]{2,1,0:T(8,128)(2,1)S(1)} %get-tuple-element.60), channel_id=1, source_target_pairs={{0,4},{4,0},{8,12},{12,8},{1,5},{5,1},{9,13},{13,9},{2,6},{6,2},{1... | collective-permute-start | bytes 1179656 | tf_op jit(solution)/shard_map/ppermute | solution.py:616
  83.3 14.5 %collective-permute-start.1 = (f32[3,64,128]{2,1,0:T(8,128)S(1)}, f32[3,64,128]{2,1,0:T(8,128)S(1)}, u32[]{:S(2)}, u32[]{:S(2)}) collective-permute-start(f32[3,64,128]{2,1,0:T(8,128)S(1)} %get-tuple-element.61), channel_id=1, source_target_pairs={{0,4},{4,0},{8,12},{12,8},{1,5},{5,1},{9,13},{13,9},{2,6},{6,2},{1... | collective-permute-start | bytes 294920 | tf_op jit(solution)/shard_map/ppermute | solution.py:606
  100.5 21.2 %collective-permute-start.2 = (bf16[3,64,1024]{2,1,0:T(8,128)(2,1)}, bf16[3,64,1024]{2,1,0:T(8,128)(2,1)S(1)}, u32[]{:S(2)}, u32[]{:S(2)}) collective-permute-start(bf16[3,64,1024]{2,1,0:T(8,128)(2,1)} %fusion.57), channel_id=1, source_target_pairs={{0,8},{4,12},{1,9},{5,13},{2,10},{6,14},{3,11},{7,15},{16,24},{20,... | collective-permute-start | bytes 1179656 | tf_op jit(solution)/shard_map/ppermute | solution.py:621
  146.6 16.2 %collective-permute-start.4 = (bf16[192,512]{1,0:T(8,128)(2,1)S(1)}, bf16[192,512]{1,0:T(8,128)(2,1)S(1)}, u32[]{:S(2)}, u32[]{:S(2)}) collective-permute-start(bf16[192,512]{1,0:T(8,128)(2,1)S(1)} %get-tuple-element.213), channel_id=1, source_target_pairs={{0,2},{1,3},{2,0},{3,1},{4,6},{5,7},{6,4},{7,5},{8,10},{9,11},{10,... | collective-permute-start | bytes 589832 | tf_op jit(solution)/shard_map/ppermute | solution.py:574
  146.6 16.2 %collective-permute-start.3 = (bf16[192,512]{1,0:T(8,128)(2,1)S(1)}, bf16[192,512]{1,0:T(8,128)(2,1)S(1)}, u32[]{:S(2)}, u32[]{:S(2)}) collective-permute-start(bf16[192,512]{1,0:T(8,128)(2,1)S(1)} %get-tuple-element.214), channel_id=1, source_target_pairs={{0,1},{1,0},{2,3},{3,2},{4,5},{5,4},{6,7},{7,6},{8,9},{9,8},{10,11... | collective-permute-start | bytes 589832 | tf_op jit(solution)/shard_map/ppermute | solution.py:574
  171.2 17.6 %collective-permute-start.9 = (bf16[64,2048]{1,0:T(8,128)(2,1)}, bf16[64,2048]{1,0:T(8,128)(2,1)S(1)}, u32[]{:S(2)}, u32[]{:S(2)}) collective-permute-start(bf16[64,2048]{1,0:T(8,128)(2,1)} %get-tuple-element.210), channel_id=1, source_target_pairs={{0,1},{1,2},{2,3},{4,5},{5,6},{6,7},{8,9},{9,10},{10,11},{12,13},{... | collective-permute-start | bytes 786440 | tf_op jit(solution)/shard_map/ppermute | solution.py:472
  176.9 16.0 %collective-permute-start.14 = (bf16[64,2048]{1,0:T(8,128)(2,1)S(1)}, bf16[64,2048]{1,0:T(8,128)(2,1)S(1)}, u32[]{:S(2)}, u32[]{:S(2)}) collective-permute-start(bf16[64,2048]{1,0:T(8,128)(2,1)S(1)} %get-tuple-element.208), channel_id=1, source_target_pairs={{1,0},{2,1},{3,2},{5,4},{6,5},{7,6},{9,8},{10,9},{11,10},{13,12},{... | collective-permute-start | bytes 786440 | tf_op jit(solution)/shard_map/ppermute | solution.py:472
  178.2 15.4 %collective-permute-start.13 = (bf16[64,2048]{1,0:T(8,128)(2,1)S(1)}, bf16[64,2048]{1,0:T(8,128)(2,1)S(1)}, u32[]{:S(2)}, u32[]{:S(2)}) collective-permute-start(bf16[64,2048]{1,0:T(8,128)(2,1)S(1)} %get-tuple-element.208), channel_id=1, source_target_pairs={{0,1},{1,2},{2,3},{4,5},{5,6},{6,7},{8,9},{9,10},{10,11},{12,13},{... | collective-permute-start | bytes 786440 | tf_op jit(solution)/shard_map/ppermute | solution.py:472
  195.6 16.0 %collective-permute-start.18 = (bf16[64,2048]{1,0:T(8,128)(2,1)S(1)}, bf16[64,2048]{1,0:T(8,128)(2,1)S(1)}, u32[]{:S(2)}, u32[]{:S(2)}) collective-permute-start(bf16[64,2048]{1,0:T(8,128)(2,1)S(1)} %collective-permute-done.12), channel_id=1, source_target_pairs={{1,0},{2,1},{5,4},{6,5},{9,8},{10,9},{13,12},{14,13},{17,16},{18,1... | collective-permute-start | bytes 786440 | tf_op jit(solution)/shard_map/ppermute | solution.py:472
  197.3 15.0 %collective-permute-start.17 = (bf16[64,2048]{1,0:T(8,128)(2,1)S(1)}, bf16[64,2048]{1,0:T(8,128)(2,1)S(1)}, u32[]{:S(2)}, u32[]{:S(2)}) collective-permute-start(bf16[64,2048]{1,0:T(8,128)(2,1)S(1)} %collective-permute-done.11), channel_id=1, source_target_pairs={{1,2},{2,3},{5,6},{6,7},{9,10},{10,11},{13,14},{14,15},{17,18},{18... | collective-permute-start | bytes 786440 | tf_op jit(solution)/shard_map/ppermute | solution.py:472
  201.6 22.5 %collective-permute-start.16 = (bf16[64,2048]{1,0:T(8,128)(2,1)S(1)}, bf16[64,2048]{1,0:T(8,128)(2,1)S(1)}, u32[]{:S(2)}, u32[]{:S(2)}) collective-permute-start(bf16[64,2048]{1,0:T(8,128)(2,1)S(1)} %collective-permute-done.10), channel_id=1, source_target_pairs={{1,0},{2,1},{5,4},{6,5},{9,8},{10,9},{13,12},{14,13},{17,16},{18,1... | collective-permute-start | bytes 786440 | tf_op jit(solution)/shard_map/ppermute | solution.py:472
  207.7 20.8 %collective-permute-start.21 = (bf16[64,2048]{1,0:T(8,128)(2,1)S(1)}, bf16[64,2048]{1,0:T(8,128)(2,1)S(1)}, u32[]{:S(2)}, u32[]{:S(2)}) collective-permute-start(bf16[64,2048]{1,0:T(8,128)(2,1)S(1)} %collective-permute-done.15), channel_id=1, source_target_pairs={{2,3},{6,7},{10,11},{14,15},{18,19},{22,23},{26,27},{30,31}} | collective-permute-start | bytes 786440 | tf_op jit(solution)/shard_map/ppermute | solution.py:472
  208.3 31.3 %collective-permute-start.26 = (bf16[64,2048]{1,0:T(8,128)(2,1)S(1)}, bf16[64,2048]{1,0:T(8,128)(2,1)S(1)}, u32[]{:S(2)}, u32[]{:S(2)}) collective-permute-start(bf16[64,2048]{1,0:T(8,128)(2,1)S(1)} %collective-permute-done.20), channel_id=1, source_target_pairs={{1,0},{5,4},{9,8},{13,12},{17,16},{21,20},{25,24},{29,28}} | collective-permute-start | bytes 786440 | tf_op jit(solution)/shard_map/ppermute | solution.py:472
  211.6 27.3 %collective-permute-start.25 = (bf16[64,2048]{1,0:T(8,128)(2,1)S(1)}, bf16[64,2048]{1,0:T(8,128)(2,1)S(1)}, u32[]{:S(2)}, u32[]{:S(2)}) collective-permute-start(bf16[64,2048]{1,0:T(8,128)(2,1)S(1)} %collective-permute-done.19), channel_id=1, source_target_pairs={{2,3},{6,7},{10,11},{14,15},{18,19},{22,23},{26,27},{30,31}} | collective-permute-start | bytes 786440 | tf_op jit(solution)/shard_map/ppermute | solution.py:472
  212.3 25.9 %collective-permute-start.24 = (bf16[64,2048]{1,0:T(8,128)(2,1)S(1)}, bf16[64,2048]{1,0:T(8,128)(2,1)S(1)}, u32[]{:S(2)}, u32[]{:S(2)}) collective-permute-start(bf16[64,2048]{1,0:T(8,128)(2,1)S(1)} %collective-permute-done.18), channel_id=1, source_target_pairs={{1,0},{5,4},{9,8},{13,12},{17,16},{21,20},{25,24},{29,28}} | collective-permute-start | bytes 786440 | tf_op jit(solution)/shard_map/ppermute | solution.py:472
  279.5 141.3 %reduce-scatter.6.cloned.1.call-start = ((), (), s32[]{:S(2)}) async-start(), calls=%async_computation.7 | async-start | bytes 3932160 | tf_op jit(solution)/shard_map/reduce_scatter | solution.py:512
  303.7 44.5 %collective-permute-start.27 = (bf16[2,2,256,2816]{3,2,1,0:T(8,128)(2,1)}, bf16[2,2,256,2816]{3,2,1,0:T(8,128)(2,1)}, u32[]{:S(2)}, u32[]{:S(2)}) collective-permute-start(bf16[2,2,256,2816]{3,2,1,0:T(8,128)(2,1)} %get-tuple-element.174), channel_id=1, source_target_pairs={{0,16},{16,0},{1,17},{17,1},{2,18},{18,2},{3,19},{19,3},{4,20},{20... | collective-permute-start | bytes 17301512 | tf_op jit(solution)/shard_map/ppermute | solution.py:533
  314.5 33.7 %collective-permute-start.28 = (bf16[2,2,256,1408]{3,2,1,0:T(8,128)(2,1)}, bf16[2,2,256,1408]{3,2,1,0:T(8,128)(2,1)}, u32[]{:S(2)}, u32[]{:S(2)}) collective-permute-start(bf16[2,2,256,1408]{3,2,1,0:T(8,128)(2,1)} %get-tuple-element.181), channel_id=1, source_target_pairs={{0,16},{16,0},{1,17},{17,1},{2,18},{18,2},{3,19},{19,3},{4,20},{20... | collective-permute-start | bytes 8650760 | tf_op jit(solution)/shard_map/ppermute | solution.py:533
  324.5 163.9 %all-gather.14.cloned.1.call-start = ((), (), s32[]{:S(2)}) async-start(), calls=%async_computation.8 | async-start | bytes 3932160 | tf_op jit(solution)/shard_map/all_gather | solution.py:515
  348.3 41.5 %collective-permute-start.31 = (bf16[192,512]{1,0:T(8,128)(2,1)S(1)}, bf16[192,512]{1,0:T(8,128)(2,1)S(1)}, u32[]{:S(2)}, u32[]{:S(2)}) collective-permute-start(bf16[192,512]{1,0:T(8,128)(2,1)S(1)} %get-tuple-element.205), channel_id=1, source_target_pairs={{0,3},{1,2},{2,1},{3,0},{4,7},{5,6},{6,5},{7,4},{8,11},{9,10},{10,... | collective-permute-start | bytes 589832 | tf_op jit(solution)/shard_map/ppermute | solution.py:574
  350.5 37.8 %collective-permute-start.30 = (bf16[192,512]{1,0:T(8,128)(2,1)S(1)}, bf16[192,512]{1,0:T(8,128)(2,1)S(1)}, u32[]{:S(2)}, u32[]{:S(2)}) collective-permute-start(bf16[192,512]{1,0:T(8,128)(2,1)S(1)} %get-tuple-element.206), channel_id=1, source_target_pairs={{0,2},{1,3},{2,0},{3,1},{4,6},{5,7},{6,4},{7,5},{8,10},{9,11},{10,... | collective-permute-start | bytes 589832 | tf_op jit(solution)/shard_map/ppermute | solution.py:574
  350.9 25.6 %collective-permute-start.29 = (bf16[192,512]{1,0:T(8,128)(2,1)S(1)}, bf16[192,512]{1,0:T(8,128)(2,1)S(1)}, u32[]{:S(2)}, u32[]{:S(2)}) collective-permute-start(bf16[192,512]{1,0:T(8,128)(2,1)S(1)} %get-tuple-element.207), channel_id=1, source_target_pairs={{0,1},{1,0},{2,3},{3,2},{4,5},{5,4},{6,7},{7,6},{8,9},{9,8},{10,11... | collective-permute-start | bytes 589832 | tf_op jit(solution)/shard_map/ppermute | solution.py:574
  360.7 60.1 %collective-permute-start.33 = (bf16[2,128,2816]{2,1,0:T(8,128)(2,1)}, bf16[2,128,2816]{2,1,0:T(8,128)(2,1)}, u32[]{:S(2)}, u32[]{:S(2)}) collective-permute-start(bf16[2,128,2816]{2,1,0:T(8,128)(2,1)} %get-tuple-element.191), channel_id=1, source_target_pairs={{0,8},{8,0},{4,12},{12,4},{1,9},{9,1},{5,13},{13,5},{2,10},{10,2},... | collective-permute-start | bytes 4325384 | tf_op jit(solution)/shard_map/ppermute | solution.py:546
  366.1 206.3 %collective-permute-start.38 = (bf16[2,128,1408]{2,1,0:T(8,128)(2,1)}, bf16[2,128,1408]{2,1,0:T(8,128)(2,1)}, u32[]{:S(2)}, u32[]{:S(2)}) collective-permute-start(bf16[2,128,1408]{2,1,0:T(8,128)(2,1)} %get-tuple-element.198), channel_id=1, source_target_pairs={{0,8},{8,0},{4,12},{12,4},{1,9},{9,1},{5,13},{13,5},{2,10},{10,2},... | collective-permute-start | bytes 2162696 | tf_op jit(solution)/shard_map/ppermute | solution.py:546
  376.5 44.3 %collective-permute-start.32 = (bf16[2,128,2816]{2,1,0:T(8,128)(2,1)}, bf16[2,128,2816]{2,1,0:T(8,128)(2,1)}, u32[]{:S(2)}, u32[]{:S(2)}) collective-permute-start(bf16[2,128,2816]{2,1,0:T(8,128)(2,1)} %get-tuple-element.193), channel_id=1, source_target_pairs={{0,4},{4,0},{8,12},{12,8},{1,5},{5,1},{9,13},{13,9},{2,6},{6,2},{1... | collective-permute-start | bytes 4325384 | tf_op jit(solution)/shard_map/ppermute | solution.py:545
  388.3 184.1 %collective-permute-start.37 = (bf16[2,128,1408]{2,1,0:T(8,128)(2,1)}, bf16[2,128,1408]{2,1,0:T(8,128)(2,1)}, u32[]{:S(2)}, u32[]{:S(2)}) collective-permute-start(bf16[2,128,1408]{2,1,0:T(8,128)(2,1)} %get-tuple-element.200), channel_id=1, source_target_pairs={{0,4},{4,0},{8,12},{12,8},{1,5},{5,1},{9,13},{13,9},{2,6},{6,2},{1... | collective-permute-start | bytes 2162696 | tf_op jit(solution)/shard_map/ppermute | solution.py:545
  423.5 148.9 %reduce-scatter.8.cloned.1.call-start = ((), (), s32[]{:S(2)}) async-start(), calls=%async_computation.9 | async-start | bytes 3932160 | tf_op jit(solution)/shard_map/reduce_scatter | solution.py:512
  424.0 14.5 %collective-permute-start.34 = (bf16[3,64,1024]{2,1,0:T(8,128)(2,1)}, bf16[3,64,1024]{2,1,0:T(8,128)(2,1)S(1)}, u32[]{:S(2)}, u32[]{:S(2)}) collective-permute-start(bf16[3,64,1024]{2,1,0:T(8,128)(2,1)} %copy-done.19), channel_id=1, source_target_pairs={{0,4},{4,0},{8,12},{12,8},{1,5},{5,1},{9,13},{13,9},{2,6},{6,2},{1... | collective-permute-start | bytes 1179656 | tf_op jit(solution)/shard_map/ppermute | solution.py:616
  426.8 17.4 %collective-permute-start.56 = (bf16[128,2816]{1,0:T(8,128)(2,1)S(1)}, bf16[128,2816]{1,0:T(8,128)(2,1)S(1)}, u32[]{:S(2)}, u32[]{:S(2)}) collective-permute-start(bf16[128,2816]{1,0:T(8,128)(2,1)S(1)} %dynamic-slice_bitcast_fusion.14), channel_id=1, source_target_pairs={{0,8},{8,0},{4,12},{12,4},{1,9},{9,1},{5,13},{13,5},{2,10},{10,2},... | collective-permute-start | bytes 2162696 | tf_op jit(solution)/shard_map/ppermute | solution.py:557
  435.8 39.3 %collective-permute-start.48 = (bf16[2,2,256,2048]{3,2,1,0:T(8,128)(2,1)}, bf16[2,2,256,2048]{3,2,1,0:T(8,128)(2,1)}, u32[]{:S(2)}, u32[]{:S(2)}) collective-permute-start(bf16[2,2,256,2048]{3,2,1,0:T(8,128)(2,1)} %dynamic-slice_bitcast_fusion.2), channel_id=1, source_target_pairs={{0,16},{16,0},{1,17},{17,1},{2,18},{18,2},{3,19},{19,3},{4,20},{20... | collective-permute-start | bytes 12582920 | tf_op jit(solution)/shard_map/ppermute | solution.py:533
  438.5 73.3 %collective-permute-start.57 = (bf16[128,2816]{1,0:T(8,128)(2,1)}, bf16[128,2816]{1,0:T(8,128)(2,1)}, u32[]{:S(2)}, u32[]{:S(2)}) collective-permute-start(bf16[128,2816]{1,0:T(8,128)(2,1)} %dynamic-slice_bitcast_fusion.13), channel_id=1, source_target_pairs={{0,4},{4,0},{8,12},{12,8},{1,5},{5,1},{9,13},{13,9},{2,6},{6,2},{1... | collective-permute-start | bytes 2162696 | tf_op jit(solution)/shard_map/ppermute | solution.py:558
  482.2 24.2 %collective-permute-start.49 = (bf16[2,128,2048]{2,1,0:T(8,128)(2,1)S(1)}, bf16[2,128,2048]{2,1,0:T(8,128)(2,1)}, u32[]{:S(2)}, u32[]{:S(2)}) collective-permute-start(bf16[2,128,2048]{2,1,0:T(8,128)(2,1)S(1)} %dynamic-slice_bitcast_fusion.11), channel_id=1, source_target_pairs={{0,4},{4,0},{8,12},{12,8},{1,5},{5,1},{9,13},{13,9},{2,6},{6,2},{1... | collective-permute-start | bytes 3145736 | tf_op jit(solution)/shard_map/ppermute | solution.py:545
  483.7 24.9 %collective-permute-start.51 = (bf16[2,128,2048]{2,1,0:T(8,128)(2,1)S(1)}, bf16[2,128,2048]{2,1,0:T(8,128)(2,1)}, u32[]{:S(2)}, u32[]{:S(2)}) collective-permute-start(bf16[2,128,2048]{2,1,0:T(8,128)(2,1)S(1)} %dynamic-slice_bitcast_fusion.10), channel_id=1, source_target_pairs={{0,8},{8,0},{4,12},{12,4},{1,9},{9,1},{5,13},{13,5},{2,10},{10,2},... | collective-permute-start | bytes 3145736 | tf_op jit(solution)/shard_map/ppermute | solution.py:546
  488.4 153.5 %all-gather.16.cloned.1.call-start = ((), (), s32[]{:S(2)}) async-start(), calls=%async_computation.10 | async-start | bytes 3932160 | tf_op jit(solution)/shard_map/all_gather | solution.py:515
  506.4 66.0 %collective-permute-start.36 = (bf16[2,2,256,1600]{2,3,1,0:T(8,128)(2,1)}, bf16[2,2,256,1600]{2,3,1,0:T(8,128)(2,1)}, u32[]{:S(2)}, u32[]{:S(2)}) collective-permute-start(bf16[2,2,256,1600]{2,3,1,0:T(8,128)(2,1)} %bitcast.299), channel_id=1, source_target_pairs={{0,16},{16,0},{1,17},{17,1},{2,18},{18,2},{3,19},{19,3},{4,20},{20... | collective-permute-start | bytes 9830408 | tf_op jit(solution)/shard_map/ppermute | solution.py:533
  527.2 24.7 %collective-permute-start.53 = (bf16[256,512]{1,0:T(8,128)(2,1)S(1)}, bf16[256,512]{1,0:T(8,128)(2,1)S(1)}, u32[]{:S(2)}, u32[]{:S(2)}) collective-permute-start(bf16[256,512]{1,0:T(8,128)(2,1)S(1)} %get-tuple-element.202), channel_id=1, source_target_pairs={{0,1},{1,0},{2,3},{3,2},{4,5},{5,4},{6,7},{7,6},{8,9},{9,8},{10,11... | collective-permute-start | bytes 786440 | tf_op jit(solution)/shard_map/ppermute | solution.py:574
  529.4 28.5 %collective-permute-start.55 = (bf16[256,512]{1,0:T(8,128)(2,1)S(1)}, bf16[256,512]{1,0:T(8,128)(2,1)S(1)}, u32[]{:S(2)}, u32[]{:S(2)}) collective-permute-start(bf16[256,512]{1,0:T(8,128)(2,1)S(1)} %get-tuple-element.203), channel_id=1, source_target_pairs={{0,3},{1,2},{2,1},{3,0},{4,7},{5,6},{6,5},{7,4},{8,11},{9,10},{10,... | collective-permute-start | bytes 786440 | tf_op jit(solution)/shard_map/ppermute | solution.py:574
  551.9 19.4 %collective-permute-start.54 = (bf16[256,512]{1,0:T(8,128)(2,1)S(1)}, bf16[256,512]{1,0:T(8,128)(2,1)S(1)}, u32[]{:S(2)}, u32[]{:S(2)}) collective-permute-start(bf16[256,512]{1,0:T(8,128)(2,1)S(1)} %get-tuple-element.204), channel_id=1, source_target_pairs={{0,2},{1,3},{2,0},{3,1},{4,6},{5,7},{6,4},{7,5},{8,10},{9,11},{10,... | collective-permute-start | bytes 786440 | tf_op jit(solution)/shard_map/ppermute | solution.py:574
  580.5 32.2 %collective-permute-start.58 = (bf16[128,1408]{1,0:T(8,128)(2,1)}, bf16[128,1408]{1,0:T(8,128)(2,1)}, u32[]{:S(2)}, u32[]{:S(2)}) collective-permute-start(bf16[128,1408]{1,0:T(8,128)(2,1)} %dynamic-slice_bitcast_fusion.24), channel_id=1, source_target_pairs={{0,8},{8,0},{4,12},{12,4},{1,9},{9,1},{5,13},{13,5},{2,10},{10,2},... | collective-permute-start | bytes 1081352 | tf_op jit(solution)/shard_map/ppermute | solution.py:557
  584.9 28.8 %collective-permute-start.59 = (bf16[128,1408]{1,0:T(8,128)(2,1)}, bf16[128,1408]{1,0:T(8,128)(2,1)}, u32[]{:S(2)}, u32[]{:S(2)}) collective-permute-start(bf16[128,1408]{1,0:T(8,128)(2,1)} %dynamic-slice_bitcast_fusion.23), channel_id=1, source_target_pairs={{0,4},{4,0},{8,12},{12,8},{1,5},{5,1},{9,13},{13,9},{2,6},{6,2},{1... | collective-permute-start | bytes 1081352 | tf_op jit(solution)/shard_map/ppermute | solution.py:558
  601.7 19.4 %collective-permute-start.46 = (bf16[2,128,1600]{1,2,0:T(8,128)(2,1)}, bf16[2,128,1600]{1,2,0:T(8,128)(2,1)}, u32[]{:S(2)}, u32[]{:S(2)}) collective-permute-start(bf16[2,128,1600]{1,2,0:T(8,128)(2,1)} %bitcast.306), channel_id=1, source_target_pairs={{0,8},{8,0},{4,12},{12,4},{1,9},{9,1},{5,13},{13,5},{2,10},{10,2},... | collective-permute-start | bytes 2457608 | tf_op jit(solution)/shard_map/ppermute | solution.py:546
  607.5 19.7 %collective-permute-start.44 = (bf16[2,128,1600]{1,2,0:T(8,128)(2,1)}, bf16[2,128,1600]{1,2,0:T(8,128)(2,1)}, u32[]{:S(2)}, u32[]{:S(2)}) collective-permute-start(bf16[2,128,1600]{1,2,0:T(8,128)(2,1)} %bitcast.307), channel_id=1, source_target_pairs={{0,4},{4,0},{8,12},{12,8},{1,5},{5,1},{9,13},{13,9},{2,6},{6,2},{1... | collective-permute-start | bytes 2457608 | tf_op jit(solution)/shard_map/ppermute | solution.py:545
  (104 other events, 1222.4 us)
Sparse Core Ops, SparseCore 0:
  12.5 50.5 all-gather.7
  65.6 62.1 all-gather.9
  129.6 101.1 all-gather.11
  279.6 58.2 reduce-scatter.3
  340.1 72.7 reduce-scatter.5
  423.6 64.6 all-gather.13
  490.6 74.4 reduce-scatter.7
  578.5 63.2 all-gather.15

commit v4 on v3

--- a/solution.py
+++ b/solution.py
@@ -164,7 +164,7 @@
         w_scr[j] = w
         return scores + w * d_scr[pl.ds(j, 1), :]
 
-    scores = lax.fori_loop(0, CHUNK, inside, jnp.zeros_like(levels), unroll=4)
+    scores = lax.fori_loop(0, CHUNK, inside, jnp.zeros_like(levels), unroll=8)
     decay = jnp.exp(levels - level_refs(levels) + aux_ref[0, base : base + 1, :])
     for c in range(1, chunks):
         w = levels[:, c * CHUNK - 1 : c * CHUNK] - levels + aux_ref[0, 2 * CHUNK + c : 2 * CHUNK + c + 1, :]
@@ -185,7 +185,7 @@
         d_scr[pl.ds(j, 1), :] = jnp.sum(w_scr[j] * probs, axis=0, keepdims=True)
         return carry
 
-    lax.fori_loop(0, CHUNK, mixing, 0, unroll=4)
+    lax.fori_loop(0, CHUNK, mixing, 0, unroll=8)
     row = lax.broadcasted_iota(jnp.int32, (tokens, tokens), 0) // CHUNK
     col = lax.broadcasted_iota(jnp.int32, (tokens, tokens), 1) // CHUNK
     mixed_t = jnp.where(row == col, jnp.concatenate([d_scr[...]] * chunks, axis=0), 0.0)
@@ -223,7 +223,7 @@
         w_scr[j] = w
         return dp + w * d_scr[pl.ds(j, 1), :]
 
-    dp = lax.fori_loop(0, CHUNK, inside, jnp.zeros_like(levels), unroll=4)
+    dp = lax.fori_loop(0, CHUNK, inside, jnp.zeros_like(levels), unroll=8)
     decay = jnp.exp(levels - level_refs(levels) + aux_ref[0, base : base + 1, :])
     for c in range(1, chunks):
         w = levels[:, c * CHUNK - 1 : c * CHUNK] - levels + aux_ref[0, 2 * CHUNK + c : 2 * CHUNK + c + 1, :]
@@ -243,7 +243,7 @@
         d_scr[pl.ds(j, 1), :] = jnp.sum(w_scr[j] * dz, axis=0, keepdims=True)
         return carry
 
-    lax.fori_loop(0, CHUNK, mixing, 0, unroll=4)
+    lax.fori_loop(0, CHUNK, mixing, 0, unroll=8)
     row = lax.broadcasted_iota(jnp.int32, (tokens, tokens), 0) // CHUNK
     col = lax.broadcasted_iota(jnp.int32, (tokens, tokens), 1) // CHUNK
     mz_t = jnp.where(row == col, jnp.concatenate([d_scr[...]] * chunks, axis=0), 0.0)
@@ -268,7 +268,7 @@
         term = group_lane(dz, i) * d_scr[pl.ds(i, 1), :] + group_lane(probs, i) * e_scr[pl.ds(i, 1), :]
         return total + jnp.exp(gap) * term
 
-    total = lax.fori_loop(0, CHUNK, onward, jnp.zeros_like(levels), unroll=4)
+    total = lax.fori_loop(0, CHUNK, onward, jnp.zeros_like(levels), unroll=8)
     cross = dot3(zst, split2(qk), 1, 0) + dot3(pst, split2(gv_n), 1, 0)
     for c in range(1, chunks):
         total += x_scr[(c - 1) * SLOTS : c * SLOTS] * cross[(c - 1) * SLOTS : c * SLOTS]
@@ -663,7 +663,7 @@
     )
     hidden = mine(x).astype(f32) + matmul(normed_heads, w_heads, 1, 1)
     unit_two, factor_two, scaled_two = rms_parts(hidden, norm2_gain)
-    normed2 = gather_in_parts(scaled_two, count)
+    normed2 = gather_in_parts(scaled_two, 1)
     pre = matmul(normed2, w_gu)
     gate_pre, up_pre = pre[:, :hidden_units], pre[:, hidden_units:]
     gate_sig = jax.nn.sigmoid(gate_pre)

time: 664 us -> 652 us (0.982)
  starting transfers between devices: 76.7 us -> 58.7 us
  waiting for transfers between devices: 204 us -> 214 us
    ppermute x18 -> x6, starting transfers between devices: 27 us -> 11.1 us  [line_gather(): value = lax.ppermute(moving[to][c], axis, [(i, i + to) for i in sources])]
    ppermute x18 -> x6, waiting for transfers between devices: 22.6 us -> 34 us  [line_gather(): value = lax.ppermute(moving[to][c], axis, [(i, i + to) for i in sources])]
  transfers between devices with their start and end apart: 68 -> 56, of which waited for: 30 -> 30; matrix products, arithmetic and copies ran while one was open for 35% -> 36% of each run, Pallas kernels for 7% -> 7%
where the time goes in v4:
time: 652 us; the launch traced here: 644 us
  waiting for transfers between devices  214 us (33%)
  matrix products  115 us (18%)
  local copies, waits for them, and re-layouts  108 us (17%)
  other arithmetic  77.8 us (12%)
  starting transfers between devices  58.7 us (9%)
  Pallas kernels  46 us (7%)
  between operations  15.9 us (2%)
  blocking collectives  8.09 us (1%)
    dot_general x14, matrix products, matmul(): lax.dot_general(a, b, (((ca,), (cb,)), ((), ())), preferred_element_type=...  115 us
    ppermute x12, waiting for transfers between devices, from_partner(): lax.ppermute(array, 'tp', [(i, i ^ distance) for i in range(members)])  86.5 us
    ppermute x6, waiting for transfers between devices, line_gather(): value = lax.ppermute(moving[to][c], axis, [(i, i + to) for i in sources])  34 us
    unnamed x178, local copies, waits for them, and re-layouts  28.5 us
    convert_element_type x12, other arithmetic, add(): return row_major((a.astype(f32) + b.astype(f32)).astype(dtype))  28.2 us
    pallas_call x1, Pallas kernels, run_backward(): pl.pallas_call(backward_kernel, grid=(count,), in_specs=[own(0), own(1),...  26.8 us
    ppermute x2, waiting for transfers between devices, exchange(): far = lax.ppermute(joined.astype(bf16), 'ctx', pairs).astype(f32)  25.2 us
    squeeze x17, local copies, waits for them, and re-layouts, pick(): return lax.dynamic_index_in_dim(value, index, axis, keepdims=False)  24.8 us
  transfers between devices with their start and end apart: 56, of which 30 were waited for; matrix products, arithmetic and copies ran while one was open for 36% of the time, Pallas kernels for 7%

profile of v4, /device:TPU:0, one launch (start us, length us, event | category | flops | bytes accessed | tf_op | source)
XLA Modules:
  0.0 643.8 jit_solution(15073318306044487057)
XLA Ops:
  12.4 5.1 collective-permute-start.8
  18.2 6.6 %collective-permute-done.8 = bf16[256,512]{0,1:T(8,128)(2,1)S(1)} collective-permute-done((bf16[256,512]{0,1:T(8,128)(2,1)S(1)}, bf16[256,512]{0,1:T(8,128)(2,1)S(1)}, u32[]{:S(2)}, u32[]{:S(2)}) %collective-permute-start.8) | collective-permute-done | bytes 262176 | tf_op jit(solution)/shard_map/ppermute | solution.py:574
  24.8 15.0 %collective-permute-done.7 = bf16[256,512]{0,1:T(8,128)(2,1)S(1)} collective-permute-done((bf16[256,512]{0,1:T(8,128)(2,1)S(1)}, bf16[256,512]{0,1:T(8,128)(2,1)S(1)}, u32[]{:S(2)}, u32[]{:S(2)}) %collective-permute-start.7) | collective-permute-done | bytes 262176 | tf_op jit(solution)/shard_map/ppermute | solution.py:574
  43.4 8.1 %all-gather.1 = s32[4,2,3]{2,1,0:T(2,128)S(1)} all-gather(s32[1,2,3]{2,1,0:T(2,128)S(1)} %add_bitcast_fusion), channel_id=2, replica_groups=mesh['dp'=2,'ctx'=4,'tp'=4] {'ctx'}, dimensions={0}, use_global_device_ids=true | all-gather | bytes 120 | tf_op jit(solution)/shard_map/all_gather | solution.py:587
  58.8 3.4 convert_multiply_fusion.2
  63.1 3.7 fusion.52
  70.0 9.8 %fusion.21 = bf16[768,1536]{1,0:T(8,128)(2,1)S(1)} fusion(bf16[2048,1600]{0,1:T(8,128)(2,1)} %all-gather.8.cloned.1.call-done, f32[768,2048]{1,0:T(8,128)} %convert_multiply_fusion.2, f32[2048]{0:T(1024)S(1)} %copy-done.75), kind=kOutput, calls=%fused_computation.45 | convolution fusion | flops 4836163584 | bytes 14950400 | tf_op jit(solution)/shard_map/dot_general | solution.py:443
  83.9 13.8 %collective-permute-done.1 = f32[3,64,128]{2,1,0:T(8,128)S(1)} collective-permute-done((f32[3,64,128]{2,1,0:T(8,128)S(1)}, f32[3,64,128]{2,1,0:T(8,128)S(1)}, u32[]{:S(2)}, u32[]{:S(2)}) %collective-permute-start.1) | collective-permute-done | bytes 98336 | tf_op jit(solution)/shard_map/ppermute | solution.py:606
  100.4 3.6 collective-permute-start.2
  105.4 16.2 %collective-permute-done.2 = bf16[3,64,1024]{2,1,0:T(8,128)(2,1)S(1)} collective-permute-done((bf16[3,64,1024]{2,1,0:T(8,128)(2,1)}, bf16[3,64,1024]{2,1,0:T(8,128)(2,1)S(1)}, u32[]{:S(2)}, u32[]{:S(2)}) %collective-permute-start.2) | collective-permute-done | bytes 393248 | tf_op jit(solution)/shard_map/ppermute | solution.py:621
  125.6 13.1 %shard_map.255 = (bf16[4,3,64,512]{3,2,1,0:T(8,128)(2,1)S(1)}, f32[768,512]{1,0:T(8,128)S(1)}, f32[64,768]{1,0:T(8,128)S(1)}, f32[64,768]{1,0:T(8,128)S(1)}, f32[3,256,256]{2,1,0:T(8,128)S(1)}) custom-call(bf16[4,3,64,1536]{3,2,1,0:T(8,128)(2,1)S(1)} %bitcast.243, bf16[4,3,64,1536]{3,2,1,0:T(8,128)(2,1)S(1)} %bitcast.244, ...), custom_call_target="tpu_custom_call" | custom-call | flops 3000000000 | bytes 9000000 | tf_op jit(solution)/shard_map/pallas_call | solution.py:365
  146.5 5.3 collective-permute-done.5
  151.8 9.9 %collective-permute-done.4 = bf16[192,512]{1,0:T(8,128)(2,1)S(1)} collective-permute-done((bf16[192,512]{1,0:T(8,128)(2,1)S(1)}, bf16[192,512]{1,0:T(8,128)(2,1)S(1)}, u32[]{:S(2)}, u32[]{:S(2)}) %collective-permute-start.4) | collective-permute-done | bytes 196640 | tf_op jit(solution)/shard_map/ppermute | solution.py:574
  162.4 5.6 multiply_reduce_fusion.2
  170.6 5.5 collective-permute-start.9
  176.1 4.9 copy.114
  181.0 9.1 %collective-permute-done.10 = bf16[192,2048]{1,0:T(8,128)(2,1)} collective-permute-done((bf16[192,2048]{1,0:T(8,128)(2,1)}, bf16[192,2048]{1,0:T(8,128)(2,1)}, u32[]{:S(2)}, u32[]{:S(2)}) %collective-permute-start.10) | collective-permute-done | bytes 786464 | tf_op jit(solution)/shard_map/ppermute | solution.py:472
  198.4 11.5 %collective-permute-done.12 = bf16[192,2048]{1,0:T(8,128)(2,1)S(1)} collective-permute-done((bf16[192,2048]{1,0:T(8,128)(2,1)}, bf16[192,2048]{1,0:T(8,128)(2,1)S(1)}, u32[]{:S(2)}, u32[]{:S(2)}) %collective-permute-start.12) | collective-permute-done | bytes 786464 | tf_op jit(solution)/shard_map/ppermute | solution.py:472
  215.1 13.4 %collective-permute-done.14 = bf16[192,2048]{1,0:T(8,128)(2,1)S(1)} collective-permute-done((bf16[192,2048]{1,0:T(8,128)(2,1)S(1)}, bf16[192,2048]{1,0:T(8,128)(2,1)S(1)}, u32[]{:S(2)}, u32[]{:S(2)}) %collective-permute-start.14) | collective-permute-done | bytes 786464 | tf_op jit(solution)/shard_map/ppermute | solution.py:472
  230.7 13.3 %fusion.2 = f32[768,2816]{0,1:T(8,128)S(1)} fusion(bf16[768,2048]{1,0:T(8,128)(2,1)} %bitcast.39, bf16[2048,4224]{0,1:T(8,128)(2,1)} %all-gather.12.cloned.1.call-done), kind=kOutput, calls=%fused_computation.4 | convolution fusion | flops 8858370048 | bytes 23330816 | tf_op jit(solution)/shard_map/dot_general | solution.py:443
  244.0 9.3 %fusion.18 = (bf16[768,1408]{0,1:T(8,128)(2,1)S(1)}, bf16[768,1408]{0,1:T(8,128)(2,1)S(1)}, bf16[768,1408]{0,1:T(8,128)(2,1)}) fusion(f32[768,2816]{0,1:T(8,128)S(1)} %fusion.2, bf16[768,2048]{1,0:T(8,128)(2,1)S(1)} %bitcast.271, bf16[2048,4224]{0,1:T(8,128)(2,1)} %all-gather.12.cloned.1.call-done), kind=kOutput, calls=%fused_computation.38 | convolution fusion | flops 4445405184 | bytes 24051712 | tf_op jit(solution)/shard_map/dot_general | solution.py:443
  255.3 13.5 %fusion.27 = bf16[768,2048]{1,0:T(8,128)(2,1)} fusion(bf16[2048,4224]{0,1:T(8,128)(2,1)} %all-gather.12.cloned.1.call-done, bf16[768,1408]{0,1:T(8,128)(2,1)S(1)} %get-tuple-element.173, bf16[768,1408]{0,1:T(8,128)(2,1)S(1)} %get-tuple-element.172), kind=kOutput, calls=%fused_computation.47 | convolution fusion | flops 8868593664 | bytes 19005440 | tf_op jit(solution)/shard_map/dot_general | solution.py:443
  269.1 14.7 %convolution_convert_fusion = bf16[2048,2816]{1,0:T(8,128)(2,1)} fusion(bf16[768,2048]{1,0:T(8,128)(2,1)} %bitcast.39, bf16[768,1408]{0,1:T(8,128)(2,1)} %copy-done.83, bf16[768,1408]{0,1:T(8,128)(2,1)} %copy-done.82), kind=kOutput, calls=%fused_computation.1 | convolution fusion | flops 8872787968 | bytes 19005440 | tf_op jit(solution)/shard_map/dot_general | solution.py:443
  283.7 9.4 %dynamic-slice_bitcast_fusion = (bf16[2,2,256,2816]{3,2,1,0:T(8,128)(2,1)}, bf16[2,2,256,2816]{3,2,1,0:T(8,128)(2,1)}) fusion(bf16[2,2,2,256,2816]{4,3,2,1,0:T(8,128)(2,1)} %bitcast.267, s32[]{:T(128)S(6)} %select_n.265, s32[]{:T(128)S(6)} %select_n.264), kind=kLoop, calls=%fused_computation.23 | loop fusion | bytes 23068680 | tf_op jit(solution)/shard_map/jit(dynamic_index_in_dim)/squeeze | solution.py:524
  293.6 7.5 %convolution_convert_fusion.2 = bf16[1408,2048]{0,1:T(8,128)(2,1)S(1)} fusion(bf16[768,1408]{0,1:T(8,128)(2,1)} %get-tuple-element.176, bf16[768,2048]{1,0:T(8,128)(2,1)} %bitcast.268), kind=kOutput, calls=%fused_computation.11 | convolution fusion | flops 4432068608 | bytes 11075584 | tf_op jit(solution)/shard_map/dot_general | solution.py:443
  304.5 9.2 %fusion.24 = bf16[768,2048]{1,0:T(8,128)(2,1)} fusion(bf16[768,1408]{0,1:T(8,128)(2,1)S(1)} %copy-done.81, bf16[2048,4224]{0,1:T(8,128)(2,1)} %all-gather.12.cloned.1.call-done), kind=kOutput, calls=%fused_computation.46 | convolution fusion | flops 4430757888 | bytes 11075584 | tf_op jit(solution)/shard_map/dot_general | solution.py:443
  314.0 16.0 %reduce-scatter.4.cloned.1.call-done = bf16[192,2048]{1,0:T(8,128)(2,1)} async-done(((bf16[768,2048]{1,0:T(8,128)(2,1)}), bf16[192,2048]{1,0:T(8,128)(2,1)}) %reduce-scatter.4.cloned.1.call-update) | async-done | bytes 786448 | tf_op jit(solution)/shard_map/reduce_scatter | solution.py:512
  333.5 6.6 %convolution_convert_fusion.4 = bf16[192,2048]{1,0:T(8,128)(2,1)S(1)} fusion(bf16[192,2048]{1,0:T(8,128)(2,1)S(1)} %fusion.89, bf16[2048,2048]{0,1:T(8,128)(2,1)} %all-gather.10.cloned.1.call-done), kind=kOutput, calls=%fused_computation.60 | convolution fusion | flops 1611005952 | bytes 9961472 | tf_op jit(solution)/shard_map/dot_general | solution.py:443
  344.7 5.7 add_convert_fusion
  362.4 6.0 collective-permute-done.17
  370.1 10.3 %collective-permute-done.18 = bf16[192,512]{1,0:T(8,128)(2,1)S(1)} collective-permute-done((bf16[192,512]{1,0:T(8,128)(2,1)S(1)}, bf16[192,512]{1,0:T(8,128)(2,1)S(1)}, u32[]{:S(2)}, u32[]{:S(2)}) %collective-permute-start.18) | collective-permute-done | bytes 196640 | tf_op jit(solution)/shard_map/ppermute | solution.py:574
  381.9 26.8 %shard_map.256 = (bf16[4,3,64,512]{3,2,1,0:T(8,128)(2,1)S(1)}, f32[768,512]{1,0:T(8,128)}, f32[768,512]{1,0:T(8,128)}, f32[64,768]{1,0:T(8,128)S(1)}, f32[64,768...) custom-call(bf16[4,3,64,1536]{3,2,1,0:T(8,128)(2,1)} %bitcast.246, ...), custom_call_target="tpu_custom_call" | custom-call | flops 8999999488 | bytes 15000000 | tf_op jit(solution)/shard_map/pallas_call | solution.py:392
  430.3 4.2 collective-permute-done.44
  437.0 8.9 %collective-permute-done.23 = bf16[3,64,1024]{2,1,0:T(8,128)(2,1)S(1)} collective-permute-done((bf16[3,64,1024]{2,1,0:T(8,128)(2,1)S(1)}, bf16[3,64,1024]{2,1,0:T(8,128)(2,1)S(1)}, u32[]{:S(2)}, u32[]{:S(2)}) %collective-permute-start.23) | collective-permute-done | bytes 393248 | tf_op jit(solution)/shard_map/ppermute | solution.py:621
  446.2 4.2 shard_map.257
  454.5 7.2 %fusion.8 = f32[768,2048]{1,0:T(8,128)S(1)} fusion(bf16[2048,1600]{0,1:T(8,128)(2,1)} %all-gather.8.cloned.1.call-done, bf16[768,512]{1,0:T(8,128)(2,1)S(1)} %bitcast.256, bf16[768,512]{1,0:T(8,128)(2,1)S(1)} %bitcast.254, bf16[768,512]{1,0:T(8,128)(2,1)S(1)} %bitcast.252), kind=kOutput, calls=%fused_computation.25 | convolution fusion | flops 4838916096 | bytes 14942208 | tf_op jit(solution)/shard_map/dot_general | solution.py:443
  461.7 3.7 add_convert_fusion.2
  465.4 5.4 fusion.4
  477.7 8.9 %convolution_convert_fusion.1 = bf16[2048,1600]{1,0:T(8,128)(2,1)S(1)} fusion(bf16[768,1600]{1,0:T(8,128)(2,1)} %pad_maximum_fusion.3, f32[768,2048]{1,0:T(8,128)} %convert_multiply_fusion.2, f32[2048]{0:T(1024)S(1)} %copy-done.76), kind=kOutput, calls=%fused_computation.10 | convolution fusion | flops 5039587328 | bytes 15310848 | tf_op jit(solution)/shard_map/dot_general | solution.py:443
  486.6 3.4 constant_dynamic-slice_fusion.4
  490.0 5.5 copy.122
  503.8 8.2 %collective-permute-done.38 = bf16[128,2048]{1,0:T(8,128)(2,1)S(1)} collective-permute-done((bf16[128,2048]{1,0:T(8,128)(2,1)S(1)}, bf16[128,2048]{1,0:T(8,128)(2,1)S(1)}, u32[]{:S(2)}, u32[]{:S(2)}) %collective-permute-start.38) | collective-permute-done | bytes 524320 | tf_op jit(solution)/shard_map/ppermute | solution.py:557
  521.0 20.0 %collective-permute-done.41 = bf16[256,512]{1,0:T(8,128)(2,1)S(1)} collective-permute-done((bf16[256,512]{1,0:T(8,128)(2,1)S(1)}, bf16[256,512]{1,0:T(8,128)(2,1)S(1)}, u32[]{:S(2)}, u32[]{:S(2)}) %collective-permute-start.41) | collective-permute-done | bytes 262176 | tf_op jit(solution)/shard_map/ppermute | solution.py:574
  541.0 4.1 multiply_reduce_fusion
  547.1 13.3 %collective-permute-done.42 = bf16[256,512]{1,0:T(8,128)(2,1)S(1)} collective-permute-done((bf16[256,512]{1,0:T(8,128)(2,1)S(1)}, bf16[256,512]{1,0:T(8,128)(2,1)S(1)}, u32[]{:S(2)}, u32[]{:S(2)}) %collective-permute-start.42) | collective-permute-done | bytes 262176 | tf_op jit(solution)/shard_map/ppermute | solution.py:574
  563.6 3.7 add_convert_fusion.6
  574.8 4.6 copy.124
  619.5 6.3 collective-permute-done.35
  (431 shorter events, 204.4 us)
Async XLA Ops:
  7.2 55.9 %all-gather.8.cloned.1.call-start = ((), (), s32[]{:S(2)}) async-start(), calls=%async_computation.3 | async-start | bytes 7372800 | tf_op jit(solution)/shard_map/all_gather | solution.py:518
  12.3 149.3 %all-gather.10.cloned.1.call-start = ((), (), s32[]{:S(2)}) async-start(), calls=%async_computation.4 | async-start | bytes 9437184 | tf_op jit(solution)/shard_map/all_gather | solution.py:518
  12.4 12.4 %collective-permute-start.8 = (bf16[256,512]{0,1:T(8,128)(2,1)S(1)}, bf16[256,512]{0,1:T(8,128)(2,1)S(1)}, u32[]{:S(2)}, u32[]{:S(2)}) collective-permute-start(bf16[256,512]{0,1:T(8,128)(2,1)S(1)} %bitcast.286), channel_id=1, source_target_pairs={{0,3},{1,2},{2,1},{3,0},{4,7},{5,6},{6,5},{7,4},{8,11},{9,10},{10,... | collective-permute-start | bytes 786440 | tf_op jit(solution)/shard_map/ppermute | solution.py:574
  17.5 22.3 %collective-permute-start.7 = (bf16[256,512]{0,1:T(8,128)(2,1)S(1)}, bf16[256,512]{0,1:T(8,128)(2,1)S(1)}, u32[]{:S(2)}, u32[]{:S(2)}) collective-permute-start(bf16[256,512]{0,1:T(8,128)(2,1)S(1)} %bitcast.287), channel_id=1, source_target_pairs={{0,2},{1,3},{2,0},{3,1},{4,6},{5,7},{6,4},{7,5},{8,10},{9,11},{10,... | collective-permute-start | bytes 786440 | tf_op jit(solution)/shard_map/ppermute | solution.py:574
  17.5 22.3 %collective-permute-start.6 = (bf16[256,512]{0,1:T(8,128)(2,1)S(1)}, bf16[256,512]{0,1:T(8,128)(2,1)S(1)}, u32[]{:S(2)}, u32[]{:S(2)}) collective-permute-start(bf16[256,512]{0,1:T(8,128)(2,1)S(1)} %bitcast.288), channel_id=1, source_target_pairs={{0,1},{1,0},{2,3},{3,2},{4,5},{5,4},{6,7},{7,6},{8,9},{9,8},{10,11... | collective-permute-start | bytes 786440 | tf_op jit(solution)/shard_map/ppermute | solution.py:574
  40.9 189.8 %all-gather.12.cloned.1.call-start = ((), (), s32[]{:S(2)}) async-start(), calls=%async_computation.5 | async-start | bytes 19464192 | tf_op jit(solution)/shard_map/all_gather | solution.py:518
  43.1 286.9 %reduce-scatter.4.cloned.1.call-start = ((), (), s32[]{:S(2)}) async-start(), calls=%async_computation.6 | async-start | bytes 3932160 | tf_op jit(solution)/shard_map/reduce_scatter | solution.py:512
  81.8 16.8 %collective-permute-start = (bf16[3,64,1024]{2,1,0:T(8,128)(2,1)S(1)}, bf16[3,64,1024]{2,1,0:T(8,128)(2,1)S(1)}, u32[]{:S(2)}, u32[]{:S(2)}) collective-permute-start(bf16[3,64,1024]{2,1,0:T(8,128)(2,1)S(1)} %get-tuple-element.60), channel_id=1, source_target_pairs={{0,4},{4,0},{8,12},{12,8},{1,5},{5,1},{9,13},{13,9},{2,6},{6,2},{1... | collective-permute-start | bytes 1179656 | tf_op jit(solution)/shard_map/ppermute | solution.py:616
  83.2 14.5 %collective-permute-start.1 = (f32[3,64,128]{2,1,0:T(8,128)S(1)}, f32[3,64,128]{2,1,0:T(8,128)S(1)}, u32[]{:S(2)}, u32[]{:S(2)}) collective-permute-start(f32[3,64,128]{2,1,0:T(8,128)S(1)} %get-tuple-element.61), channel_id=1, source_target_pairs={{0,4},{4,0},{8,12},{12,8},{1,5},{5,1},{9,13},{13,9},{2,6},{6,2},{1... | collective-permute-start | bytes 294920 | tf_op jit(solution)/shard_map/ppermute | solution.py:606
  100.4 21.2 %collective-permute-start.2 = (bf16[3,64,1024]{2,1,0:T(8,128)(2,1)}, bf16[3,64,1024]{2,1,0:T(8,128)(2,1)S(1)}, u32[]{:S(2)}, u32[]{:S(2)}) collective-permute-start(bf16[3,64,1024]{2,1,0:T(8,128)(2,1)} %fusion.57), channel_id=1, source_target_pairs={{0,8},{4,12},{1,9},{5,13},{2,10},{6,14},{3,11},{7,15},{16,24},{20,... | collective-permute-start | bytes 1179656 | tf_op jit(solution)/shard_map/ppermute | solution.py:621
  145.4 16.2 %collective-permute-start.4 = (bf16[192,512]{1,0:T(8,128)(2,1)S(1)}, bf16[192,512]{1,0:T(8,128)(2,1)S(1)}, u32[]{:S(2)}, u32[]{:S(2)}) collective-permute-start(bf16[192,512]{1,0:T(8,128)(2,1)S(1)} %get-tuple-element.210), channel_id=1, source_target_pairs={{0,2},{1,3},{2,0},{3,1},{4,6},{5,7},{6,4},{7,5},{8,10},{9,11},{10,... | collective-permute-start | bytes 589832 | tf_op jit(solution)/shard_map/ppermute | solution.py:574
  145.4 16.2 %collective-permute-start.3 = (bf16[192,512]{1,0:T(8,128)(2,1)S(1)}, bf16[192,512]{1,0:T(8,128)(2,1)S(1)}, u32[]{:S(2)}, u32[]{:S(2)}) collective-permute-start(bf16[192,512]{1,0:T(8,128)(2,1)S(1)} %get-tuple-element.211), channel_id=1, source_target_pairs={{0,1},{1,0},{2,3},{3,2},{4,5},{5,4},{6,7},{7,6},{8,9},{9,8},{10,11... | collective-permute-start | bytes 589832 | tf_op jit(solution)/shard_map/ppermute | solution.py:574
  169.3 20.8 %collective-permute-start.10 = (bf16[192,2048]{1,0:T(8,128)(2,1)}, bf16[192,2048]{1,0:T(8,128)(2,1)}, u32[]{:S(2)}, u32[]{:S(2)}) collective-permute-start(bf16[192,2048]{1,0:T(8,128)(2,1)} %multiply_convert_fusion.2), channel_id=1, source_target_pairs={{1,0},{2,1},{3,2},{5,4},{6,5},{7,6},{9,8},{10,9},{11,10},{13,12},{... | collective-permute-start | bytes 2359304 | tf_op jit(solution)/shard_map/ppermute | solution.py:472
  170.6 20.8 %collective-permute-start.9 = (bf16[192,2048]{1,0:T(8,128)(2,1)}, bf16[192,2048]{1,0:T(8,128)(2,1)}, u32[]{:S(2)}, u32[]{:S(2)}) collective-permute-start(bf16[192,2048]{1,0:T(8,128)(2,1)} %multiply_convert_fusion.2), channel_id=1, source_target_pairs={{0,1},{1,2},{2,3},{4,5},{5,6},{6,7},{8,9},{9,10},{10,11},{12,13},{... | collective-permute-start | bytes 2359304 | tf_op jit(solution)/shard_map/ppermute | solution.py:472
  190.1 19.7 %collective-permute-start.12 = (bf16[192,2048]{1,0:T(8,128)(2,1)}, bf16[192,2048]{1,0:T(8,128)(2,1)S(1)}, u32[]{:S(2)}, u32[]{:S(2)}) collective-permute-start(bf16[192,2048]{1,0:T(8,128)(2,1)} %collective-permute-done.10), channel_id=1, source_target_pairs={{1,0},{2,1},{5,4},{6,5},{9,8},{10,9},{13,12},{14,13},{17,16},{18,1... | collective-permute-start | bytes 2359304 | tf_op jit(solution)/shard_map/ppermute | solution.py:472
  191.4 19.7 %collective-permute-start.11 = (bf16[192,2048]{1,0:T(8,128)(2,1)}, bf16[192,2048]{1,0:T(8,128)(2,1)S(1)}, u32[]{:S(2)}, u32[]{:S(2)}) collective-permute-start(bf16[192,2048]{1,0:T(8,128)(2,1)} %collective-permute-done.9), channel_id=1, source_target_pairs={{1,2},{2,3},{5,6},{6,7},{9,10},{10,11},{13,14},{14,15},{17,18},{18... | collective-permute-start | bytes 2359304 | tf_op jit(solution)/shard_map/ppermute | solution.py:472
  209.8 18.7 %collective-permute-start.14 = (bf16[192,2048]{1,0:T(8,128)(2,1)S(1)}, bf16[192,2048]{1,0:T(8,128)(2,1)S(1)}, u32[]{:S(2)}, u32[]{:S(2)}) collective-permute-start(bf16[192,2048]{1,0:T(8,128)(2,1)S(1)} %collective-permute-done.12), channel_id=1, source_target_pairs={{1,0},{5,4},{9,8},{13,12},{17,16},{21,20},{25,24},{29,28}} | collective-permute-start | bytes 2359304 | tf_op jit(solution)/shard_map/ppermute | solution.py:472
  268.9 142.0 %reduce-scatter.6.cloned.1.call-start = ((), (), s32[]{:S(2)}) async-start(), calls=%async_computation.7 | async-start | bytes 3932160 | tf_op jit(solution)/shard_map/reduce_scatter | solution.py:512
  293.1 47.0 %collective-permute-start.15 = (bf16[2,2,256,2816]{3,2,1,0:T(8,128)(2,1)}, bf16[2,2,256,2816]{3,2,1,0:T(8,128)(2,1)}, u32[]{:S(2)}, u32[]{:S(2)}) collective-permute-start(bf16[2,2,256,2816]{3,2,1,0:T(8,128)(2,1)} %get-tuple-element.174), channel_id=1, source_target_pairs={{0,16},{16,0},{1,17},{17,1},{2,18},{18,2},{3,19},{19,3},{4,20},{20... | collective-permute-start | bytes 17301512 | tf_op jit(solution)/shard_map/ppermute | solution.py:533
  304.1 36.0 %collective-permute-start.16 = (bf16[2,2,256,1408]{3,2,1,0:T(8,128)(2,1)}, bf16[2,2,256,1408]{3,2,1,0:T(8,128)(2,1)}, u32[]{:S(2)}, u32[]{:S(2)}) collective-permute-start(bf16[2,2,256,1408]{3,2,1,0:T(8,128)(2,1)} %get-tuple-element.181), channel_id=1, source_target_pairs={{0,16},{16,0},{1,17},{17,1},{2,18},{18,2},{3,19},{19,3},{4,20},{20... | collective-permute-start | bytes 8650760 | tf_op jit(solution)/shard_map/ppermute | solution.py:533
  313.7 163.7 %all-gather.14.cloned.1.call-start = ((), (), s32[]{:S(2)}) async-start(), calls=%async_computation.8 | async-start | bytes 3932160 | tf_op jit(solution)/shard_map/all_gather | solution.py:515
  340.2 41.6 %collective-permute-start.19 = (bf16[192,512]{1,0:T(8,128)(2,1)S(1)}, bf16[192,512]{1,0:T(8,128)(2,1)S(1)}, u32[]{:S(2)}, u32[]{:S(2)}) collective-permute-start(bf16[192,512]{1,0:T(8,128)(2,1)S(1)} %get-tuple-element.205), channel_id=1, source_target_pairs={{0,3},{1,2},{2,1},{3,0},{4,7},{5,6},{6,5},{7,4},{8,11},{9,10},{10,... | collective-permute-start | bytes 589832 | tf_op jit(solution)/shard_map/ppermute | solution.py:574
  342.4 37.9 %collective-permute-start.18 = (bf16[192,512]{1,0:T(8,128)(2,1)S(1)}, bf16[192,512]{1,0:T(8,128)(2,1)S(1)}, u32[]{:S(2)}, u32[]{:S(2)}) collective-permute-start(bf16[192,512]{1,0:T(8,128)(2,1)S(1)} %get-tuple-element.206), channel_id=1, source_target_pairs={{0,2},{1,3},{2,0},{3,1},{4,6},{5,7},{6,4},{7,5},{8,10},{9,11},{10,... | collective-permute-start | bytes 589832 | tf_op jit(solution)/shard_map/ppermute | solution.py:574
  342.8 25.6 %collective-permute-start.17 = (bf16[192,512]{1,0:T(8,128)(2,1)S(1)}, bf16[192,512]{1,0:T(8,128)(2,1)S(1)}, u32[]{:S(2)}, u32[]{:S(2)}) collective-permute-start(bf16[192,512]{1,0:T(8,128)(2,1)S(1)} %get-tuple-element.207), channel_id=1, source_target_pairs={{0,1},{1,0},{2,3},{3,2},{4,5},{5,4},{6,7},{7,6},{8,9},{9,8},{10,11... | collective-permute-start | bytes 589832 | tf_op jit(solution)/shard_map/ppermute | solution.py:574
  352.6 58.2 %collective-permute-start.21 = (bf16[2,128,2816]{2,1,0:T(8,128)(2,1)}, bf16[2,128,2816]{2,1,0:T(8,128)(2,1)}, u32[]{:S(2)}, u32[]{:S(2)}) collective-permute-start(bf16[2,128,2816]{2,1,0:T(8,128)(2,1)} %get-tuple-element.191), channel_id=1, source_target_pairs={{0,8},{8,0},{4,12},{12,4},{1,9},{9,1},{5,13},{13,5},{2,10},{10,2},... | collective-permute-start | bytes 4325384 | tf_op jit(solution)/shard_map/ppermute | solution.py:546
  358.1 203.4 %collective-permute-start.26 = (bf16[2,128,1408]{2,1,0:T(8,128)(2,1)}, bf16[2,128,1408]{2,1,0:T(8,128)(2,1)}, u32[]{:S(2)}, u32[]{:S(2)}) collective-permute-start(bf16[2,128,1408]{2,1,0:T(8,128)(2,1)} %get-tuple-element.198), channel_id=1, source_target_pairs={{0,8},{8,0},{4,12},{12,4},{1,9},{9,1},{5,13},{13,5},{2,10},{10,2},... | collective-permute-start | bytes 2162696 | tf_op jit(solution)/shard_map/ppermute | solution.py:546
  368.4 42.5 %collective-permute-start.20 = (bf16[2,128,2816]{2,1,0:T(8,128)(2,1)}, bf16[2,128,2816]{2,1,0:T(8,128)(2,1)}, u32[]{:S(2)}, u32[]{:S(2)}) collective-permute-start(bf16[2,128,2816]{2,1,0:T(8,128)(2,1)} %get-tuple-element.193), channel_id=1, source_target_pairs={{0,4},{4,0},{8,12},{12,8},{1,5},{5,1},{9,13},{13,9},{2,6},{6,2},{1... | collective-permute-start | bytes 4325384 | tf_op jit(solution)/shard_map/ppermute | solution.py:545
  380.3 181.2 %collective-permute-start.25 = (bf16[2,128,1408]{2,1,0:T(8,128)(2,1)}, bf16[2,128,1408]{2,1,0:T(8,128)(2,1)}, u32[]{:S(2)}, u32[]{:S(2)}) collective-permute-start(bf16[2,128,1408]{2,1,0:T(8,128)(2,1)} %get-tuple-element.200), channel_id=1, source_target_pairs={{0,4},{4,0},{8,12},{12,8},{1,5},{5,1},{9,13},{13,9},{2,6},{6,2},{1... | collective-permute-start | bytes 2162696 | tf_op jit(solution)/shard_map/ppermute | solution.py:545
  413.6 148.0 %reduce-scatter.8.cloned.1.call-start = ((), (), s32[]{:S(2)}) async-start(), calls=%async_computation.9 | async-start | bytes 3932160 | tf_op jit(solution)/shard_map/reduce_scatter | solution.py:512
  414.1 14.4 %collective-permute-start.22 = (bf16[3,64,1024]{2,1,0:T(8,128)(2,1)}, bf16[3,64,1024]{2,1,0:T(8,128)(2,1)S(1)}, u32[]{:S(2)}, u32[]{:S(2)}) collective-permute-start(bf16[3,64,1024]{2,1,0:T(8,128)(2,1)} %copy-done.19), channel_id=1, source_target_pairs={{0,4},{4,0},{8,12},{12,8},{1,5},{5,1},{9,13},{13,9},{2,6},{6,2},{1... | collective-permute-start | bytes 1179656 | tf_op jit(solution)/shard_map/ppermute | solution.py:616
  417.0 17.5 %collective-permute-start.44 = (bf16[128,2816]{1,0:T(8,128)(2,1)S(1)}, bf16[128,2816]{1,0:T(8,128)(2,1)S(1)}, u32[]{:S(2)}, u32[]{:S(2)}) collective-permute-start(bf16[128,2816]{1,0:T(8,128)(2,1)S(1)} %dynamic-slice_bitcast_fusion.14), channel_id=1, source_target_pairs={{0,8},{8,0},{4,12},{12,4},{1,9},{9,1},{5,13},{13,5},{2,10},{10,2},... | collective-permute-start | bytes 2162696 | tf_op jit(solution)/shard_map/ppermute | solution.py:557
  423.5 42.0 %collective-permute-start.36 = (bf16[2,2,256,2048]{3,2,1,0:T(8,128)(2,1)}, bf16[2,2,256,2048]{3,2,1,0:T(8,128)(2,1)}, u32[]{:S(2)}, u32[]{:S(2)}) collective-permute-start(bf16[2,2,256,2048]{3,2,1,0:T(8,128)(2,1)} %dynamic-slice_bitcast_fusion.2), channel_id=1, source_target_pairs={{0,16},{16,0},{1,17},{17,1},{2,18},{18,2},{3,19},{19,3},{4,20},{20... | collective-permute-start | bytes 12582920 | tf_op jit(solution)/shard_map/ppermute | solution.py:533
  428.5 72.5 %collective-permute-start.45 = (bf16[128,2816]{1,0:T(8,128)(2,1)}, bf16[128,2816]{1,0:T(8,128)(2,1)}, u32[]{:S(2)}, u32[]{:S(2)}) collective-permute-start(bf16[128,2816]{1,0:T(8,128)(2,1)} %dynamic-slice_bitcast_fusion.13), channel_id=1, source_target_pairs={{0,4},{4,0},{8,12},{12,8},{1,5},{5,1},{9,13},{13,9},{2,6},{6,2},{1... | collective-permute-start | bytes 2162696 | tf_op jit(solution)/shard_map/ppermute | solution.py:558
  434.5 11.5 %collective-permute-start.23 = (bf16[3,64,1024]{2,1,0:T(8,128)(2,1)S(1)}, bf16[3,64,1024]{2,1,0:T(8,128)(2,1)S(1)}, u32[]{:S(2)}, u32[]{:S(2)}) collective-permute-start(bf16[3,64,1024]{2,1,0:T(8,128)(2,1)S(1)} %fusion.61), channel_id=1, source_target_pairs={{8,0},{12,4},{9,1},{13,5},{10,2},{14,6},{11,3},{15,7},{24,16},{28,... | collective-permute-start | bytes 1179656 | tf_op jit(solution)/shard_map/ppermute | solution.py:621
  472.6 23.0 %collective-permute-start.37 = (bf16[2,128,2048]{2,1,0:T(8,128)(2,1)S(1)}, bf16[2,128,2048]{2,1,0:T(8,128)(2,1)}, u32[]{:S(2)}, u32[]{:S(2)}) collective-permute-start(bf16[2,128,2048]{2,1,0:T(8,128)(2,1)S(1)} %dynamic-slice_bitcast_fusion.11), channel_id=1, source_target_pairs={{0,4},{4,0},{8,12},{12,8},{1,5},{5,1},{9,13},{13,9},{2,6},{6,2},{1... | collective-permute-start | bytes 3145736 | tf_op jit(solution)/shard_map/ppermute | solution.py:545
  474.1 23.7 %collective-permute-start.39 = (bf16[2,128,2048]{2,1,0:T(8,128)(2,1)S(1)}, bf16[2,128,2048]{2,1,0:T(8,128)(2,1)}, u32[]{:S(2)}, u32[]{:S(2)}) collective-permute-start(bf16[2,128,2048]{2,1,0:T(8,128)(2,1)S(1)} %dynamic-slice_bitcast_fusion.10), channel_id=1, source_target_pairs={{0,8},{8,0},{4,12},{12,4},{1,9},{9,1},{5,13},{13,5},{2,10},{10,2},... | collective-permute-start | bytes 3145736 | tf_op jit(solution)/shard_map/ppermute | solution.py:546
  477.5 153.3 %all-gather.16.cloned.1.call-start = ((), (), s32[]{:S(2)}) async-start(), calls=%async_computation.10 | async-start | bytes 3932160 | tf_op jit(solution)/shard_map/all_gather | solution.py:515
  495.6 66.0 %collective-permute-start.24 = (bf16[2,2,256,1600]{2,3,1,0:T(8,128)(2,1)}, bf16[2,2,256,1600]{2,3,1,0:T(8,128)(2,1)}, u32[]{:S(2)}, u32[]{:S(2)}) collective-permute-start(bf16[2,2,256,1600]{2,3,1,0:T(8,128)(2,1)} %bitcast.275), channel_id=1, source_target_pairs={{0,16},{16,0},{1,17},{17,1},{2,18},{18,2},{3,19},{19,3},{4,20},{20... | collective-permute-start | bytes 9830408 | tf_op jit(solution)/shard_map/ppermute | solution.py:533
  497.8 14.2 %collective-permute-start.38 = (bf16[128,2048]{1,0:T(8,128)(2,1)S(1)}, bf16[128,2048]{1,0:T(8,128)(2,1)S(1)}, u32[]{:S(2)}, u32[]{:S(2)}) collective-permute-start(bf16[128,2048]{1,0:T(8,128)(2,1)S(1)} %dynamic-slice_bitcast_fusion.20), channel_id=1, source_target_pairs={{0,8},{8,0},{4,12},{12,4},{1,9},{9,1},{5,13},{13,5},{2,10},{10,2},... | collective-permute-start | bytes 1572872 | tf_op jit(solution)/shard_map/ppermute | solution.py:557
  501.0 13.9 %collective-permute-start.40 = (bf16[128,2048]{1,0:T(8,128)(2,1)S(1)}, bf16[128,2048]{1,0:T(8,128)(2,1)S(1)}, u32[]{:S(2)}, u32[]{:S(2)}) collective-permute-start(bf16[128,2048]{1,0:T(8,128)(2,1)S(1)} %dynamic-slice_bitcast_fusion.19), channel_id=1, source_target_pairs={{0,4},{4,0},{8,12},{12,8},{1,5},{5,1},{9,13},{13,9},{2,6},{6,2},{1... | collective-permute-start | bytes 1572872 | tf_op jit(solution)/shard_map/ppermute | solution.py:558
  516.3 24.7 %collective-permute-start.41 = (bf16[256,512]{1,0:T(8,128)(2,1)S(1)}, bf16[256,512]{1,0:T(8,128)(2,1)S(1)}, u32[]{:S(2)}, u32[]{:S(2)}) collective-permute-start(bf16[256,512]{1,0:T(8,128)(2,1)S(1)} %get-tuple-element.202), channel_id=1, source_target_pairs={{0,1},{1,0},{2,3},{3,2},{4,5},{5,4},{6,7},{7,6},{8,9},{9,8},{10,11... | collective-permute-start | bytes 786440 | tf_op jit(solution)/shard_map/ppermute | solution.py:574
  519.5 27.5 %collective-permute-start.43 = (bf16[256,512]{1,0:T(8,128)(2,1)S(1)}, bf16[256,512]{1,0:T(8,128)(2,1)S(1)}, u32[]{:S(2)}, u32[]{:S(2)}) collective-permute-start(bf16[256,512]{1,0:T(8,128)(2,1)S(1)} %get-tuple-element.203), channel_id=1, source_target_pairs={{0,3},{1,2},{2,1},{3,0},{4,7},{5,6},{6,5},{7,4},{8,11},{9,10},{10,... | collective-permute-start | bytes 786440 | tf_op jit(solution)/shard_map/ppermute | solution.py:574
  541.0 19.4 %collective-permute-start.42 = (bf16[256,512]{1,0:T(8,128)(2,1)S(1)}, bf16[256,512]{1,0:T(8,128)(2,1)S(1)}, u32[]{:S(2)}, u32[]{:S(2)}) collective-permute-start(bf16[256,512]{1,0:T(8,128)(2,1)S(1)} %get-tuple-element.204), channel_id=1, source_target_pairs={{0,2},{1,3},{2,0},{3,1},{4,6},{5,7},{6,4},{7,5},{8,10},{9,11},{10,... | collective-permute-start | bytes 786440 | tf_op jit(solution)/shard_map/ppermute | solution.py:574
  567.4 12.1 %collective-permute-start.27 = (f32[4864]{0:T(1024)S(1)}, f32[4864]{0:T(1024)S(1)}, u32[]{:S(2)}, u32[]{:S(2)}) collective-permute-start(f32[4864]{0:T(1024)S(1)} %pad_maximum_fusion.13), channel_id=1, source_target_pairs={{0,16},{16,0},{1,17},{17,1},{2,18},{18,2},{3,19},{19,3},{4,20},{20... | collective-permute-start | bytes 58376 | tf_op jit(solution)/shard_map/ppermute | solution.py:735
  569.6 32.1 %collective-permute-start.46 = (bf16[128,1408]{1,0:T(8,128)(2,1)}, bf16[128,1408]{1,0:T(8,128)(2,1)}, u32[]{:S(2)}, u32[]{:S(2)}) collective-permute-start(bf16[128,1408]{1,0:T(8,128)(2,1)} %dynamic-slice_bitcast_fusion.24), channel_id=1, source_target_pairs={{0,8},{8,0},{4,12},{12,4},{1,9},{9,1},{5,13},{13,5},{2,10},{10,2},... | collective-permute-start | bytes 1081352 | tf_op jit(solution)/shard_map/ppermute | solution.py:557
  573.4 29.6 %collective-permute-start.47 = (bf16[128,1408]{1,0:T(8,128)(2,1)}, bf16[128,1408]{1,0:T(8,128)(2,1)}, u32[]{:S(2)}, u32[]{:S(2)}) collective-permute-start(bf16[128,1408]{1,0:T(8,128)(2,1)} %dynamic-slice_bitcast_fusion.23), channel_id=1, source_target_pairs={{0,4},{4,0},{8,12},{12,8},{1,5},{5,1},{9,13},{13,9},{2,6},{6,2},{1... | collective-permute-start | bytes 1081352 | tf_op jit(solution)/shard_map/ppermute | solution.py:558
  591.4 19.2 %collective-permute-start.34 = (bf16[2,128,1600]{1,2,0:T(8,128)(2,1)}, bf16[2,128,1600]{1,2,0:T(8,128)(2,1)}, u32[]{:S(2)}, u32[]{:S(2)}) collective-permute-start(bf16[2,128,1600]{1,2,0:T(8,128)(2,1)} %bitcast.282), channel_id=1, source_target_pairs={{0,8},{8,0},{4,12},{12,4},{1,9},{9,1},{5,13},{13,5},{2,10},{10,2},... | collective-permute-start | bytes 2457608 | tf_op jit(solution)/shard_map/ppermute | solution.py:546
  597.2 20.4 %collective-permute-start.32 = (bf16[2,128,1600]{1,2,0:T(8,128)(2,1)}, bf16[2,128,1600]{1,2,0:T(8,128)(2,1)}, u32[]{:S(2)}, u32[]{:S(2)}) collective-permute-start(bf16[2,128,1600]{1,2,0:T(8,128)(2,1)} %bitcast.283), channel_id=1, source_target_pairs={{0,4},{4,0},{8,12},{12,8},{1,5},{5,1},{9,13},{13,9},{2,6},{6,2},{1... | collective-permute-start | bytes 2457608 | tf_op jit(solution)/shard_map/ppermute | solution.py:545
  (92 other events, 1004.2 us)
Sparse Core Ops, SparseCore 0:
  12.5 50.5 all-gather.7
  65.5 62.1 all-gather.9
  129.5 101.1 all-gather.11
  269.0 60.9 reduce-scatter.3
  332.2 72.7 reduce-scatter.5
  413.7 63.7 all-gather.13
  479.8 74.7 reduce-scatter.7
  567.5 63.2 all-gather.15

commit v5 on v4

--- a/solution.py
+++ b/solution.py
@@ -164,7 +164,7 @@
         w_scr[j] = w
         return scores + w * d_scr[pl.ds(j, 1), :]
 
-    scores = lax.fori_loop(0, CHUNK, inside, jnp.zeros_like(levels), unroll=8)
+    scores = lax.fori_loop(0, CHUNK, inside, jnp.zeros_like(levels), unroll=16)
     decay = jnp.exp(levels - level_refs(levels) + aux_ref[0, base : base + 1, :])
     for c in range(1, chunks):
         w = levels[:, c * CHUNK - 1 : c * CHUNK] - levels + aux_ref[0, 2 * CHUNK + c : 2 * CHUNK + c + 1, :]
@@ -185,7 +185,7 @@
         d_scr[pl.ds(j, 1), :] = jnp.sum(w_scr[j] * probs, axis=0, keepdims=True)
         return carry
 
-    lax.fori_loop(0, CHUNK, mixing, 0, unroll=8)
+    lax.fori_loop(0, CHUNK, mixing, 0, unroll=16)
     row = lax.broadcasted_iota(jnp.int32, (tokens, tokens), 0) // CHUNK
     col = lax.broadcasted_iota(jnp.int32, (tokens, tokens), 1) // CHUNK
     mixed_t = jnp.where(row == col, jnp.concatenate([d_scr[...]] * chunks, axis=0), 0.0)
@@ -223,7 +223,7 @@
         w_scr[j] = w
         return dp + w * d_scr[pl.ds(j, 1), :]
 
-    dp = lax.fori_loop(0, CHUNK, inside, jnp.zeros_like(levels), unroll=8)
+    dp = lax.fori_loop(0, CHUNK, inside, jnp.zeros_like(levels), unroll=16)
     decay = jnp.exp(levels - level_refs(levels) + aux_ref[0, base : base + 1, :])
     for c in range(1, chunks):
         w = levels[:, c * CHUNK - 1 : c * CHUNK] - levels + aux_ref[0, 2 * CHUNK + c : 2 * CHUNK + c + 1, :]
@@ -243,7 +243,7 @@
         d_scr[pl.ds(j, 1), :] = jnp.sum(w_scr[j] * dz, axis=0, keepdims=True)
         return carry
 
-    lax.fori_loop(0, CHUNK, mixing, 0, unroll=8)
+    lax.fori_loop(0, CHUNK, mixing, 0, unroll=16)
     row = lax.broadcasted_iota(jnp.int32, (tokens, tokens), 0) // CHUNK
     col = lax.broadcasted_iota(jnp.int32, (tokens, tokens), 1) // CHUNK
     mz_t = jnp.where(row == col, jnp.concatenate([d_scr[...]] * chunks, axis=0), 0.0)
@@ -268,7 +268,7 @@
         term = group_lane(dz, i) * d_scr[pl.ds(i, 1), :] + group_lane(probs, i) * e_scr[pl.ds(i, 1), :]
         return total + jnp.exp(gap) * term
 
-    total = lax.fori_loop(0, CHUNK, onward, jnp.zeros_like(levels), unroll=8)
+    total = lax.fori_loop(0, CHUNK, onward, jnp.zeros_like(levels), unroll=16)
     cross = dot3(zst, split2(qk), 1, 0) + dot3(pst, split2(gv_n), 1, 0)
     for c in range(1, chunks):
         total += x_scr[(c - 1) * SLOTS : c * SLOTS] * cross[(c - 1) * SLOTS : c * SLOTS]
@@ -739,10 +739,18 @@
     held_in = scatter_first(held_in)
     rows_wo, rows_wgu, rows_wd = scatter_end(held_wo), scatter_end(held_wgu), scatter_end(held_wd)
     rows_att = scatter_end(scatter_second(held_in))
-    rows_wo = rows_wo[:, :heads] + sum(
-        from_partner(rows_wo[:, r * heads : (r + 1) * heads].astype(bf16), r).astype(f32)
-        for r in range(1, members)
-    )
+    blocks_wo = [rows_wo[:, r * heads : (r + 1) * heads] for r in range(members)]
+    distance = 1
+    while len(blocks_wo) > 1:
+        there = from_partner(jnp.concatenate(blocks_wo[1::2], axis=1).astype(bf16), distance)
+        if 2 * distance == members:
+            there, small = tie(there, small)
+        blocks_wo = [
+            block + there[:, i * heads : (i + 1) * heads].astype(f32)
+            for i, block in enumerate(blocks_wo[::2])
+        ]
+        distance *= 2
+    rows_wo = blocks_wo[0]
     input_grad = natural(input_grad).astype(f32)
     return (
         natural(output).reshape(count, tokens, width),

time: 652 us -> 644 us (0.988)
  waiting for transfers between devices: 214 us -> 201 us
    ppermute x12 -> x11, waiting for transfers between devices: 86.5 us -> 74.3 us  [from_partner(): lax.ppermute(array, 'tp', [(i, i ^ distance) for i in range(members)])]
    ppermute x4, waiting for transfers between devices: 1.11 us -> 9.43 us  [scatter_first(): lax.ppermute(pick(upper, 1 - x_at, 1), 'ctx', swap_x)]
    unnamed x178 -> x182, local copies, waits for them, and re-layouts: 28.5 us -> 27.5 us
    ppermute x12 -> x11, starting transfers between devices: 16.2 us -> 15.6 us  [from_partner(): lax.ppermute(array, 'tp', [(i, i ^ distance) for i in range(members)])]
  transfers between devices with their start and end apart: 56 -> 55, of which waited for: 30 -> 29; matrix products, arithmetic and copies ran while one was open for 36% -> 37% of each run, Pallas kernels for 7% -> 7%
where the time goes in v5:
time: 644 us; the launch traced here: 635 us
  waiting for transfers between devices  201 us (31%)
  matrix products  115 us (18%)
  local copies, waits for them, and re-layouts  111 us (17%)
  other arithmetic  74.4 us (12%)
  starting transfers between devices  63.8 us (10%)
  Pallas kernels  45.3 us (7%)
  between operations  15.9 us (2%)
  blocking collectives  8.09 us (1%)
    dot_general x14, matrix products, matmul(): lax.dot_general(a, b, (((ca,), (cb,)), ((), ())), preferred_element_type=...  115 us
    ppermute x11, waiting for transfers between devices, from_partner(): lax.ppermute(array, 'tp', [(i, i ^ distance) for i in range(members)])  74.3 us
    ppermute x6, waiting for transfers between devices, line_gather(): value = lax.ppermute(moving[to][c], axis, [(i, i + to) for i in sources])  34 us
    convert_element_type x12, other arithmetic, add(): return row_major((a.astype(f32) + b.astype(f32)).astype(dtype))  29.1 us
    unnamed x182, local copies, waits for them, and re-layouts  27.5 us
    squeeze x17, local copies, waits for them, and re-layouts, pick(): return lax.dynamic_index_in_dim(value, index, axis, keepdims=False)  27 us
    pallas_call x1, Pallas kernels, run_backward(): pl.pallas_call(backward_kernel, grid=(count,), in_specs=[own(0), own(1),...  26.1 us
    ppermute x2, waiting for transfers between devices, exchange(): far = lax.ppermute(joined.astype(bf16), 'ctx', pairs).astype(f32)  19.2 us
  transfers between devices with their start and end apart: 55, of which 29 were waited for; matrix products, arithmetic and copies ran while one was open for 37% of the time, Pallas kernels for 7%

profile of v5, /device:TPU:0, one launch (start us, length us, event | category | flops | bytes accessed | tf_op | source)
XLA Modules:
  0.0 634.9 jit_solution(4475857756206982785)
XLA Ops:
  12.4 5.1 collective-permute-start.8
  18.2 6.6 %collective-permute-done.8 = bf16[256,512]{0,1:T(8,128)(2,1)S(1)} collective-permute-done((bf16[256,512]{0,1:T(8,128)(2,1)S(1)}, bf16[256,512]{0,1:T(8,128)(2,1)S(1)}, u32[]{:S(2)}, u32[]{:S(2)}) %collective-permute-start.8) | collective-permute-done | bytes 262176 | tf_op jit(solution)/shard_map/ppermute | solution.py:574
  24.8 15.0 %collective-permute-done.7 = bf16[256,512]{0,1:T(8,128)(2,1)S(1)} collective-permute-done((bf16[256,512]{0,1:T(8,128)(2,1)S(1)}, bf16[256,512]{0,1:T(8,128)(2,1)S(1)}, u32[]{:S(2)}, u32[]{:S(2)}) %collective-permute-start.7) | collective-permute-done | bytes 262176 | tf_op jit(solution)/shard_map/ppermute | solution.py:574
  43.3 8.1 %all-gather.1 = s32[4,2,3]{2,1,0:T(2,128)S(1)} all-gather(s32[1,2,3]{2,1,0:T(2,128)S(1)} %add_bitcast_fusion), channel_id=2, replica_groups=mesh['dp'=2,'ctx'=4,'tp'=4] {'ctx'}, dimensions={0}, use_global_device_ids=true | all-gather | bytes 120 | tf_op jit(solution)/shard_map/all_gather | solution.py:587
  63.1 3.7 fusion.52
  70.0 9.8 %fusion.21 = bf16[768,1536]{1,0:T(8,128)(2,1)S(1)} fusion(bf16[2048,1600]{0,1:T(8,128)(2,1)} %all-gather.8.cloned.1.call-done, f32[768,2048]{1,0:T(8,128)} %convert_multiply_fusion.2, f32[2048]{0:T(1024)S(1)} %copy-done.77), kind=kOutput, calls=%fused_computation.45 | convolution fusion | flops 4836163584 | bytes 14950400 | tf_op jit(solution)/shard_map/dot_general | solution.py:443
  83.9 13.8 %collective-permute-done.1 = f32[3,64,128]{2,1,0:T(8,128)S(1)} collective-permute-done((f32[3,64,128]{2,1,0:T(8,128)S(1)}, f32[3,64,128]{2,1,0:T(8,128)S(1)}, u32[]{:S(2)}, u32[]{:S(2)}) %collective-permute-start.1) | collective-permute-done | bytes 98336 | tf_op jit(solution)/shard_map/ppermute | solution.py:606
  100.4 3.6 collective-permute-start.2
  105.4 16.3 %collective-permute-done.2 = bf16[3,64,1024]{2,1,0:T(8,128)(2,1)S(1)} collective-permute-done((bf16[3,64,1024]{2,1,0:T(8,128)(2,1)}, bf16[3,64,1024]{2,1,0:T(8,128)(2,1)S(1)}, u32[]{:S(2)}, u32[]{:S(2)}) %collective-permute-start.2) | collective-permute-done | bytes 393248 | tf_op jit(solution)/shard_map/ppermute | solution.py:621
  125.6 12.5 %shard_map.255 = (bf16[4,3,64,512]{3,2,1,0:T(8,128)(2,1)S(1)}, f32[768,512]{1,0:T(8,128)S(1)}, f32[64,768]{1,0:T(8,128)S(1)}, f32[64,768]{1,0:T(8,128)S(1)}, f32[3,256,256]{2,1,0:T(8,128)S(1)}) custom-call(bf16[4,3,64,1536]{3,2,1,0:T(8,128)(2,1)S(1)} %bitcast.243, bf16[4,3,64,1536]{3,2,1,0:T(8,128)(2,1)S(1)} %bitcast.244, ...), custom_call_target="tpu_custom_call" | custom-call | flops 3000000000 | bytes 9000000 | tf_op jit(solution)/shard_map/pallas_call | solution.py:365
  145.9 5.3 collective-permute-done.5
  151.2 9.9 %collective-permute-done.4 = bf16[192,512]{1,0:T(8,128)(2,1)S(1)} collective-permute-done((bf16[192,512]{1,0:T(8,128)(2,1)S(1)}, bf16[192,512]{1,0:T(8,128)(2,1)S(1)}, u32[]{:S(2)}, u32[]{:S(2)}) %collective-permute-start.4) | collective-permute-done | bytes 196640 | tf_op jit(solution)/shard_map/ppermute | solution.py:574
  161.8 5.6 multiply_reduce_fusion.2
  170.0 5.4 collective-permute-start.9
  175.5 5.0 copy.114
  180.5 9.0 %collective-permute-done.10 = bf16[192,2048]{1,0:T(8,128)(2,1)} collective-permute-done((bf16[192,2048]{1,0:T(8,128)(2,1)}, bf16[192,2048]{1,0:T(8,128)(2,1)}, u32[]{:S(2)}, u32[]{:S(2)}) %collective-permute-start.10) | collective-permute-done | bytes 786464 | tf_op jit(solution)/shard_map/ppermute | solution.py:472
  197.7 11.5 %collective-permute-done.12 = bf16[192,2048]{1,0:T(8,128)(2,1)S(1)} collective-permute-done((bf16[192,2048]{1,0:T(8,128)(2,1)}, bf16[192,2048]{1,0:T(8,128)(2,1)S(1)}, u32[]{:S(2)}, u32[]{:S(2)}) %collective-permute-start.12) | collective-permute-done | bytes 786464 | tf_op jit(solution)/shard_map/ppermute | solution.py:472
  214.5 13.4 %collective-permute-done.14 = bf16[192,2048]{1,0:T(8,128)(2,1)S(1)} collective-permute-done((bf16[192,2048]{1,0:T(8,128)(2,1)S(1)}, bf16[192,2048]{1,0:T(8,128)(2,1)S(1)}, u32[]{:S(2)}, u32[]{:S(2)}) %collective-permute-start.14) | collective-permute-done | bytes 786464 | tf_op jit(solution)/shard_map/ppermute | solution.py:472
  230.7 13.3 %fusion.2 = f32[768,2816]{0,1:T(8,128)S(1)} fusion(bf16[768,2048]{1,0:T(8,128)(2,1)} %bitcast.39, bf16[2048,4224]{0,1:T(8,128)(2,1)} %all-gather.12.cloned.1.call-done), kind=kOutput, calls=%fused_computation.4 | convolution fusion | flops 8858370048 | bytes 23330816 | tf_op jit(solution)/shard_map/dot_general | solution.py:443
  244.0 9.3 %fusion.18 = (bf16[768,1408]{0,1:T(8,128)(2,1)S(1)}, bf16[768,1408]{0,1:T(8,128)(2,1)S(1)}, bf16[768,1408]{0,1:T(8,128)(2,1)}) fusion(f32[768,2816]{0,1:T(8,128)S(1)} %fusion.2, bf16[768,2048]{1,0:T(8,128)(2,1)S(1)} %bitcast.271, bf16[2048,4224]{0,1:T(8,128)(2,1)} %all-gather.12.cloned.1.call-done), kind=kOutput, calls=%fused_computation.38 | convolution fusion | flops 4445405184 | bytes 24051712 | tf_op jit(solution)/shard_map/dot_general | solution.py:443
  255.3 13.5 %fusion.27 = bf16[768,2048]{1,0:T(8,128)(2,1)} fusion(bf16[2048,4224]{0,1:T(8,128)(2,1)} %all-gather.12.cloned.1.call-done, bf16[768,1408]{0,1:T(8,128)(2,1)S(1)} %get-tuple-element.177, bf16[768,1408]{0,1:T(8,128)(2,1)S(1)} %get-tuple-element.176), kind=kOutput, calls=%fused_computation.47 | convolution fusion | flops 8868593664 | bytes 19005440 | tf_op jit(solution)/shard_map/dot_general | solution.py:443
  269.1 14.7 %convolution_convert_fusion = bf16[2048,2816]{1,0:T(8,128)(2,1)} fusion(bf16[768,2048]{1,0:T(8,128)(2,1)} %bitcast.39, bf16[768,1408]{0,1:T(8,128)(2,1)} %copy-done.85, bf16[768,1408]{0,1:T(8,128)(2,1)} %copy-done.84), kind=kOutput, calls=%fused_computation.1 | convolution fusion | flops 8872787968 | bytes 19005440 | tf_op jit(solution)/shard_map/dot_general | solution.py:443
  283.8 9.4 %dynamic-slice_bitcast_fusion = (bf16[2,2,256,2816]{3,2,1,0:T(8,128)(2,1)}, bf16[2,2,256,2816]{3,2,1,0:T(8,128)(2,1)}) fusion(bf16[2,2,2,256,2816]{4,3,2,1,0:T(8,128)(2,1)} %bitcast.267, s32[]{:T(128)S(6)} %select_n.265, s32[]{:T(128)S(6)} %select_n.264), kind=kLoop, calls=%fused_computation.23 | loop fusion | bytes 23068680 | tf_op jit(solution)/shard_map/jit(dynamic_index_in_dim)/squeeze | solution.py:524
  293.6 7.5 %convolution_convert_fusion.2 = bf16[1408,2048]{0,1:T(8,128)(2,1)S(1)} fusion(bf16[768,1408]{0,1:T(8,128)(2,1)} %get-tuple-element.180, bf16[768,2048]{1,0:T(8,128)(2,1)} %bitcast.268), kind=kOutput, calls=%fused_computation.11 | convolution fusion | flops 4432068608 | bytes 11075584 | tf_op jit(solution)/shard_map/dot_general | solution.py:443
  304.7 9.2 %fusion.24 = bf16[768,2048]{1,0:T(8,128)(2,1)} fusion(bf16[768,1408]{0,1:T(8,128)(2,1)S(1)} %copy-done.83, bf16[2048,4224]{0,1:T(8,128)(2,1)} %all-gather.12.cloned.1.call-done), kind=kOutput, calls=%fused_computation.46 | convolution fusion | flops 4430757888 | bytes 11075584 | tf_op jit(solution)/shard_map/dot_general | solution.py:443
  314.2 15.2 %reduce-scatter.4.cloned.1.call-done = bf16[192,2048]{1,0:T(8,128)(2,1)} async-done(((bf16[768,2048]{1,0:T(8,128)(2,1)}), bf16[192,2048]{1,0:T(8,128)(2,1)}) %reduce-scatter.4.cloned.1.call-update) | async-done | bytes 786448 | tf_op jit(solution)/shard_map/reduce_scatter | solution.py:512
  332.9 6.6 %convolution_convert_fusion.4 = bf16[192,2048]{1,0:T(8,128)(2,1)S(1)} fusion(bf16[192,2048]{1,0:T(8,128)(2,1)S(1)} %fusion.93, bf16[2048,2048]{0,1:T(8,128)(2,1)} %all-gather.10.cloned.1.call-done), kind=kOutput, calls=%fused_computation.65 | convolution fusion | flops 1611005952 | bytes 9961472 | tf_op jit(solution)/shard_map/dot_general | solution.py:443
  344.1 5.7 add_convert_fusion
  361.7 6.1 collective-permute-done.17
  369.5 10.6 %collective-permute-done.18 = bf16[192,512]{1,0:T(8,128)(2,1)S(1)} collective-permute-done((bf16[192,512]{1,0:T(8,128)(2,1)S(1)}, bf16[192,512]{1,0:T(8,128)(2,1)S(1)}, u32[]{:S(2)}, u32[]{:S(2)}) %collective-permute-start.18) | collective-permute-done | bytes 196640 | tf_op jit(solution)/shard_map/ppermute | solution.py:574
  381.6 26.1 %shard_map.256 = (bf16[4,3,64,512]{3,2,1,0:T(8,128)(2,1)S(1)}, f32[768,512]{1,0:T(8,128)}, f32[768,512]{1,0:T(8,128)}, f32[64,768]{1,0:T(8,128)S(1)}, f32[64,768...) custom-call(bf16[4,3,64,1536]{3,2,1,0:T(8,128)(2,1)} %bitcast.246, ...), custom_call_target="tpu_custom_call" | custom-call | flops 8999999488 | bytes 15000000 | tf_op jit(solution)/shard_map/pallas_call | solution.py:392
  426.0 7.2 %collective-permute-done.43 = bf16[128,2816]{1,0:T(8,128)(2,1)S(1)} collective-permute-done((bf16[128,2816]{1,0:T(8,128)(2,1)S(1)}, bf16[128,2816]{1,0:T(8,128)(2,1)S(1)}, u32[]{:S(2)}, u32[]{:S(2)}) %collective-permute-start.43) | collective-permute-done | bytes 720928 | tf_op jit(solution)/shard_map/ppermute | solution.py:557
  434.7 5.3 collective-permute-done.44
  445.2 4.7 shard_map.257
  454.1 7.2 %fusion.8 = f32[768,2048]{1,0:T(8,128)S(1)} fusion(bf16[2048,1600]{0,1:T(8,128)(2,1)} %all-gather.8.cloned.1.call-done, bf16[768,512]{1,0:T(8,128)(2,1)S(1)} %bitcast.256, bf16[768,512]{1,0:T(8,128)(2,1)S(1)} %bitcast.254, bf16[768,512]{1,0:T(8,128)(2,1)S(1)} %bitcast.252), kind=kOutput, calls=%fused_computation.25 | convolution fusion | flops 4838916096 | bytes 14942208 | tf_op jit(solution)/shard_map/dot_general | solution.py:443
  461.3 3.6 add_convert_fusion.2
  464.8 5.4 fusion.4
  479.8 9.0 %convolution_convert_fusion.1 = bf16[2048,1600]{1,0:T(8,128)(2,1)S(1)} fusion(bf16[768,1600]{1,0:T(8,128)(2,1)} %pad_maximum_fusion.4, f32[768,2048]{1,0:T(8,128)} %convert_multiply_fusion.2, f32[2048]{0:T(1024)S(1)} %copy-done.78), kind=kOutput, calls=%fused_computation.10 | convolution fusion | flops 5039587328 | bytes 15310848 | tf_op jit(solution)/shard_map/dot_general | solution.py:443
  488.8 3.5 constant_dynamic-slice_fusion.4
  492.3 5.5 copy.122
  497.9 4.1 collective-permute-done.28
  509.6 4.1 copy.121
  516.6 3.8 collective-permute-done.31
  525.5 20.8 %collective-permute-done.32 = bf16[256,1024]{1,0:T(8,128)(2,1)S(1)} collective-permute-done((bf16[256,1024]{1,0:T(8,128)(2,1)S(1)}, bf16[256,1024]{1,0:T(8,128)(2,1)S(1)}, u32[]{:S(2)}, u32[]{:S(2)}) %collective-permute-start.32) | collective-permute-done | bytes 524320 | tf_op jit(solution)/shard_map/ppermute | solution.py:574
  562.7 5.5 copy.125
  568.8 3.8 add_convert_fusion.1
  603.4 5.3 collective-permute-done.39
  612.2 4.3 collective-permute-done.42
  (435 shorter events, 209.1 us)
Async XLA Ops:
  7.2 55.9 %all-gather.8.cloned.1.call-start = ((), (), s32[]{:S(2)}) async-start(), calls=%async_computation.3 | async-start | bytes 7372800 | tf_op jit(solution)/shard_map/all_gather | solution.py:518
  12.3 148.8 %all-gather.10.cloned.1.call-start = ((), (), s32[]{:S(2)}) async-start(), calls=%async_computation.4 | async-start | bytes 9437184 | tf_op jit(solution)/shard_map/all_gather | solution.py:518
  12.4 12.4 %collective-permute-start.8 = (bf16[256,512]{0,1:T(8,128)(2,1)S(1)}, bf16[256,512]{0,1:T(8,128)(2,1)S(1)}, u32[]{:S(2)}, u32[]{:S(2)}) collective-permute-start(bf16[256,512]{0,1:T(8,128)(2,1)S(1)} %bitcast.286), channel_id=1, source_target_pairs={{0,3},{1,2},{2,1},{3,0},{4,7},{5,6},{6,5},{7,4},{8,11},{9,10},{10,... | collective-permute-start | bytes 786440 | tf_op jit(solution)/shard_map/ppermute | solution.py:574
  17.5 22.3 %collective-permute-start.7 = (bf16[256,512]{0,1:T(8,128)(2,1)S(1)}, bf16[256,512]{0,1:T(8,128)(2,1)S(1)}, u32[]{:S(2)}, u32[]{:S(2)}) collective-permute-start(bf16[256,512]{0,1:T(8,128)(2,1)S(1)} %bitcast.287), channel_id=1, source_target_pairs={{0,2},{1,3},{2,0},{3,1},{4,6},{5,7},{6,4},{7,5},{8,10},{9,11},{10,... | collective-permute-start | bytes 786440 | tf_op jit(solution)/shard_map/ppermute | solution.py:574
  17.5 22.3 %collective-permute-start.6 = (bf16[256,512]{0,1:T(8,128)(2,1)S(1)}, bf16[256,512]{0,1:T(8,128)(2,1)S(1)}, u32[]{:S(2)}, u32[]{:S(2)}) collective-permute-start(bf16[256,512]{0,1:T(8,128)(2,1)S(1)} %bitcast.288), channel_id=1, source_target_pairs={{0,1},{1,0},{2,3},{3,2},{4,5},{5,4},{6,7},{7,6},{8,9},{9,8},{10,11... | collective-permute-start | bytes 786440 | tf_op jit(solution)/shard_map/ppermute | solution.py:574
  40.9 189.8 %all-gather.12.cloned.1.call-start = ((), (), s32[]{:S(2)}) async-start(), calls=%async_computation.5 | async-start | bytes 19464192 | tf_op jit(solution)/shard_map/all_gather | solution.py:518
  43.1 286.3 %reduce-scatter.4.cloned.1.call-start = ((), (), s32[]{:S(2)}) async-start(), calls=%async_computation.6 | async-start | bytes 3932160 | tf_op jit(solution)/shard_map/reduce_scatter | solution.py:512
  81.8 16.8 %collective-permute-start = (bf16[3,64,1024]{2,1,0:T(8,128)(2,1)S(1)}, bf16[3,64,1024]{2,1,0:T(8,128)(2,1)S(1)}, u32[]{:S(2)}, u32[]{:S(2)}) collective-permute-start(bf16[3,64,1024]{2,1,0:T(8,128)(2,1)S(1)} %get-tuple-element.62), channel_id=1, source_target_pairs={{0,4},{4,0},{8,12},{12,8},{1,5},{5,1},{9,13},{13,9},{2,6},{6,2},{1... | collective-permute-start | bytes 1179656 | tf_op jit(solution)/shard_map/ppermute | solution.py:616
  83.3 14.5 %collective-permute-start.1 = (f32[3,64,128]{2,1,0:T(8,128)S(1)}, f32[3,64,128]{2,1,0:T(8,128)S(1)}, u32[]{:S(2)}, u32[]{:S(2)}) collective-permute-start(f32[3,64,128]{2,1,0:T(8,128)S(1)} %get-tuple-element.63), channel_id=1, source_target_pairs={{0,4},{4,0},{8,12},{12,8},{1,5},{5,1},{9,13},{13,9},{2,6},{6,2},{1... | collective-permute-start | bytes 294920 | tf_op jit(solution)/shard_map/ppermute | solution.py:606
  100.4 21.2 %collective-permute-start.2 = (bf16[3,64,1024]{2,1,0:T(8,128)(2,1)}, bf16[3,64,1024]{2,1,0:T(8,128)(2,1)S(1)}, u32[]{:S(2)}, u32[]{:S(2)}) collective-permute-start(bf16[3,64,1024]{2,1,0:T(8,128)(2,1)} %fusion.57), channel_id=1, source_target_pairs={{0,8},{4,12},{1,9},{5,13},{2,10},{6,14},{3,11},{7,15},{16,24},{20,... | collective-permute-start | bytes 1179656 | tf_op jit(solution)/shard_map/ppermute | solution.py:621
  144.9 16.2 %collective-permute-start.4 = (bf16[192,512]{1,0:T(8,128)(2,1)S(1)}, bf16[192,512]{1,0:T(8,128)(2,1)S(1)}, u32[]{:S(2)}, u32[]{:S(2)}) collective-permute-start(bf16[192,512]{1,0:T(8,128)(2,1)S(1)} %get-tuple-element.213), channel_id=1, source_target_pairs={{0,2},{1,3},{2,0},{3,1},{4,6},{5,7},{6,4},{7,5},{8,10},{9,11},{10,... | collective-permute-start | bytes 589832 | tf_op jit(solution)/shard_map/ppermute | solution.py:574
  144.9 16.2 %collective-permute-start.3 = (bf16[192,512]{1,0:T(8,128)(2,1)S(1)}, bf16[192,512]{1,0:T(8,128)(2,1)S(1)}, u32[]{:S(2)}, u32[]{:S(2)}) collective-permute-start(bf16[192,512]{1,0:T(8,128)(2,1)S(1)} %get-tuple-element.214), channel_id=1, source_target_pairs={{0,1},{1,0},{2,3},{3,2},{4,5},{5,4},{6,7},{7,6},{8,9},{9,8},{10,11... | collective-permute-start | bytes 589832 | tf_op jit(solution)/shard_map/ppermute | solution.py:574
  168.7 20.7 %collective-permute-start.10 = (bf16[192,2048]{1,0:T(8,128)(2,1)}, bf16[192,2048]{1,0:T(8,128)(2,1)}, u32[]{:S(2)}, u32[]{:S(2)}) collective-permute-start(bf16[192,2048]{1,0:T(8,128)(2,1)} %multiply_convert_fusion.2), channel_id=1, source_target_pairs={{1,0},{2,1},{3,2},{5,4},{6,5},{7,6},{9,8},{10,9},{11,10},{13,12},{... | collective-permute-start | bytes 2359304 | tf_op jit(solution)/shard_map/ppermute | solution.py:472
  170.0 20.7 %collective-permute-start.9 = (bf16[192,2048]{1,0:T(8,128)(2,1)}, bf16[192,2048]{1,0:T(8,128)(2,1)}, u32[]{:S(2)}, u32[]{:S(2)}) collective-permute-start(bf16[192,2048]{1,0:T(8,128)(2,1)} %multiply_convert_fusion.2), channel_id=1, source_target_pairs={{0,1},{1,2},{2,3},{4,5},{5,6},{6,7},{8,9},{9,10},{10,11},{12,13},{... | collective-permute-start | bytes 2359304 | tf_op jit(solution)/shard_map/ppermute | solution.py:472
  189.5 19.7 %collective-permute-start.12 = (bf16[192,2048]{1,0:T(8,128)(2,1)}, bf16[192,2048]{1,0:T(8,128)(2,1)S(1)}, u32[]{:S(2)}, u32[]{:S(2)}) collective-permute-start(bf16[192,2048]{1,0:T(8,128)(2,1)} %collective-permute-done.10), channel_id=1, source_target_pairs={{1,0},{2,1},{5,4},{6,5},{9,8},{10,9},{13,12},{14,13},{17,16},{18,1... | collective-permute-start | bytes 2359304 | tf_op jit(solution)/shard_map/ppermute | solution.py:472
  190.8 19.7 %collective-permute-start.11 = (bf16[192,2048]{1,0:T(8,128)(2,1)}, bf16[192,2048]{1,0:T(8,128)(2,1)S(1)}, u32[]{:S(2)}, u32[]{:S(2)}) collective-permute-start(bf16[192,2048]{1,0:T(8,128)(2,1)} %collective-permute-done.9), channel_id=1, source_target_pairs={{1,2},{2,3},{5,6},{6,7},{9,10},{10,11},{13,14},{14,15},{17,18},{18... | collective-permute-start | bytes 2359304 | tf_op jit(solution)/shard_map/ppermute | solution.py:472
  209.2 18.7 %collective-permute-start.14 = (bf16[192,2048]{1,0:T(8,128)(2,1)S(1)}, bf16[192,2048]{1,0:T(8,128)(2,1)S(1)}, u32[]{:S(2)}, u32[]{:S(2)}) collective-permute-start(bf16[192,2048]{1,0:T(8,128)(2,1)S(1)} %collective-permute-done.12), channel_id=1, source_target_pairs={{1,0},{5,4},{9,8},{13,12},{17,16},{21,20},{25,24},{29,28}} | collective-permute-start | bytes 2359304 | tf_op jit(solution)/shard_map/ppermute | solution.py:472
  268.9 141.0 %reduce-scatter.6.cloned.1.call-start = ((), (), s32[]{:S(2)}) async-start(), calls=%async_computation.7 | async-start | bytes 3932160 | tf_op jit(solution)/shard_map/reduce_scatter | solution.py:512
  293.2 46.4 %collective-permute-start.15 = (bf16[2,2,256,2816]{3,2,1,0:T(8,128)(2,1)}, bf16[2,2,256,2816]{3,2,1,0:T(8,128)(2,1)}, u32[]{:S(2)}, u32[]{:S(2)}) collective-permute-start(bf16[2,2,256,2816]{3,2,1,0:T(8,128)(2,1)} %get-tuple-element.178), channel_id=1, source_target_pairs={{0,16},{16,0},{1,17},{17,1},{2,18},{18,2},{3,19},{19,3},{4,20},{20... | collective-permute-start | bytes 17301512 | tf_op jit(solution)/shard_map/ppermute | solution.py:533
  304.3 35.3 %collective-permute-start.16 = (bf16[2,2,256,1408]{3,2,1,0:T(8,128)(2,1)}, bf16[2,2,256,1408]{3,2,1,0:T(8,128)(2,1)}, u32[]{:S(2)}, u32[]{:S(2)}) collective-permute-start(bf16[2,2,256,1408]{3,2,1,0:T(8,128)(2,1)} %get-tuple-element.185), channel_id=1, source_target_pairs={{0,16},{16,0},{1,17},{17,1},{2,18},{18,2},{3,19},{19,3},{4,20},{20... | collective-permute-start | bytes 8650760 | tf_op jit(solution)/shard_map/ppermute | solution.py:533
  314.0 161.7 %all-gather.14.cloned.1.call-start = ((), (), s32[]{:S(2)}) async-start(), calls=%async_computation.8 | async-start | bytes 3932160 | tf_op jit(solution)/shard_map/all_gather | solution.py:515
  339.6 41.9 %collective-permute-start.19 = (bf16[192,512]{1,0:T(8,128)(2,1)S(1)}, bf16[192,512]{1,0:T(8,128)(2,1)S(1)}, u32[]{:S(2)}, u32[]{:S(2)}) collective-permute-start(bf16[192,512]{1,0:T(8,128)(2,1)S(1)} %get-tuple-element.208), channel_id=1, source_target_pairs={{0,3},{1,2},{2,1},{3,0},{4,7},{5,6},{6,5},{7,4},{8,11},{9,10},{10,... | collective-permute-start | bytes 589832 | tf_op jit(solution)/shard_map/ppermute | solution.py:574
  341.8 38.2 %collective-permute-start.18 = (bf16[192,512]{1,0:T(8,128)(2,1)S(1)}, bf16[192,512]{1,0:T(8,128)(2,1)S(1)}, u32[]{:S(2)}, u32[]{:S(2)}) collective-permute-start(bf16[192,512]{1,0:T(8,128)(2,1)S(1)} %get-tuple-element.209), channel_id=1, source_target_pairs={{0,2},{1,3},{2,0},{3,1},{4,6},{5,7},{6,4},{7,5},{8,10},{9,11},{10,... | collective-permute-start | bytes 589832 | tf_op jit(solution)/shard_map/ppermute | solution.py:574
  342.2 25.6 %collective-permute-start.17 = (bf16[192,512]{1,0:T(8,128)(2,1)S(1)}, bf16[192,512]{1,0:T(8,128)(2,1)S(1)}, u32[]{:S(2)}, u32[]{:S(2)}) collective-permute-start(bf16[192,512]{1,0:T(8,128)(2,1)S(1)} %get-tuple-element.210), channel_id=1, source_target_pairs={{0,1},{1,0},{2,3},{3,2},{4,5},{5,4},{6,7},{7,6},{8,9},{9,8},{10,11... | collective-permute-start | bytes 589832 | tf_op jit(solution)/shard_map/ppermute | solution.py:574
  352.0 57.9 %collective-permute-start.21 = (bf16[2,128,2816]{2,1,0:T(8,128)(2,1)}, bf16[2,128,2816]{2,1,0:T(8,128)(2,1)}, u32[]{:S(2)}, u32[]{:S(2)}) collective-permute-start(bf16[2,128,2816]{2,1,0:T(8,128)(2,1)} %get-tuple-element.195), channel_id=1, source_target_pairs={{0,8},{8,0},{4,12},{12,4},{1,9},{9,1},{5,13},{13,5},{2,10},{10,2},... | collective-permute-start | bytes 4325384 | tf_op jit(solution)/shard_map/ppermute | solution.py:546
  357.5 190.6 %collective-permute-start.26 = (bf16[2,128,1408]{2,1,0:T(8,128)(2,1)}, bf16[2,128,1408]{2,1,0:T(8,128)(2,1)}, u32[]{:S(2)}, u32[]{:S(2)}) collective-permute-start(bf16[2,128,1408]{2,1,0:T(8,128)(2,1)} %get-tuple-element.202), channel_id=1, source_target_pairs={{0,8},{8,0},{4,12},{12,4},{1,9},{9,1},{5,13},{13,5},{2,10},{10,2},... | collective-permute-start | bytes 2162696 | tf_op jit(solution)/shard_map/ppermute | solution.py:546
  367.8 42.1 %collective-permute-start.20 = (bf16[2,128,2816]{2,1,0:T(8,128)(2,1)}, bf16[2,128,2816]{2,1,0:T(8,128)(2,1)}, u32[]{:S(2)}, u32[]{:S(2)}) collective-permute-start(bf16[2,128,2816]{2,1,0:T(8,128)(2,1)} %get-tuple-element.197), channel_id=1, source_target_pairs={{0,4},{4,0},{8,12},{12,8},{1,5},{5,1},{9,13},{13,9},{2,6},{6,2},{1... | collective-permute-start | bytes 4325384 | tf_op jit(solution)/shard_map/ppermute | solution.py:545
  380.0 168.1 %collective-permute-start.25 = (bf16[2,128,1408]{2,1,0:T(8,128)(2,1)}, bf16[2,128,1408]{2,1,0:T(8,128)(2,1)}, u32[]{:S(2)}, u32[]{:S(2)}) collective-permute-start(bf16[2,128,1408]{2,1,0:T(8,128)(2,1)} %get-tuple-element.204), channel_id=1, source_target_pairs={{0,4},{4,0},{8,12},{12,8},{1,5},{5,1},{9,13},{13,9},{2,6},{6,2},{1... | collective-permute-start | bytes 2162696 | tf_op jit(solution)/shard_map/ppermute | solution.py:545
  412.6 135.5 %reduce-scatter.8.cloned.1.call-start = ((), (), s32[]{:S(2)}) async-start(), calls=%async_computation.9 | async-start | bytes 3932160 | tf_op jit(solution)/shard_map/reduce_scatter | solution.py:512
  412.7 13.1 %collective-permute-start.22 = (bf16[3,64,1024]{2,1,0:T(8,128)(2,1)}, bf16[3,64,1024]{2,1,0:T(8,128)(2,1)S(1)}, u32[]{:S(2)}, u32[]{:S(2)}) collective-permute-start(bf16[3,64,1024]{2,1,0:T(8,128)(2,1)} %copy-done.19), channel_id=1, source_target_pairs={{0,4},{4,0},{8,12},{12,8},{1,5},{5,1},{9,13},{13,9},{2,6},{6,2},{1... | collective-permute-start | bytes 1179656 | tf_op jit(solution)/shard_map/ppermute | solution.py:616
  415.6 17.7 %collective-permute-start.43 = (bf16[128,2816]{1,0:T(8,128)(2,1)S(1)}, bf16[128,2816]{1,0:T(8,128)(2,1)S(1)}, u32[]{:S(2)}, u32[]{:S(2)}) collective-permute-start(bf16[128,2816]{1,0:T(8,128)(2,1)S(1)} %dynamic-slice_bitcast_fusion.14), channel_id=1, source_target_pairs={{0,8},{8,0},{4,12},{12,4},{1,9},{9,1},{5,13},{13,5},{2,10},{10,2},... | collective-permute-start | bytes 2162696 | tf_op jit(solution)/shard_map/ppermute | solution.py:557
  418.9 21.1 %collective-permute-start.44 = (bf16[128,2816]{1,0:T(8,128)(2,1)S(1)}, bf16[128,2816]{1,0:T(8,128)(2,1)S(1)}, u32[]{:S(2)}, u32[]{:S(2)}) collective-permute-start(bf16[128,2816]{1,0:T(8,128)(2,1)S(1)} %dynamic-slice_bitcast_fusion.13), channel_id=1, source_target_pairs={{0,4},{4,0},{8,12},{12,8},{1,5},{5,1},{9,13},{13,9},{2,6},{6,2},{1... | collective-permute-start | bytes 2162696 | tf_op jit(solution)/shard_map/ppermute | solution.py:558
  425.8 39.1 %collective-permute-start.27 = (bf16[2,2,256,2048]{3,2,1,0:T(8,128)(2,1)}, bf16[2,2,256,2048]{3,2,1,0:T(8,128)(2,1)}, u32[]{:S(2)}, u32[]{:S(2)}) collective-permute-start(bf16[2,2,256,2048]{3,2,1,0:T(8,128)(2,1)} %dynamic-slice_bitcast_fusion.2), channel_id=1, source_target_pairs={{0,16},{16,0},{1,17},{17,1},{2,18},{18,2},{3,19},{19,3},{4,20},{20... | collective-permute-start | bytes 12582920 | tf_op jit(solution)/shard_map/ppermute | solution.py:533
  433.3 11.7 %collective-permute-start.23 = (bf16[3,64,1024]{2,1,0:T(8,128)(2,1)S(1)}, bf16[3,64,1024]{2,1,0:T(8,128)(2,1)S(1)}, u32[]{:S(2)}, u32[]{:S(2)}) collective-permute-start(bf16[3,64,1024]{2,1,0:T(8,128)(2,1)S(1)} %fusion.61), channel_id=1, source_target_pairs={{8,0},{12,4},{9,1},{13,5},{10,2},{14,6},{11,3},{15,7},{24,16},{28,... | collective-permute-start | bytes 1179656 | tf_op jit(solution)/shard_map/ppermute | solution.py:621
  475.7 146.2 %all-gather.16.cloned.1.call-start = ((), (), s32[]{:S(2)}) async-start(), calls=%async_computation.10 | async-start | bytes 3932160 | tf_op jit(solution)/shard_map/all_gather | solution.py:515
  476.8 25.2 %collective-permute-start.28 = (bf16[2,128,2048]{2,1,0:T(8,128)(2,1)}, bf16[2,128,2048]{2,1,0:T(8,128)(2,1)}, u32[]{:S(2)}, u32[]{:S(2)}) collective-permute-start(bf16[2,128,2048]{2,1,0:T(8,128)(2,1)} %dynamic-slice_bitcast_fusion.11), channel_id=1, source_target_pairs={{0,4},{4,0},{8,12},{12,8},{1,5},{5,1},{9,13},{13,9},{2,6},{6,2},{1... | collective-permute-start | bytes 3145736 | tf_op jit(solution)/shard_map/ppermute | solution.py:545
  478.3 26.9 %collective-permute-start.30 = (bf16[2,128,2048]{2,1,0:T(8,128)(2,1)}, bf16[2,128,2048]{2,1,0:T(8,128)(2,1)}, u32[]{:S(2)}, u32[]{:S(2)}) collective-permute-start(bf16[2,128,2048]{2,1,0:T(8,128)(2,1)} %dynamic-slice_bitcast_fusion.10), channel_id=1, source_target_pairs={{0,8},{8,0},{4,12},{12,4},{1,9},{9,1},{5,13},{13,5},{2,10},{10,2},... | collective-permute-start | bytes 3145736 | tf_op jit(solution)/shard_map/ppermute | solution.py:546
  497.9 50.2 %collective-permute-start.24 = (bf16[2,2,256,1600]{2,3,1,0:T(8,128)(2,1)}, bf16[2,2,256,1600]{2,3,1,0:T(8,128)(2,1)}, u32[]{:S(2)}, u32[]{:S(2)}) collective-permute-start(bf16[2,2,256,1600]{2,3,1,0:T(8,128)(2,1)} %bitcast.275), channel_id=1, source_target_pairs={{0,16},{16,0},{1,17},{17,1},{2,18},{18,2},{3,19},{19,3},{4,20},{20... | collective-permute-start | bytes 9830408 | tf_op jit(solution)/shard_map/ppermute | solution.py:533
  503.7 12.8 %collective-permute-start.29 = (bf16[128,2048]{1,0:T(8,128)(2,1)S(1)}, bf16[128,2048]{1,0:T(8,128)(2,1)S(1)}, u32[]{:S(2)}, u32[]{:S(2)}) collective-permute-start(bf16[128,2048]{1,0:T(8,128)(2,1)S(1)} %dynamic-slice_bitcast_fusion.20), channel_id=1, source_target_pairs={{0,8},{8,0},{4,12},{12,4},{1,9},{9,1},{5,13},{13,5},{2,10},{10,2},... | collective-permute-start | bytes 1572872 | tf_op jit(solution)/shard_map/ppermute | solution.py:557
  507.7 12.7 %collective-permute-start.31 = (bf16[128,2048]{1,0:T(8,128)(2,1)}, bf16[128,2048]{1,0:T(8,128)(2,1)S(1)}, u32[]{:S(2)}, u32[]{:S(2)}) collective-permute-start(bf16[128,2048]{1,0:T(8,128)(2,1)} %dynamic-slice_bitcast_fusion.19), channel_id=1, source_target_pairs={{0,4},{4,0},{8,12},{12,8},{1,5},{5,1},{9,13},{13,9},{2,6},{6,2},{1... | collective-permute-start | bytes 1572872 | tf_op jit(solution)/shard_map/ppermute | solution.py:558
  520.8 25.4 %collective-permute-start.32 = (bf16[256,1024]{1,0:T(8,128)(2,1)S(1)}, bf16[256,1024]{1,0:T(8,128)(2,1)S(1)}, u32[]{:S(2)}, u32[]{:S(2)}) collective-permute-start(bf16[256,1024]{1,0:T(8,128)(2,1)S(1)} %pad_maximum_fusion.10), channel_id=1, source_target_pairs={{0,1},{1,0},{2,3},{3,2},{4,5},{5,4},{6,7},{7,6},{8,9},{9,8},{10,11... | collective-permute-start | bytes 1572872 | tf_op jit(solution)/shard_map/ppermute | solution.py:574
  547.1 41.5 %collective-permute-start.33 = (bf16[256,512]{1,0:T(8,128)(2,1)}, bf16[256,512]{1,0:T(8,128)(2,1)}, u32[]{:S(2)}, u32[]{:S(2)}) collective-permute-start(bf16[256,512]{1,0:T(8,128)(2,1)} %fusion.68), channel_id=1, source_target_pairs={{0,2},{1,3},{2,0},{3,1},{4,6},{5,7},{6,4},{7,5},{8,10},{9,11},{10,... | collective-permute-start | bytes 786440 | tf_op jit(solution)/shard_map/ppermute | solution.py:574
  553.6 14.5 %collective-permute-start.34 = (f32[4864]{0:T(1024)S(1)}, f32[4864]{0:T(1024)S(1)}, u32[]{:S(2)}, u32[]{:S(2)}) collective-permute-start(f32[4864]{0:T(1024)S(1)} %pad_maximum_fusion.14), channel_id=1, source_target_pairs={{0,16},{16,0},{1,17},{17,1},{2,18},{18,2},{3,19},{19,3},{4,20},{20... | collective-permute-start | bytes 58376 | tf_op jit(solution)/shard_map/ppermute | solution.py:735
  556.9 35.6 %collective-permute-start.45 = (bf16[128,1408]{1,0:T(8,128)(2,1)}, bf16[128,1408]{1,0:T(8,128)(2,1)}, u32[]{:S(2)}, u32[]{:S(2)}) collective-permute-start(bf16[128,1408]{1,0:T(8,128)(2,1)} %dynamic-slice_bitcast_fusion.24), channel_id=1, source_target_pairs={{0,8},{8,0},{4,12},{12,4},{1,9},{9,1},{5,13},{13,5},{2,10},{10,2},... | collective-permute-start | bytes 1081352 | tf_op jit(solution)/shard_map/ppermute | solution.py:557
  561.2 32.4 %collective-permute-start.46 = (bf16[128,1408]{1,0:T(8,128)(2,1)}, bf16[128,1408]{1,0:T(8,128)(2,1)}, u32[]{:S(2)}, u32[]{:S(2)}) collective-permute-start(bf16[128,1408]{1,0:T(8,128)(2,1)} %dynamic-slice_bitcast_fusion.23), channel_id=1, source_target_pairs={{0,4},{4,0},{8,12},{12,8},{1,5},{5,1},{9,13},{13,9},{2,6},{6,2},{1... | collective-permute-start | bytes 1081352 | tf_op jit(solution)/shard_map/ppermute | solution.py:558
  578.3 19.1 %collective-permute-start.41 = (bf16[2,128,1600]{1,2,0:T(8,128)(2,1)}, bf16[2,128,1600]{1,2,0:T(8,128)(2,1)}, u32[]{:S(2)}, u32[]{:S(2)}) collective-permute-start(bf16[2,128,1600]{1,2,0:T(8,128)(2,1)} %bitcast.282), channel_id=1, source_target_pairs={{0,8},{8,0},{4,12},{12,4},{1,9},{9,1},{5,13},{13,5},{2,10},{10,2},... | collective-permute-start | bytes 2457608 | tf_op jit(solution)/shard_map/ppermute | solution.py:546
  587.2 21.5 %collective-permute-start.39 = (bf16[2,128,1600]{1,2,0:T(8,128)(2,1)}, bf16[2,128,1600]{1,2,0:T(8,128)(2,1)}, u32[]{:S(2)}, u32[]{:S(2)}) collective-permute-start(bf16[2,128,1600]{1,2,0:T(8,128)(2,1)} %bitcast.283), channel_id=1, source_target_pairs={{0,4},{4,0},{8,12},{12,8},{1,5},{5,1},{9,13},{13,9},{2,6},{6,2},{1... | collective-permute-start | bytes 2457608 | tf_op jit(solution)/shard_map/ppermute | solution.py:545
  602.0 14.5 %collective-permute-start.42 = (bf16[128,1600]{1,0:T(8,128)(2,1)}, bf16[128,1600]{1,0:T(8,128)(2,1)}, u32[]{:S(2)}, u32[]{:S(2)}) collective-permute-start(bf16[128,1600]{1,0:T(8,128)(2,1)} %dynamic-slice_bitcast_fusion.21), channel_id=1, source_target_pairs={{0,4},{4,0},{8,12},{12,8},{1,5},{5,1},{9,13},{13,9},{2,6},{6,2},{1... | collective-permute-start | bytes 1228808 | tf_op jit(solution)/shard_map/ppermute | solution.py:558
  (93 other events, 947.9 us)
Sparse Core Ops, SparseCore 0:
  12.5 50.5 all-gather.7
  65.5 62.1 all-gather.9
  129.5 101.1 all-gather.11
  269.0 60.4 reduce-scatter.3
  332.2 72.7 reduce-scatter.5
  412.7 62.9 all-gather.13
  478.0 69.9 reduce-scatter.7
  553.7 64.4 all-gather.15
